TPU v7x, 32 devices: a whole 2x2x4 slice. The times are simulated.
32 devices in a mesh: wide: 8 (over y, x, core), shard: 4 (over z).
Axes of the slice: x: 2, y: 2, z: 4, core: 2. Of those that a mesh axis runs over, the one named last changes fastest.
Arguments:
- tokens: bfloat16 [32768, 1152], P(('wide', 'shard')), may hold values from -6 to 6
- seg_ids: int32 [32768], P(('wide', 'shard')), may hold values from -1 to 63, as said below
- cotangent: bfloat16 [32768, 1152], P(('wide', 'shard')), may hold values from -6 to 6
- params: float32 [23296, 1152], P('shard'), may hold values from -6 to 6
- gains: float32 [4, 1152], P(None, 'shard'), may hold values from -0.06 to 0.06
- first_moment: float32 [23296, 1152], P('shard'), may hold values from -119.47276 to 119.47276
- second_moment: float32 [23296, 1152], P('shard'), may hold values from 1736.704 to 6881.28
- gain_first: float32 [4, 1152], P(None, 'shard'), may hold values from -119.47276 to 119.47276
- gain_second: float32 [4, 1152], P(None, 'shard'), may hold values from 1736.704 to 6881.28
Outputs:
- result: bfloat16 [32768, 1152], P(('wide', 'shard'))
- input_grad: bfloat16 [32768, 1152], P(('wide', 'shard'))
- row_grad: float32 [23296, 1152], P('shard')
- gain_grad: float32 [4, 1152], P(None, 'shard')
- new_params: float32 [23296, 1152], P('shard')
- new_gains: float32 [4, 1152], P(None, 'shard')
- new_first: float32 [23296, 1152], P('shard')
- new_second: float32 [23296, 1152], P('shard')
- new_gain_first: float32 [4, 1152], P(None, 'shard')
- new_gain_second: float32 [4, 1152], P(None, 'shard')
Inputs may be any that keep to these rules, and one draw needn't show every extreme that they name: `seg_ids`: within each device's 1024 slots the ids start at 0, never fall, and each id covers consecutive slots of one sequence; -1 marks the empty slots at the end of a device; some device holds one sequence of 1024 tokens, some device has empty slots, and some device holds 64 sequences.
All inputs are finite; a program needn't handle non-finite values.
Results may differ from a plain program's by a relative error of at most 0.018.
The roundings to bfloat16 on the way count: a program that leaves them out, or rounds other values in their place, can miss the bound.
Values may be sent and summed in bfloat16 or wider, within the bound.
No kernel may reach another device: no remote copies, remote signals or barrier semaphores. Data moves between devices by JAX's collectives and lax.ppermute only.
A program may use at most 704 MiB of HBM per device.

v0:
```python
import jax
import jax.numpy as jnp
from jax import lax
from jax.sharding import PartitionSpec as P

D = 1152
FF = 6912
HEADS = 4
KV_HEADS = 1
HD = 256
WINDOW = 512


norm_epsilon = 1e-06
softcap_limit = 50.0
rope_base = 10000.0
beta_first = 0.9
beta_second = 0.95
learn_rate = 0.02
adam_epsilon = 1e-08
weight_decay = 0.1
adam_step = 10.0
masked_floor = -1e30


def rms_scale(values, gain_row):
    return (
        values
        * lax.rsqrt(jnp.mean(values * values, axis=-1, keepdims=True) + norm_epsilon)
        * (1.0 + gain_row)
    )


def positions_of(segments):
    index_row = jnp.arange(segments.shape[0], dtype=jnp.int32)
    previous = jnp.concatenate([segments[:1] - 1, segments[:-1]])
    first_slot = lax.cummax(jnp.where(segments != previous, index_row, 0), axis=0)
    return index_row - first_slot


def rotary_tables(positions, head_width):
    half_width = head_width // 2
    frequency = rope_base ** (-2.0 * jnp.arange(half_width, dtype=jnp.float32) / head_width)
    angles = positions.astype(jnp.float32)[:, None] * frequency[None, :]
    return (jnp.cos(angles), jnp.sin(angles))


def rotate(values, cosine_table, sine_table):
    half_width = values.shape[-1] // 2
    first_half = values[..., :half_width]
    second_half = values[..., half_width:]
    cosine_part = cosine_table[:, None, :]
    sine_part = sine_table[:, None, :]
    return jnp.concatenate(
        [
            first_half * cosine_part - second_half * sine_part,
            second_half * cosine_part + first_half * sine_part,
        ],
        axis=-1,
    )


def geglu(gate_value, up_value):
    return jax.nn.gelu(gate_value, approximate=True) * up_value


def contract_rows(left_side, right_side):
    return lax.dot_general(
        left_side, right_side, (((0,), (0,)), ((), ())), preferred_element_type=jnp.float32
    )


def times_transposed(left_side, right_side):
    return lax.dot_general(
        left_side, right_side, (((1,), (1,)), ((), ())), preferred_element_type=jnp.float32
    )


def block_mask(query_segments, key_segments, first_row):
    query_index = first_row + jnp.arange(query_segments.shape[0], dtype=jnp.int32)
    key_index = jnp.arange(key_segments.shape[0], dtype=jnp.int32)
    return (
        (query_segments[:, None] == key_segments[None, :])
        & (key_index[None, :] <= query_index[:, None])
        & (query_index[:, None] - key_index[None, :] < WINDOW)
    )


def adam_update(param_old, grad_sum, first_old, second_old, decay_rate):
    first_new = beta_first * first_old + (1.0 - beta_first) * grad_sum
    second_new = beta_second * second_old + (1.0 - beta_second) * grad_sum * grad_sum
    corrected = (
        first_new
        / (1.0 - beta_first**adam_step)
        / (jnp.sqrt(second_new / (1.0 - beta_second**adam_step)) + adam_epsilon)
    )
    return (param_old - learn_rate * (corrected + decay_rate * param_old), first_new, second_new)


def per_device(
    tokens, seg_ids, cotangent, params, gains, first_moment, second_moment, gain_first, gain_second
):
    rows_used, gains_used = (
        lax.all_gather(params.astype(jnp.bfloat16), "shard", axis=0, tiled=True),
        lax.all_gather(gains.astype(jnp.bfloat16), "shard", axis=1, tiled=True),
    )
    gains_float = gains_used.astype(jnp.float32)
    query_width = HEADS * HD
    kv_width = KV_HEADS * HD
    per_group = HEADS // KV_HEADS
    qkv_rows = query_width + 2 * kv_width
    out_end = qkv_rows + query_width
    gate_end = out_end + 2 * FF
    w_qkv = rows_used[:qkv_rows]
    w_out = rows_used[qkv_rows:out_end]
    w_gate_up = rows_used[out_end:gate_end]
    w_down = rows_used[gate_end:]
    row_count = tokens.shape[0]
    block_rows = min(512, row_count)
    block_count = row_count // block_rows
    query_scale = HD ** (-0.5)
    inputs = tokens.astype(jnp.float32)
    cosine_table, sine_table = rotary_tables(positions_of(seg_ids), HD)
    normed, pull_first = jax.vjp(rms_scale, inputs, gains_float[0])
    normed_low = normed.astype(jnp.bfloat16)
    projected = times_transposed(normed_low, w_qkv)
    query_raw = projected[:, :query_width].reshape(row_count, HEADS, HD)
    key_raw = projected[:, query_width : query_width + kv_width].reshape(row_count, KV_HEADS, HD)
    value_heads = (
        projected[:, query_width + kv_width :].astype(jnp.bfloat16).reshape(row_count, KV_HEADS, HD)
    )
    queries = (rotate(query_raw, cosine_table, sine_table) * query_scale).astype(jnp.bfloat16)
    key_heads = rotate(key_raw, cosine_table, sine_table).astype(jnp.bfloat16)
    query_blocks = queries.reshape(block_count, block_rows, KV_HEADS, per_group, HD)
    segment_blocks = seg_ids.reshape(block_count, block_rows)
    block_starts = jnp.arange(block_count, dtype=jnp.int32) * block_rows

    def forward_block(inputs_block):
        query_block, segment_block, first_row = inputs_block
        scores = jnp.einsum(
            "qgnd,kgd->gnqk", query_block, key_heads, preferred_element_type=jnp.float32
        )
        capped = softcap_limit * jnp.tanh(scores / softcap_limit)
        allowed = block_mask(segment_block, seg_ids, first_row)
        row_top = jnp.max(jnp.where(allowed, capped, masked_floor), axis=-1, keepdims=True)
        weights_exp = jnp.where(allowed, jnp.exp(jnp.where(allowed, capped - row_top, 0.0)), 0.0)
        totals = jnp.sum(weights_exp, axis=-1, keepdims=True)
        probability = (weights_exp / totals).astype(jnp.bfloat16)
        mixed_block = jnp.einsum(
            "gnqk,kgd->qgnd", probability, value_heads, preferred_element_type=jnp.float32
        )
        return (mixed_block, row_top + jnp.log(totals))

    mixed_heads, log_totals = lax.map(forward_block, (query_blocks, segment_blocks, block_starts))
    mixed_low = mixed_heads.reshape(row_count, query_width).astype(jnp.bfloat16)
    attended = jnp.dot(mixed_low, w_out, preferred_element_type=jnp.float32)
    attn_normed, pull_second = jax.vjp(rms_scale, attended, gains_float[1])
    first_sum = inputs + attn_normed
    ffn_input, pull_third = jax.vjp(rms_scale, first_sum, gains_float[2])
    ffn_low = ffn_input.astype(jnp.bfloat16)
    gate_up = times_transposed(ffn_low, w_gate_up)
    hidden, pull_fourth = jax.vjp(geglu, gate_up[:, :FF], gate_up[:, FF:])
    hidden_low = hidden.astype(jnp.bfloat16)
    branch = jnp.dot(hidden_low, w_down, preferred_element_type=jnp.float32)
    ffn_normed, pull_fifth = jax.vjp(rms_scale, branch, gains_float[3])
    result = first_sum + ffn_normed
    upstream = cotangent.astype(jnp.float32)
    branch_grad, gain_four = pull_fifth(upstream)
    branch_low = branch_grad.astype(jnp.bfloat16)
    grad_down = contract_rows(hidden_low, branch_low)
    hidden_grad = times_transposed(branch_low, w_down)
    gate_grad, up_grad = pull_fourth(hidden_grad)
    gate_up_low = jnp.concatenate([gate_grad, up_grad], axis=1).astype(jnp.bfloat16)
    grad_gate_up = contract_rows(gate_up_low, ffn_low)
    ffn_input_grad = jnp.dot(gate_up_low, w_gate_up, preferred_element_type=jnp.float32)
    sum_grad_part, gain_three = pull_third(ffn_input_grad)
    sum_grad = upstream + sum_grad_part
    attended_grad, gain_two = pull_second(sum_grad)
    attended_low = attended_grad.astype(jnp.bfloat16)
    grad_out = contract_rows(mixed_low, attended_low)
    mixed_grad = (
        times_transposed(attended_low, w_out)
        .astype(jnp.bfloat16)
        .reshape(block_count, block_rows, KV_HEADS, per_group, HD)
    )

    def backward_block(running, inputs_block):
        key_acc, value_acc = running
        query_block, grad_block, segment_block, first_row, log_block = inputs_block
        scores = jnp.einsum(
            "qgnd,kgd->gnqk", query_block, key_heads, preferred_element_type=jnp.float32
        )
        capped = softcap_limit * jnp.tanh(scores / softcap_limit)
        allowed = block_mask(segment_block, seg_ids, first_row)
        probability = jnp.where(allowed, jnp.exp(jnp.where(allowed, capped - log_block, 0.0)), 0.0)
        probability_low = probability.astype(jnp.bfloat16)
        value_acc = value_acc + jnp.einsum(
            "gnqk,qgnd->kgd", probability_low, grad_block, preferred_element_type=jnp.float32
        )
        prob_grad = jnp.einsum(
            "qgnd,kgd->gnqk", grad_block, value_heads, preferred_element_type=jnp.float32
        )
        centred = jnp.sum(probability * prob_grad, axis=-1, keepdims=True)
        score_grad = (
            probability * (prob_grad - centred) * (1.0 - (capped / softcap_limit) ** 2)
        ).astype(jnp.bfloat16)
        query_grad_block = jnp.einsum(
            "gnqk,kgd->qgnd", score_grad, key_heads, preferred_element_type=jnp.float32
        )
        key_acc = key_acc + jnp.einsum(
            "gnqk,qgnd->kgd", score_grad, query_block, preferred_element_type=jnp.float32
        )
        return ((key_acc, value_acc), query_grad_block)

    zero_heads = jnp.zeros((row_count, KV_HEADS, HD), jnp.float32)
    (key_grad, value_grad), query_grad = lax.scan(
        backward_block,
        (zero_heads, zero_heads),
        (query_blocks, mixed_grad, segment_blocks, block_starts, log_totals),
    )
    query_raw_grad = rotate(
        query_grad.reshape(row_count, HEADS, HD) * query_scale, cosine_table, -sine_table
    )
    key_raw_grad = rotate(key_grad, cosine_table, -sine_table)
    qkv_low = jnp.concatenate(
        [
            query_raw_grad.reshape(row_count, query_width),
            key_raw_grad.reshape(row_count, kv_width),
            value_grad.reshape(row_count, kv_width),
        ],
        axis=1,
    ).astype(jnp.bfloat16)
    grad_qkv = contract_rows(qkv_low, normed_low)
    normed_grad = jnp.dot(qkv_low, w_qkv, preferred_element_type=jnp.float32)
    input_part, gain_one = pull_first(normed_grad)
    input_grad = sum_grad + input_part
    row_terms = jnp.concatenate([grad_qkv, grad_out, grad_gate_up, grad_down], axis=0)
    gain_terms = jnp.stack([gain_one, gain_two, gain_three, gain_four])
    wide_count = lax.axis_size("wide")
    shard_count = lax.axis_size("shard")
    total_rows = row_terms.shape[0]
    row_order = row_terms.reshape(
        shard_count, wide_count, total_rows // (shard_count * wide_count), D
    )
    row_order = row_order.transpose(1, 0, 2, 3).reshape(total_rows, D)
    gain_order = gain_terms.reshape(4, shard_count, wide_count, D // (shard_count * wide_count))
    gain_order = gain_order.transpose(0, 2, 1, 3).reshape(4, D)
    piece_rows, piece_gains = (
        lax.psum_scatter(row_order, ("wide", "shard"), scatter_dimension=0, tiled=True),
        lax.psum_scatter(gain_order, ("wide", "shard"), scatter_dimension=1, tiled=True),
    )
    row_grad, gain_grad = (
        lax.all_gather(piece_rows.astype(jnp.bfloat16), "wide", axis=0, tiled=True).astype(
            piece_rows.dtype
        ),
        lax.all_gather(piece_gains.astype(jnp.bfloat16), "wide", axis=1, tiled=True).astype(
            piece_gains.dtype
        ),
    )
    new_params, new_first, new_second = adam_update(
        params, row_grad, first_moment, second_moment, weight_decay
    )
    new_gains, new_gain_first, new_gain_second = adam_update(
        gains, gain_grad, gain_first, gain_second, 0.0
    )
    return (
        result.astype(jnp.bfloat16),
        input_grad.astype(jnp.bfloat16),
        row_grad,
        gain_grad,
        new_params,
        new_gains,
        new_first,
        new_second,
        new_gain_first,
        new_gain_second,
    )


def solution(mesh):
    return jax.shard_map(
        per_device,
        mesh=mesh,
        in_specs=(
            P(("wide", "shard"), None),
            P(("wide", "shard")),
            P(("wide", "shard"), None),
            P("shard", None),
            P(None, "shard"),
            P("shard", None),
            P("shard", None),
            P(None, "shard"),
            P(None, "shard"),
        ),
        out_specs=(
            P(("wide", "shard"), None),
            P(("wide", "shard"), None),
            P("shard", None),
            P(None, "shard"),
            P("shard", None),
            P(None, "shard"),
            P("shard", None),
            P("shard", None),
            P(None, "shard"),
            P(None, "shard"),
        ),
        check_vma=False,
    )
```

profile of v0, /device:TPU:0, one launch (start us, length us, event | category | flops | bytes accessed | tf_op | source)
XLA Modules:
  0.0 2478.9 jit_solution(4736457812752093211)
XLA Ops:
  7.2 15.1 convert_element_type.105
  24.7 14.8 all-gather
  44.6 872.8 %all-gather.5.cloned.1.call-done = bf16[23296,1152]{1,0:T(8,128)(2,1)} async-done(((bf16[5824,1152]{1,0:T(8,128)(2,1)}), bf16[23296,1152]{1,0:T(8,128)(2,1)}) %all-gather.5.cloned.1.call-update) | async-done | bytes 53674000 | tf_op jit(solution)/shard_map/all_gather | solution.py:104
  917.4 6.3 fusion.100
  930.2 5.6 reshape.532
  940.0 27.0 %while.29 = (s32[]{:T(128)}, bf16[2,512,1,4,256]{4,1,3,2,0:T(8,128)(2,1)}, f32[2,1,4,512,1]{3,2,4,1,0:T(4,128)S(1)}, s32[2,512]{1,0:T(2,128)S(1)}, s32[1024]{0:T...) while((s32[]{:T(128)}, ...), condition=%wide.region_6.7_spmd, body=%wide.region_3.6_spmd.sunk | while | flops 2186279424 | bytes 48314564 | solution.py:154
  971.7 5.4 multiply_reduce_fusion.6
  979.4 46.3 %fusion.75 = f32[1024,13824]{1,0:T(8,128)} fusion(bf16[23296,1152]{1,0:T(8,128)(2,1)} %all-gather.5.cloned.1.call-done, f32[1024,1152]{1,0:T(8,128)S(1)} %get-tuple-element.412, f32[1152]{0:T(1024)S(1)} %get-tuple-element.358, f32[1024]{0:T(1024)S(1)} %fusion.139), kind=kOutput, calls=%fused_computation.92 | convolution fusion | flops 32618446848 | bytes 93200896 | tf_op jit(solution)/shard_map/dot_general | solution.py:74
  1025.7 24.6 multiply_convert_fusion.1
  1050.3 23.3 multiply_reduce_fusion.4
  1078.5 25.4 %fusion.150 = f32[6912,1152]{1,0:T(8,128)} fusion(bf16[1024,6912]{1,0:T(8,128)(2,1)} %multiply_convert_fusion.1, bf16[1024,1152]{1,0:T(8,128)(2,1)S(1)} %get-tuple-element.423), kind=kOutput, calls=%fused_computation.227 | convolution fusion | flops 16307453952 | bytes 48365568 | tf_op jit(solution)/shard_map/dot_general | solution.py:68
  1103.9 45.3 %fusion.72 = (bf16[1024,6912]{1,0:T(8,128)(2,1)}, bf16[1024,6912]{1,0:T(8,128)(2,1)}) fusion(f32[1024,13824]{1,0:T(8,128)} %fusion.75, bf16[1024,1152]{1,0:T(8,128)(2,1)S(1)} %get-tuple-element.423, bf16[23296,1152]{1,0:T(8,128)(2,1)} %all-gather.5.cloned.1.call-done), kind=kOutput, calls=%fused_computation.86 | convolution fusion | flops 16477323264 | bytes 103219200 | tf_op jit(solution)/shard_map/dot_general | solution.py:74
  1149.2 48.2 %fusion.78 = f32[13824,1152]{1,0:T(8,128)} fusion(bf16[1024,6912]{1,0:T(8,128)(2,1)} %get-tuple-element.418, bf16[1024,6912]{1,0:T(8,128)(2,1)} %get-tuple-element.417, f32[1024,1152]{1,0:T(8,128)} %copy-done.2, f32[1152]{0:T(1024)S(1)} %copy-done.53, f32[1024]{0:T(1024)S(1)} %copy-done.62), kind=kOutput, calls=%fused_computation.98 | convolution fusion | flops 32675069952 | bytes 96739840 | tf_op jit(solution)/shard_map/dot_general | solution.py:68
  1197.5 50.0 %multiply_reduce_fusion = (f32[1152]{0:T(1024)}, f32[1024]{0:T(1024)S(1)}, f32[1024,1152]{1,0:T(8,128)S(1)}) fusion(f32[1024,1152]{1,0:T(8,128)} %copy-done.2, f32[1024]{0:T(1024)S(1)} %copy-done.62, f32[1152]{0:T(1024)S(1)} %copy-done.53, bf16[23296,1152]{1,0:T(8,128)(2,1)} %all-gather.5.cloned.1.call-done, bf16[1024,6912]{1,0:T(8,128)(2,1)} %get-tuple-element.418, ...), kind=kOutput, calls=%fused_computation.129 | convolution fusion | flops 32678604800 | bytes 69616640 | tf_op jit(solution)/shard_map/dot_general | solution.py:175
  1254.2 4.6 fusion.149
  1258.8 5.9 fusion.106
  1264.7 4.5 reshape.537
  1269.3 48.9 %while.30 = (s32[]{:T(128)}, f32[1024,1,256]{0,2,1:T(8,128)S(1)}, f32[1024,1,256]{0,2,1:T(8,128)}, f32[2,512,1,4,256]{4,1,0,3,2:T(8,128)}, bf16[2,512,1,4,256]{4...) while((s32[]{:T(128)}, f32[1024,1,256]{0,2,1:T(8,128)S(1)}, ...), condition=%wide.region_15.16_spmd.clone, body=%wide.region_13.15_spmd.clone.sunk | while | flops 5423233536 | bytes 125376880 | solution.py:216
  1279.4 4.3 fusion.192
  1283.7 4.4 fusion.193
  1303.7 4.3 fusion.192
  1308.1 4.4 fusion.193
  1328.7 9.8 fusion.109
  1338.5 73.1 %pad_maximum_fusion = f32[23296,1152]{1,0:T(8,128)} fusion(f32[6912,1152]{1,0:T(8,128)} %fusion.150, f32[13824,1152]{1,0:T(8,128)} %fusion.78, f32[1024,1152]{1,0:T(8,128)} %fusion.149, f32[1536,1152]{1,0:T(8,128)} %fusion.109), kind=kLoop, calls=%fused_computation.76 | loop fusion | flops 80510976 | bytes 214695936 | tf_op jit(solution)/shard_map/concatenate | solution.py:237
  1411.7 71.4 %copy.88 = f32[8,4,728,1152]{3,2,1,0:T(8,128)} copy(f32[8,4,728,1152]{3,2,0,1:T(8,128)} %bitcast.32) | data formatting | bytes 214695936 | tf_op jit(solution)/shard_map/transpose | solution.py:245
  1483.5 842.5 %reduce-scatter.5.cloned.1.call-done = f32[728,1152]{1,0:T(8,128)} async-done(((f32[23296,1152]{1,0:T(8,128)}), f32[728,1152]{1,0:T(8,128)}) %reduce-scatter.5.cloned.1.call-update) | async-done | bytes 3354640
  2329.8 9.7 fusion.88
  2339.7 40.7 %all-reduce.1 = bf16[4,1152]{1,0:T(4,128)(2,1)S(1)} all-reduce(f32[4,1152]{1,0:T(4,128)S(1)} %reshape.543), channel_id=3, replica_groups=mesh['wide'=8,'shard'=4] {'wide','shard'}, use_global_device_ids=true, to_apply=%region_22.23.clone | all-reduce | flops 4608 | bytes 27648
  2380.5 10.2 all-gather.1
  2391.5 5.5 fusion.94
  2396.9 8.6 all-gather.7.cloned.1.call-done
  2405.5 66.4 %multiply_subtract_fusion = (f32[5824,1152]{1,0:T(8,128)}, f32[5824,1152]{1,0:T(8,128)}, f32[5824,1152]{1,0:T(8,128)}, f32[5824,1152]{1,0:T(8,128)}) fusion(f32[5824,1152]{1,0:T(8,128)} %param.16, f32[5824,1152]{1,0:T(8,128)} %param.18, f32[5824,1152]{1,0:T(8,128)} %param.19, bf16[5824,1152]{1,0:T(8,128)(2,1)} %all-gather.7.cloned.1.call-done), kind=kLoop, calls=%fused_computation.95 | loop fusion | flops 107347968 | bytes 201277440 | tf_op jit(solution)/shard_map/sub | solution.py:97
  (274 shorter events, 108.6 us)
Async XLA Ops:
  7.2 910.2 %all-gather.5.cloned.1.call-start = ((), (), s32[]{:S(2)}) async-start(), calls=%async_computation.1 | async-start | bytes 67092480 | tf_op jit(solution)/shard_map/all_gather | solution.py:104
  22.4 2303.6 %reduce-scatter.5.cloned.1.call-start = ((), (), s32[]{:S(2)}) async-start(), calls=%async_computation.3 | async-start | bytes 110702592
  39.7 887.4 %copy-start.71 = (f32[128]{0:T(128)}, f32[128]{0:T(128)S(1)}, u32[]{:S(2)}) copy-start(f32[128]{0:T(128)S(1)} %multiply_power_fusion) | copy-start | bytes 1540
  40.4 883.3 %copy-start.54 = (f32[1152]{0:T(1024)}, f32[1152]{0:T(1024)S(1)}, u32[]{:S(2)}) copy-start(f32[1152]{0:T(1024)S(1)} %get-tuple-element.360) | copy-start | bytes 13828
  40.4 936.8 %copy-start.38 = (f32[1152]{0:T(1024)}, f32[1152]{0:T(1024)S(1)}, u32[]{:S(2)}) copy-start(f32[1152]{0:T(1024)S(1)} %get-tuple-element.359) | copy-start | bytes 13828
  40.4 938.9 %copy-start.52 = (f32[1152]{0:T(1024)}, f32[1152]{0:T(1024)S(1)}, u32[]{:S(2)}) copy-start(f32[1152]{0:T(1024)S(1)} %get-tuple-element.358) | copy-start | bytes 13828
  41.6 882.1 %copy-start.65 = (f32[1024]{0:T(1024)}, f32[1024]{0:T(1024)S(1)}, u32[]{:S(2)}) copy-start(f32[1024]{0:T(1024)S(1)} %fusion.137) | copy-start | bytes 12292
  41.6 885.5 %copy-start.43 = (f32[1024]{0:T(1024)}, f32[1024]{0:T(1024)S(1)}, u32[]{:S(2)}) copy-start(f32[1024]{0:T(1024)S(1)} %fusion.136) | copy-start | bytes 12292
  44.6 893.7 %copy-start.15 = (f32[1024,128]{1,0:T(8,128)}, f32[1024,128]{1,0:T(8,128)S(1)}, u32[]{:S(2)}) copy-start(f32[1024,128]{1,0:T(8,128)S(1)} %get-tuple-element.433) | copy-start | bytes 1572868
  979.3 46.4 %copy-start.49 = (f32[1024]{0:T(1024)}, f32[1024]{0:T(1024)S(1)}, u32[]{:S(2)}) copy-start(f32[1024]{0:T(1024)S(1)} %get-tuple-element.411) | copy-start | bytes 12292
  979.3 96.3 %copy-start.2 = (f32[1024,1152]{1,0:T(8,128)}, f32[1024,1152]{1,0:T(8,128)S(1)}, u32[]{:S(2)}) copy-start(f32[1024,1152]{1,0:T(8,128)S(1)} %get-tuple-element.412) | copy-start | bytes 14155780
  979.4 46.3 %copy-start.61 = (f32[1024]{0:T(1024)}, f32[1024]{0:T(1024)S(1)}, u32[]{:S(2)}) copy-start(f32[1024]{0:T(1024)S(1)} %fusion.139) | copy-start | bytes 12292
  1103.9 45.3 %copy-start.62 = (f32[1024]{0:T(1024)S(1)}, f32[1024]{0:T(1024)}, u32[]{:S(2)}) copy-start(f32[1024]{0:T(1024)} %copy-done.61) | copy-start | bytes 12292
  1197.4 50.1 %copy-start.50 = (f32[1024]{0:T(1024)S(1)}, f32[1024]{0:T(1024)}, u32[]{:S(2)}) copy-start(f32[1024]{0:T(1024)} %copy-done.49) | copy-start | bytes 12292
  1197.4 50.1 %copy-start.3 = (f32[1024,1152]{1,0:T(8,128)S(1)}, f32[1024,1152]{1,0:T(8,128)}, u32[]{:S(2)}) copy-start(f32[1024,1152]{1,0:T(8,128)} %copy-done.2) | copy-start | bytes 14155780
  1197.4 50.1 %copy-start.5 = (f32[1024,1152]{1,0:T(8,128)S(1)}, f32[1024,1152]{1,0:T(8,128)}, u32[]{:S(2)}) copy-start(f32[1024,1152]{1,0:T(8,128)} %copy-done.4) | copy-start | bytes 14155780
  1197.4 50.1 %copy-start.9 = (bf16[1024,1152]{1,0:T(8,128)(2,1)S(1)}, bf16[1024,1152]{1,0:T(8,128)(2,1)}, u32[]{:S(2)}) copy-start(bf16[1024,1152]{1,0:T(8,128)(2,1)} %param.15) | copy-start | bytes 7077892
  1197.4 50.1 %copy-start.39 = (f32[1152]{0:T(1024)S(1)}, f32[1152]{0:T(1024)}, u32[]{:S(2)}) copy-start(f32[1152]{0:T(1024)} %copy-done.38) | copy-start | bytes 13828
  1197.4 50.1 %copy-start.46 = (f32[1024]{0:T(1024)S(1)}, f32[1024]{0:T(1024)}, u32[]{:S(2)}) copy-start(f32[1024]{0:T(1024)} %copy-done.45) | copy-start | bytes 12292
  1483.1 846.2 %copy-start.57 = (f32[1152]{0:T(1024)S(1)}, f32[1152]{0:T(1024)}, u32[]{:S(2)}) copy-start(f32[1152]{0:T(1024)} %get-tuple-element.355) | copy-start | bytes 13828
  1483.1 846.3 %copy-start.68 = (f32[1152]{0:T(1024)S(1)}, f32[1152]{0:T(1024)}, u32[]{:S(2)}) copy-start(f32[1152]{0:T(1024)} %get-tuple-element.351) | copy-start | bytes 13828
  1483.1 846.4 %copy-start.51 = (f32[1152]{0:T(1024)S(1)}, f32[1152]{0:T(1024)}, u32[]{:S(2)}) copy-start(f32[1152]{0:T(1024)} %get-tuple-element.349) | copy-start | bytes 13828
  1483.1 846.5 %copy-start.12 = (bf16[1024,1152]{1,0:T(8,128)(2,1)S(1)}, bf16[1024,1152]{1,0:T(8,128)(2,1)}, u32[]{:S(2)}) copy-start(bf16[1024,1152]{1,0:T(8,128)(2,1)} %param.13) | copy-start | bytes 7077892
  1483.2 846.5 %copy-start.31 = (bf16[1024,256]{0,1:T(8,128)(2,1)S(1)}, bf16[1024,256]{0,1:T(8,128)(2,1)}, u32[]{:S(2)}) copy-start(bf16[1024,256]{0,1:T(8,128)(2,1)} %copy-done.30) | copy-start | bytes 1572868
  1483.2 846.5 %copy-start.35 = (bf16[1024,256]{0,1:T(8,128)(2,1)S(1)}, bf16[1024,256]{0,1:T(8,128)(2,1)}, u32[]{:S(2)}) copy-start(bf16[1024,256]{0,1:T(8,128)(2,1)} %copy-done.34) | copy-start | bytes 1572868
  1483.2 846.5 %copy-start.56 = (f32[1152]{0:T(1024)S(1)}, f32[1152]{0:T(1024)}, u32[]{:S(2)}) copy-start(f32[1152]{0:T(1024)} %copy-done.54) | copy-start | bytes 13828
  1483.2 846.5 %copy-start.67 = (f32[1024]{0:T(1024)S(1)}, f32[1024]{0:T(1024)}, u32[]{:S(2)}) copy-start(f32[1024]{0:T(1024)} %copy-done.65) | copy-start | bytes 12292
  1483.2 922.3 %all-gather.7.cloned.1.call-start = ((), (), s32[]{:S(2)}) async-start(), calls=%async_computation.2 | async-start | bytes 15095808 | tf_op jit(solution)/shard_map/all_gather | solution.py:253
  2329.7 61.1 %copy-start.48 = (f32[1024]{0:T(1024)S(1)}, f32[1024]{0:T(1024)}, u32[]{:S(2)}) copy-start(f32[1024]{0:T(1024)} %copy-done.47) | copy-start | bytes 12292
  2329.7 61.1 %copy-start.59 = (f32[4,288]{1,0:T(4,128)S(1)}, f32[4,288]{1,0:T(4,128)}, u32[]{:S(2)}) copy-start(f32[4,288]{1,0:T(4,128)} %param.17) | copy-start | bytes 13828
  2329.8 61.1 %copy-start.69 = (f32[4,288]{1,0:T(4,128)S(1)}, f32[4,288]{1,0:T(4,128)}, u32[]{:S(2)}) copy-start(f32[4,288]{1,0:T(4,128)} %param.20) | copy-start | bytes 13828
  2329.8 61.1 %copy-start.70 = (f32[4,288]{1,0:T(4,128)S(1)}, f32[4,288]{1,0:T(4,128)}, u32[]{:S(2)}) copy-start(f32[4,288]{1,0:T(4,128)} %param.21) | copy-start | bytes 13828
  (54 other events, 350.8 us)
Sparse Core Ops, SparseCore 0:
  22.5 894.8 all-gather.4
  1483.2 842.7 reduce-scatter.4
  2329.5 76.0 all-gather.6
where the time goes:
time: 2490 us; the launch traced here: 2480 us
  waiting for transfers between devices  1720 us (69%)
  matrix products  319 us (13%)
  other arithmetic  237 us (10%)
  local copies, waits for them, and re-layouts  116 us (5%)
  blocking collectives  65.7 us (3%)
    all_gather x1, waiting for transfers between devices, per_device(): lax.all_gather(params.astype(jnp.bfloat16), 'shard', axis=0, tiled=True)  873 us
    unnamed x4, waiting for transfers between devices  843 us
    dot_general x4, matrix products, times_transposed(): lax.dot_general(left_side, right_side, (((1,), (1,)), ((), ())), preferre...  104 us
    dot_general x4, matrix products, contract_rows(): lax.dot_general(left_side, right_side, (((0,), (0,)), ((), ())), preferre...  88 us
    concatenate x1, other arithmetic, per_device(): jnp.concatenate([grad_qkv, grad_out, grad_gate_up, grad_down], axis=0)  73.1 us
    transpose x1, local copies, waits for them, and re-layouts, per_device(): row_order = row_order.transpose(1, 0, 2, 3).reshape(total_rows, D)  71.4 us
    sub x2, other arithmetic, adam_update(): param_old - learn_rate * (corrected + decay_rate * param_old)  67.1 us
    dot_general x1, matrix products, per_device(): jnp.dot(gate_up_low, w_gate_up, preferred_element_type=jnp.float32)  50 us
  transfers between devices with their start and end apart: 3, of which 3 were waited for; matrix products, arithmetic and copies ran while one was open for 1% of the time, Pallas kernels for 0%

commit v1 on v0

--- a/solution.py
+++ b/solution.py
@@ -1,6 +1,8 @@
 import jax
 import jax.numpy as jnp
 from jax import lax
+from jax.experimental import pallas as pl
+from jax.experimental.pallas import tpu as pltpu
 from jax.sharding import PartitionSpec as P
 
 D = 1152
@@ -97,13 +99,135 @@
     return (param_old - learn_rate * (corrected + decay_rate * param_old), first_new, second_new)
 
 
+def power_of_two(count):
+    return count & (count - 1) == 0
+
+
+def butterfly_sum(values, axis_name):
+    count = lax.axis_size(axis_name)
+    if not power_of_two(count):
+        return lax.psum(values, axis_name)
+    step = 1
+    while step < count:
+        values = values + lax.ppermute(values, axis_name, [(i, i ^ step) for i in range(count)])
+        step *= 2
+    return values
+
+
+def gather_columns(values, axis_name):
+    count = lax.axis_size(axis_name)
+    index = lax.axis_index(axis_name)
+    width = values.shape[1]
+    whole = jnp.zeros((values.shape[0], width * count), values.dtype)
+    whole = lax.dynamic_update_slice_in_dim(whole, values, index * width, axis=1)
+    for shift in range(1, count):
+        moved = lax.ppermute(values, axis_name, [(i, (i + shift) % count) for i in range(count)])
+        source = lax.rem(index + count - shift, count)
+        whole = lax.dynamic_update_slice_in_dim(whole, moved, source * width, axis=1)
+    return whole
+
+
+def spread_first(rows):
+    place = lax.axis_index("shard")
+    rows = jnp.where(place == 0, rows, lax.ppermute(rows, "shard", [(0, 2)]))
+    rows = jnp.where(
+        lax.rem(place, 2) == 1, lax.ppermute(rows, "shard", [(0, 1), (2, 3)]), rows
+    )
+    index = lax.axis_index("wide")
+    blocks = {0: rows}
+    for bit in (4, 2, 1):
+        upper = (index & bit) != 0
+        grown = {}
+        for key, block in blocks.items():
+            other = lax.ppermute(block, "wide", [(i, i ^ bit) for i in range(8)])
+            grown[key] = jnp.where(upper, other, block)
+            grown[key | bit] = jnp.where(upper, block, other)
+        blocks = grown
+    return jnp.concatenate([blocks[key] for key in range(8)], axis=0)
+
+
+owner_tree = {
+    0: ([(3, 2), (1, 0)], [(2, 0)]),
+    1: ([(0, 1), (3, 2)], [(2, 1)]),
+    2: ([(3, 2), (0, 1)], [(1, 2)]),
+    3: ([(0, 1), (2, 3)], [(1, 3)]),
+}
+
+
+def add_low(left, right):
+    return (left.astype(jnp.float32) + right.astype(jnp.float32)).astype(left.dtype)
+
+
+def tied(anchor, values):
+    return lax.optimization_barrier((anchor, values))
+
+
+def choose_owner(pieces):
+    place = lax.axis_index("shard")
+    own = pieces[0]
+    for owner in range(1, len(pieces)):
+        own = jnp.where(place == owner, pieces[owner], own)
+    return own
+
+
+def row_block(count):
+    return max(size for size in range(8, 329, 8) if count % size == 0)
+
+
+def adam_rows(first, grad_low, state, carried):
+    count = grad_low.shape[0]
+    block = row_block(count)
+    spec = pl.BlockSpec((pl.Element(block), pl.Element(D)), lambda i: (pl.multiple_of(first + i * block, 8), 0))
+
+    def body(grad_ref, param_ref, first_ref, second_ref, *rest):
+        out_refs = rest[-4:]
+        grad = grad_ref[...].astype(jnp.float32)
+        param_new, first_new, second_new = adam_update(
+            param_ref[...], grad, first_ref[...], second_ref[...], weight_decay
+        )
+        for ref, value in zip(out_refs, (grad, param_new, first_new, second_new)):
+            ref[...] = value
+
+    shape = jax.ShapeDtypeStruct(state[0].shape, jnp.float32)
+    return pl.pallas_call(
+        body,
+        grid=(count // block,),
+        in_specs=[pl.BlockSpec((block, D), lambda i: (i, 0))]
+        + [spec] * 3
+        + [pl.BlockSpec(memory_space=pl.ANY)] * len(carried),
+        out_specs=[spec] * 4,
+        out_shape=[shape] * 4,
+        input_output_aliases={4 + k: k for k in range(len(carried))},
+        cost_estimate=pl.CostEstimate(
+            flops=20 * count * D, transcendentals=count * D, bytes_accessed=30 * count * D
+        ),
+        compiler_params=pltpu.CompilerParams(vmem_limit_bytes=48 * 2**20),
+        name="adam_rows",
+    )(grad_low, *state, *carried)
+
+
 def per_device(
     tokens, seg_ids, cotangent, params, gains, first_moment, second_moment, gain_first, gain_second
 ):
-    rows_used, gains_used = (
-        lax.all_gather(params.astype(jnp.bfloat16), "shard", axis=0, tiled=True),
-        lax.all_gather(gains.astype(jnp.bfloat16), "shard", axis=1, tiled=True),
-    )
+    wide_count = lax.axis_size("wide")
+    shard_count = lax.axis_size("shard")
+    owner_rows = params.shape[0]
+    total_rows = owner_rows * shard_count
+    early_rows = (HEADS + 2 * KV_HEADS) * HD + HEADS * HD
+    wide_index = lax.axis_index("wide")
+
+    def own_slice(first, count):
+        part = count // wide_count
+        return lax.dynamic_slice_in_dim(
+            params, first + wide_index * part, part, axis=0
+        ).astype(jnp.bfloat16)
+
+    rows_used = lax.all_gather(own_slice(0, owner_rows), ("shard", "wide"), axis=0, tiled=True)
+    if wide_count == 8 and shard_count == 4:
+        early_used = spread_first(own_slice(0, early_rows))
+    else:
+        early_used = rows_used[:early_rows]
+    gains_used = gather_columns(gains.astype(jnp.bfloat16), "shard")
     gains_float = gains_used.astype(jnp.float32)
     query_width = HEADS * HD
     kv_width = KV_HEADS * HD
@@ -111,8 +235,8 @@
     qkv_rows = query_width + 2 * kv_width
     out_end = qkv_rows + query_width
     gate_end = out_end + 2 * FF
-    w_qkv = rows_used[:qkv_rows]
-    w_out = rows_used[qkv_rows:out_end]
+    w_qkv = early_used[:qkv_rows]
+    w_out = early_used[qkv_rows:out_end]
     w_gate_up = rows_used[out_end:gate_end]
     w_down = rows_used[gate_end:]
     row_count = tokens.shape[0]
@@ -167,22 +291,78 @@
     upstream = cotangent.astype(jnp.float32)
     branch_grad, gain_four = pull_fifth(upstream)
     branch_low = branch_grad.astype(jnp.bfloat16)
-    grad_down = contract_rows(hidden_low, branch_low)
+    tree = wide_count == 8 and shard_count == 4
+    factors = {"down": (gate_end, total_rows, hidden_low, branch_low)}
+    reduced, steps = {}, {}
+
+    def bounds(owner, part):
+        edges = (0, early_rows, owner_rows)
+        return owner * owner_rows + edges[part], owner * owner_rows + edges[part + 1]
+
+    def plane_terms(first, last):
+        parts = [
+            contract_rows(
+                left[:, max(first, start) - start : min(last, end) - start], right
+            ).astype(jnp.bfloat16)
+            for start, end, left, right in sorted(factors.values(), key=lambda f: f[0])
+            if max(first, start) < min(last, end)
+        ]
+        return parts[0] if len(parts) == 1 else jnp.concatenate(parts, axis=0)
+
+    def plane_sum(first, last):
+        return lax.psum_scatter(
+            plane_terms(first, last), "wide", scatter_dimension=0, tiled=True
+        )
+
+    def start_ready(anchor, lowest):
+        keys = [
+            (owner, part)
+            for part in (1, 0)
+            for owner in range(shard_count)
+            if (owner, part) not in reduced and bounds(owner, part)[0] >= lowest
+        ]
+        terms = [plane_terms(*bounds(*key)) for key in keys]
+        for key, term in zip(keys, terms):
+            reduced[key] = lax.psum_scatter(term, "wide", scatter_dimension=0, tiled=True)
+            steps[key] = [reduced[key]]
+        return tied(anchor, terms)[0]
+
+    def advance(key):
+        owner, _ = key
+        pairs = owner_tree[owner][len(steps[key]) - 1]
+        held = steps[key][-1]
+        steps[key].append(add_low(held, lax.ppermute(held, "shard", pairs)))
+
+    def tick(anchor, *keys):
+        if not tree:
+            return anchor
+        anchor, values = tied(anchor, [steps[key][-1] for key in keys])
+        for key, value in zip(keys, values):
+            steps[key][-1] = value
+            advance(key)
+        return anchor
+
+    branch_low = start_ready(branch_low, gate_end)
     hidden_grad = times_transposed(branch_low, w_down)
     gate_grad, up_grad = pull_fourth(hidden_grad)
     gate_up_low = jnp.concatenate([gate_grad, up_grad], axis=1).astype(jnp.bfloat16)
-    grad_gate_up = contract_rows(gate_up_low, ffn_low)
+    factors["gate_up"] = (out_end, gate_end, gate_up_low, ffn_low)
+    gate_up_low = start_ready(gate_up_low, out_end)
+    gate_up_low = tick(gate_up_low, (3, 1), (3, 0))
     ffn_input_grad = jnp.dot(gate_up_low, w_gate_up, preferred_element_type=jnp.float32)
+    ffn_input_grad = tick(ffn_input_grad, (3, 1), (3, 0), (0, 1))
     sum_grad_part, gain_three = pull_third(ffn_input_grad)
     sum_grad = upstream + sum_grad_part
     attended_grad, gain_two = pull_second(sum_grad)
     attended_low = attended_grad.astype(jnp.bfloat16)
-    grad_out = contract_rows(mixed_low, attended_low)
+    factors["out"] = (qkv_rows, out_end, mixed_low, attended_low)
     mixed_grad = (
         times_transposed(attended_low, w_out)
         .astype(jnp.bfloat16)
         .reshape(block_count, block_rows, KV_HEADS, per_group, HD)
     )
+
+    mixed_grad = tick(mixed_grad, (0, 1), (1, 1))
 
     def backward_block(running, inputs_block):
         key_acc, value_acc = running
@@ -218,6 +398,7 @@
         (zero_heads, zero_heads),
         (query_blocks, mixed_grad, segment_blocks, block_starts, log_totals),
     )
+    query_grad = tick(query_grad, (1, 1), (2, 1))
     query_raw_grad = rotate(
         query_grad.reshape(row_count, HEADS, HD) * query_scale, cosine_table, -sine_table
     )
@@ -230,35 +411,37 @@
         ],
         axis=1,
     ).astype(jnp.bfloat16)
-    grad_qkv = contract_rows(qkv_low, normed_low)
+    factors["qkv"] = (0, qkv_rows, qkv_low, normed_low)
     normed_grad = jnp.dot(qkv_low, w_qkv, preferred_element_type=jnp.float32)
     input_part, gain_one = pull_first(normed_grad)
     input_grad = sum_grad + input_part
-    row_terms = jnp.concatenate([grad_qkv, grad_out, grad_gate_up, grad_down], axis=0)
+    reduced[0, 0] = plane_sum(0, early_rows)
+    steps[0, 0] = [reduced[0, 0]]
+    if tree:
+        for key in sorted(reduced, key=lambda k: k[1], reverse=True):
+            while len(steps[key]) < 3:
+                advance(key)
+        late_piece = choose_owner([steps[owner, 1][-1] for owner in range(shard_count)])
+        early_piece = choose_owner([steps[owner, 0][-1] for owner in range(shard_count)])
+    else:
+        late_piece, early_piece = [
+            lax.psum_scatter(
+                jnp.concatenate([reduced[owner, part] for owner in range(shard_count)], axis=0),
+                "shard",
+                scatter_dimension=0,
+                tiled=True,
+            )
+            for part in (1, 0)
+        ]
+    late_low = lax.all_gather(late_piece, "wide", axis=0, tiled=True)
+    early_low = lax.all_gather(early_piece, "wide", axis=0, tiled=True)
+    state = (params, first_moment, second_moment)
+    carried = adam_rows(early_rows, late_low, state, ())
+    row_grad, new_params, new_first, new_second = adam_rows(0, early_low, state, carried)
     gain_terms = jnp.stack([gain_one, gain_two, gain_three, gain_four])
-    wide_count = lax.axis_size("wide")
-    shard_count = lax.axis_size("shard")
-    total_rows = row_terms.shape[0]
-    row_order = row_terms.reshape(
-        shard_count, wide_count, total_rows // (shard_count * wide_count), D
-    )
-    row_order = row_order.transpose(1, 0, 2, 3).reshape(total_rows, D)
-    gain_order = gain_terms.reshape(4, shard_count, wide_count, D // (shard_count * wide_count))
-    gain_order = gain_order.transpose(0, 2, 1, 3).reshape(4, D)
-    piece_rows, piece_gains = (
-        lax.psum_scatter(row_order, ("wide", "shard"), scatter_dimension=0, tiled=True),
-        lax.psum_scatter(gain_order, ("wide", "shard"), scatter_dimension=1, tiled=True),
-    )
-    row_grad, gain_grad = (
-        lax.all_gather(piece_rows.astype(jnp.bfloat16), "wide", axis=0, tiled=True).astype(
-            piece_rows.dtype
-        ),
-        lax.all_gather(piece_gains.astype(jnp.bfloat16), "wide", axis=1, tiled=True).astype(
-            piece_gains.dtype
-        ),
-    )
-    new_params, new_first, new_second = adam_update(
-        params, row_grad, first_moment, second_moment, weight_decay
+    gain_total = butterfly_sum(butterfly_sum(gain_terms, "wide"), "shard")
+    gain_grad = lax.dynamic_slice_in_dim(
+        gain_total, lax.axis_index("shard") * gains.shape[1], gains.shape[1], axis=1
     )
     new_gains, new_gain_first, new_gain_second = adam_update(
         gains, gain_grad, gain_first, gain_second, 0.0

time: 2490 us -> 1170 us (0.47)
  waiting for transfers between devices: 1720 us -> 446 us
  other arithmetic: 237 us -> 156 us
  starting transfers between devices: 0.37 us -> 74.3 us
  Pallas kernels: 0 us -> 72.8 us
  blocking collectives: 65.7 us -> 0 us
  local copies, waits for them, and re-layouts: 116 us -> 62.9 us
    unnamed x4 -> x11, waiting for transfers between devices: 843 us -> 0.18 us
    all_gather x2 -> x3, waiting for transfers between devices: 881 us -> 122 us  [the longest x1 122 us: per_device(): lax.all_gather(own_slice(0, owner_rows), ('shard', 'wide'), axis=0, tiled...]
    ppermute x0 -> x33, waiting for transfers between devices: none -> 183 us  [the longest x7 68.2 us: spread_first(): other = lax.ppermute(block, 'wide', [(i, i ^ bit) for i in range(8)])]
    reduce_scatter x0 -> x4, waiting for transfers between devices: none -> 115 us  [the longest x1 59.5 us: plane_sum(): lax.psum_scatter(plane_terms(first, last), 'wide', scatter_dimension=0, t...]
    ppermute x0 -> x33, starting transfers between devices: none -> 73.9 us  [the longest x16 45.2 us: advance(): steps[key].append(add_low(held, lax.ppermute(held, 'shard', pairs)))]
    pallas_call x0 -> x2, Pallas kernels: none -> 72.8 us  [adam_rows(): pl.pallas_call(body, grid=(count // block,), in_specs=[pl.BlockSpec((bloc...]
    transpose x2 -> x0, local copies, waits for them, and re-layouts: 71.4 us -> none  [the longest x1 71.4 us: per_device(): row_order = row_order.transpose(1, 0, 2, 3).reshape(total_rows, D)]
    sub x2 -> x1, other arithmetic: 67.1 us -> 0.7 us  [adam_update(): param_old - learn_rate * (corrected + decay_rate * param_old)]
  transfers between devices with their start and end apart: 3 -> 44, of which waited for: 3 -> 21; matrix products, arithmetic and copies ran while one was open for 1% -> 35% of each run, Pallas kernels for 0% -> 4%
where the time goes in v1:
time: 1170 us; the launch traced here: 1160 us
  waiting for transfers between devices  446 us (38%)
  matrix products  328 us (28%)
  other arithmetic  156 us (13%)
  starting transfers between devices  74.3 us (6%)
  Pallas kernels  72.8 us (6%)
  local copies, waits for them, and re-layouts  62.9 us (5%)
  between operations  16.4 us (1%)
    all_gather x1, waiting for transfers between devices, per_device(): lax.all_gather(own_slice(0, owner_rows), ('shard', 'wide'), axis=0, tiled...  122 us
    dot_general x10, matrix products, contract_rows(): lax.dot_general(left_side, right_side, (((0,), (0,)), ((), ())), preferre...  110 us
    dot_general x4, matrix products, times_transposed(): lax.dot_general(left_side, right_side, (((1,), (1,)), ((), ())), preferre...  99.3 us
    pallas_call x2, Pallas kernels, adam_rows(): pl.pallas_call(body, grid=(count // block,), in_specs=[pl.BlockSpec((bloc...  72.8 us
    ppermute x7, waiting for transfers between devices, spread_first(): other = lax.ppermute(block, 'wide', [(i, i ^ bit) for i in range(8)])  68.2 us
    reduce_scatter x1, waiting for transfers between devices, plane_sum(): lax.psum_scatter(plane_terms(first, last), 'wide', scatter_dimension=0, t...  59.5 us
    ppermute x16, waiting for transfers between devices, advance(): steps[key].append(add_low(held, lax.ppermute(held, 'shard', pairs)))  58.3 us
    reduce_scatter x3, waiting for transfers between devices, start_ready(): lax.psum_scatter(term, 'wide', scatter_dimension=0, tiled=True)  55.6 us
  transfers between devices with their start and end apart: 44, of which 21 were waited for; matrix products, arithmetic and copies ran while one was open for 35% of the time, Pallas kernels for 4%

profile of v1, /device:TPU:0, one launch (start us, length us, event | category | flops | bytes accessed | tf_op | source)
XLA Modules:
  0.0 1157.3 jit_solution(12509120597692218187)
XLA Ops:
  19.1 24.9 %collective-permute-done.3 = bf16[320,1152]{1,0:T(8,128)(2,1)} collective-permute-done((bf16[320,1152]{1,0:T(8,128)(2,1)S(1)}, bf16[320,1152]{1,0:T(8,128)(2,1)}, u32[]{:S(2)}, u32[]{:S(2)}) %collective-permute-start.3) | collective-permute-done | bytes 737312 | tf_op jit(solution)/shard_map/ppermute | solution.py:132
  54.7 23.6 %collective-permute-done.4 = bf16[320,1152]{1,0:T(8,128)(2,1)} collective-permute-done((bf16[320,1152]{1,0:T(8,128)(2,1)S(1)}, bf16[320,1152]{1,0:T(8,128)(2,1)}, u32[]{:S(2)}, u32[]{:S(2)}) %collective-permute-start.4) | collective-permute-done | bytes 737312 | tf_op jit(solution)/shard_map/ppermute | solution.py:134
  83.4 11.5 collective-permute-done.5
  102.6 30.2 %collective-permute-done.6 = bf16[320,1152]{1,0:T(8,128)(2,1)} collective-permute-done((bf16[320,1152]{1,0:T(8,128)(2,1)}, bf16[320,1152]{1,0:T(8,128)(2,1)}, u32[]{:S(2)}, u32[]{:S(2)}) %collective-permute-start.6) | collective-permute-done | bytes 737312 | tf_op jit(solution)/shard_map/ppermute | solution.py:142
  137.0 25.2 %collective-permute-done.9 = bf16[320,1152]{1,0:T(8,128)(2,1)} collective-permute-done((bf16[320,1152]{1,0:T(8,128)(2,1)}, bf16[320,1152]{1,0:T(8,128)(2,1)}, u32[]{:S(2)}, u32[]{:S(2)}) %collective-permute-start.9) | collective-permute-done | bytes 737312 | tf_op jit(solution)/shard_map/ppermute | solution.py:142
  195.4 27.3 %while.31 = (s32[]{:T(128)}, bf16[2,512,1,4,256]{4,1,3,2,0:T(8,128)(2,1)}, f32[2,1,4,512,1]{3,2,4,1,0:T(4,128)S(1)}, s32[2,512]{1,0:T(2,128)S(1)}, s32[1024]{0:T...) while((s32[]{:T(128)}, ...), condition=%wide.region_6.7_spmd.clone, body=%wide.region_3.6_spmd.sunk.clone | while | flops 2186279424 | bytes 50411736 | solution.py:278
  237.6 121.9 %all-gather.4.cloned.1.call-done = bf16[23296,1152]{1,0:T(8,128)(2,1)} async-done(((bf16[728,1152]{1,0:T(8,128)(2,1)}), bf16[23296,1152]{1,0:T(8,128)(2,1)}) %all-gather.4.cloned.1.call-update) | async-done | bytes 53674000 | tf_op jit(solution)/shard_map/all_gather | solution.py:225
  359.5 44.1 %fusion.75 = f32[1024,13824]{1,0:T(8,128)} fusion(bf16[1024,1152]{1,0:T(8,128)(2,1)S(1)} %multiply_convert_fusion.2, bf16[23296,1152]{1,0:T(8,128)(2,1)} %all-gather.4.cloned.1.call-done), kind=kOutput, calls=%fused_computation.92 | convolution fusion | flops 32614907904 | bytes 90832896 | tf_op jit(solution)/shard_map/dot_general | solution.py:76
  403.6 24.9 %multiply_convert_fusion.1 = bf16[1024,6912]{1,0:T(8,128)(2,1)} fusion(f32[1024,13824]{1,0:T(8,128)} %fusion.75), kind=kLoop, calls=%fused_computation.89 | loop fusion | flops 70778880 | bytes 70778880 | tf_op jit(solution)/shard_map/convert_element_type | solution.py:287
  428.5 23.3 %multiply_reduce_fusion.4 = (f32[1024]{0:T(1024)S(1)}, f32[1024,1152]{1,0:T(8,128)S(1)}) fusion(bf16[1024,6912]{1,0:T(8,128)(2,1)} %multiply_convert_fusion.1, bf16[23296,1152]{1,0:T(8,128)(2,1)} %all-gather.4.cloned.1.call-done), kind=kOutput, calls=%fused_computation.147 | convolution fusion | flops 16309812224 | bytes 34803712 | tf_op jit(solution)/shard_map/dot_general | solution.py:288
  456.7 12.6 %convolution_convert_fusion.6 = bf16[2560,1152]{1,0:T(8,128)(2,1)} fusion(bf16[1024,1152]{1,0:T(8,128)(2,1)S(1)} %get-tuple-element.233, bf16[1024,6912]{1,0:T(8,128)(2,1)} %multiply_convert_fusion.1), kind=kOutput, calls=%fused_computation.105 | convolution fusion | flops 6042746880 | bytes 13500416 | tf_op jit(solution)/shard_map/dot_general | solution.py:70
  469.3 14.6 %convolution_convert_fusion.2 = bf16[3264,1152]{1,0:T(8,128)(2,1)} fusion(bf16[1024,1152]{1,0:T(8,128)(2,1)S(1)} %get-tuple-element.233, bf16[1024,6912]{1,0:T(8,128)(2,1)} %multiply_convert_fusion.1), kind=kOutput, calls=%fused_computation.97 | convolution fusion | flops 7704502272 | bytes 16695296 | tf_op jit(solution)/shard_map/dot_general | solution.py:70
  484.0 46.3 %fusion.72 = (bf16[1024,6912]{1,0:T(8,128)(2,1)}, bf16[1024,6912]{1,0:T(8,128)(2,1)}) fusion(f32[1024,13824]{1,0:T(8,128)} %fusion.75, bf16[1024,1152]{1,0:T(8,128)(2,1)S(1)} %get-tuple-element.233, bf16[23296,1152]{1,0:T(8,128)(2,1)} %all-gather.4.cloned.1.call-done), kind=kOutput, calls=%fused_computation.87 | convolution fusion | flops 16477323264 | bytes 103219200 | tf_op jit(solution)/shard_map/dot_general | solution.py:76
  530.3 14.0 %convolution_convert_fusion.1 = bf16[3264,1152]{1,0:T(8,128)(2,1)} fusion(bf16[1024,1152]{1,0:T(8,128)(2,1)} %copy-done.24, bf16[1024,6912]{1,0:T(8,128)(2,1)} %get-tuple-element.441), kind=kOutput, calls=%fused_computation.96 | convolution fusion | flops 7704502272 | bytes 16695296 | tf_op jit(solution)/shard_map/dot_general | solution.py:70
  546.3 16.1 %convolution_convert_fusion = bf16[3264,1152]{1,0:T(8,128)(2,1)} fusion(bf16[1024,1152]{1,0:T(8,128)(2,1)S(1)} %copy-done.25, bf16[1024,6912]{1,0:T(8,128)(2,1)} %get-tuple-element.441, bf16[1024,6912]{1,0:T(8,128)(2,1)} %get-tuple-element.442), kind=kOutput, calls=%fused_computation.95 | convolution fusion | flops 7717871616 | bytes 38191104 | tf_op jit(solution)/shard_map/dot_general | solution.py:70
  568.2 11.2 convolution_convert_fusion.5
  587.2 11.9 %convolution_convert_fusion.4 = bf16[2560,1152]{1,0:T(8,128)(2,1)} fusion(bf16[1024,1152]{1,0:T(8,128)(2,1)S(1)} %copy-done.27, bf16[1024,6912]{1,0:T(8,128)(2,1)} %get-tuple-element.441), kind=kOutput, calls=%fused_computation.103 | convolution fusion | flops 6042746880 | bytes 13500416 | tf_op jit(solution)/shard_map/dot_general | solution.py:70
  599.2 11.5 convolution_convert_fusion.3
  610.7 20.6 %pad_maximum_fusion = bf16[1024,13824]{1,0:T(8,128)(2,1)} fusion(bf16[1024,6912]{1,0:T(8,128)(2,1)} %get-tuple-element.442, bf16[1024,6912]{1,0:T(8,128)(2,1)} %get-tuple-element.441), kind=kLoop, calls=%fused_computation.79 | loop fusion | flops 56623104 | bytes 56623104 | tf_op jit(solution)/shard_map/concatenate | solution.py:348
  637.0 43.9 %fusion.73 = f32[1024,1152]{1,0:T(8,128)} fusion(bf16[1024,13824]{1,0:T(8,128)(2,1)} %pad_maximum_fusion, bf16[23296,1152]{1,0:T(8,128)(2,1)} %all-gather.4.cloned.1.call-done), kind=kOutput, calls=%fused_computation.90 | convolution fusion | flops 32614907904 | bytes 64880640 | tf_op jit(solution)/shard_map/dot_general | solution.py:352
  724.5 16.1 %reduce-scatter.29.cloned.1.call-done = bf16[408,1152]{1,0:T(8,128)(2,1)} async-done(((bf16[3264,1152]{1,0:T(8,128)(2,1)}), bf16[408,1152]{1,0:T(8,128)(2,1)}) %reduce-scatter.29.cloned.1.call-update) | async-done | bytes 940048 | tf_op jit(solution)/shard_map/optimization_barrier | solution.py:162
  744.9 49.6 %while.32 = (s32[]{:T(128)}, f32[1024,1,256]{0,2,1:T(8,128)S(1)}, f32[1024,1,256]{0,2,1:T(8,128)}, f32[2,512,1,4,256]{4,1,3,2,0:T(8,128)}, bf16[2,512,1,4,256]{4...) while((s32[]{:T(128)}, f32[1024,1,256]{0,2,1:T(8,128)S(1)}, ...), condition=%wide.region_19.20_spmd.clone.clone, body=%wide.region_17.19_spmd.clone.sunk.clone | while | flops 5423233536 | bytes 125376864 | solution.py:396
  801.8 10.3 reduce-scatter.31.cloned.1.call-done
  838.4 15.9 %collective-permute-done.24 = bf16[408,1152]{1,0:T(8,128)(2,1)S(1)} collective-permute-done((bf16[408,1152]{1,0:T(8,128)(2,1)}, bf16[408,1152]{1,0:T(8,128)(2,1)S(1)}, u32[]{:S(2)}, u32[]{:S(2)}) %collective-permute-start.24) | collective-permute-done | bytes 940064 | tf_op jit(solution)/shard_map/ppermute | solution.py:334
  875.2 14.9 %collective-permute-start.19 = (bf16[320,1152]{1,0:T(8,128)(2,1)}, bf16[320,1152]{1,0:T(8,128)(2,1)}, u32[]{:S(2)}, u32[]{:S(2)}) collective-permute-start(bf16[320,1152]{1,0:T(8,128)(2,1)} %reduce-scatter.21.cloned.1.call-done), channel_id=1, source_target_pairs={{0,1},{3,2},{4,5},{7,6},{8,9},{11,10},{12,13},{15,14},{16,17},{19,... | collective-permute-start | bytes 2211848 | tf_op jit(solution)/shard_map/ppermute | solution.py:334
  890.1 48.3 %reduce-scatter.19.cloned.1.call-done = bf16[320,1152]{1,0:T(8,128)(2,1)} async-done(((bf16[2560,1152]{1,0:T(8,128)(2,1)}), bf16[320,1152]{1,0:T(8,128)(2,1)}) %reduce-scatter.19.cloned.1.call-update) | async-done | bytes 737296 | tf_op jit(solution)/shard_map/reduce_scatter | solution.py:326
  942.6 59.5 %reduce-scatter.23.cloned.1.call-done = bf16[320,1152]{1,0:T(8,128)(2,1)} async-done(((bf16[2560,1152]{1,0:T(8,128)(2,1)}), bf16[320,1152]{1,0:T(8,128)(2,1)}) %reduce-scatter.23.cloned.1.call-update) | async-done | bytes 737296 | tf_op jit(solution)/shard_map/reduce_scatter | solution.py:313
  1008.9 13.5 %collective-permute-done.21 = bf16[320,1152]{1,0:T(8,128)(2,1)S(1)} collective-permute-done((bf16[320,1152]{1,0:T(8,128)(2,1)}, bf16[320,1152]{1,0:T(8,128)(2,1)S(1)}, u32[]{:S(2)}, u32[]{:S(2)}) %collective-permute-start.21) | collective-permute-done | bytes 737312 | tf_op jit(solution)/shard_map/ppermute | solution.py:334
  1024.2 18.5 %collective-permute-done.22 = bf16[320,1152]{1,0:T(8,128)(2,1)S(1)} collective-permute-done((bf16[320,1152]{1,0:T(8,128)(2,1)S(1)}, bf16[320,1152]{1,0:T(8,128)(2,1)S(1)}, u32[]{:S(2)}, u32[]{:S(2)}) %collective-permute-start.22) | collective-permute-done | bytes 737312 | tf_op jit(solution)/shard_map/ppermute | solution.py:334
  1045.6 8.2 fusion.93
  1074.8 42.4 %adam_rows.2 = (f32[5824,1152]{1,0:T(8,128)}, f32[5824,1152]{1,0:T(8,128)}, f32[5824,1152]{1,0:T(8,128)}, f32[5824,1152]{1,0:T(8,128)}) custom-call(bf16[3264,1152]{1,0:T(8,128)(2,1)} %all-gather.8.cloned.1.call-done.grad_ref, f32[5824,1152]{1,0:T(8,128)} %param_ref.3, f32[5824,1152]{1,0:T(8,128)} %first_ref.3, f32[5824,1152]{1,0:T(8,128)} %second_ref.3), custom_call_target="tpu_custom_call" | custom-call | flops 75202560 | bytes 112803840 | tf_op jit(solution)/shard_map/adam_rows/pallas_call | solution.py:192
  1119.9 30.4 %adam_rows.3 = (f32[5824,1152]{1,0:T(8,128)}, f32[5824,1152]{1,0:T(8,128)}, f32[5824,1152]{1,0:T(8,128)}, f32[5824,1152]{1,0:T(8,128)}) custom-call(bf16[2560,1152]{1,0:T(8,128)(2,1)S(1)} %copy-done, f32[5824,1152]{1,0:T(8,128)} %param_ref.3, f32[5824,1152]{1,0:T(8,128)} %first_ref.3, ...), custom_call_target="tpu_custom_call", output_to_operand_aliasing={{0}: (4, {}), {1}: (5, {}), {2}: (6, {}), {3}: (7, {})} | custom-call | flops 58982400 | bytes 88473600 | tf_op jit(solution)/shard_map/adam_rows/pallas_call | solution.py:192
  (442 shorter events, 329.4 us)
Async XLA Ops:
  7.2 352.3 %all-gather.4.cloned.1.call-start = ((), (), s32[]{:S(2)}) async-start(), calls=%async_computation.8 | async-start | bytes 55351296 | tf_op jit(solution)/shard_map/all_gather | solution.py:225
  10.6 620.8 %reduce-scatter.17.cloned.1.call-start = ((), (), s32[]{:S(2)}) async-start(), calls=%async_computation.9 | async-start | bytes 6635520 | tf_op jit(solution)/shard_map/reduce_scatter | solution.py:326
  12.2 31.8 %collective-permute-start.3 = (bf16[320,1152]{1,0:T(8,128)(2,1)S(1)}, bf16[320,1152]{1,0:T(8,128)(2,1)}, u32[]{:S(2)}, u32[]{:S(2)}) collective-permute-start(bf16[320,1152]{1,0:T(8,128)(2,1)S(1)} %dynamic-slice_convert_fusion.1), channel_id=1, source_target_pairs={{0,2},{4,6},{8,10},{12,14},{16,18},{20,22},{24,26},{28,30}} | collective-permute-start | bytes 2211848 | tf_op jit(solution)/shard_map/ppermute | solution.py:132
  45.6 32.7 %collective-permute-start.4 = (bf16[320,1152]{1,0:T(8,128)(2,1)S(1)}, bf16[320,1152]{1,0:T(8,128)(2,1)}, u32[]{:S(2)}, u32[]{:S(2)}) collective-permute-start(bf16[320,1152]{1,0:T(8,128)(2,1)S(1)} %broadcast_select_fusion), channel_id=1, source_target_pairs={{0,1},{2,3},{4,5},{6,7},{8,9},{10,11},{12,13},{14,15},{16,17},{18,... | collective-permute-start | bytes 2211848 | tf_op jit(solution)/shard_map/ppermute | solution.py:134
  47.7 88.3 %collective-permute-start.2 = (bf16[4,288]{1,0:T(4,128)(2,1)S(1)}, bf16[4,288]{1,0:T(4,128)(2,1)S(1)}, u32[]{:S(2)}, u32[]{:S(2)}) collective-permute-start(bf16[4,288]{1,0:T(4,128)(2,1)S(1)} %convert_element_type.267), channel_id=1, source_target_pairs={{0,3},{1,0},{2,1},{3,2},{4,7},{5,4},{6,5},{7,6},{8,11},{9,8},{10,9... | collective-permute-start | bytes 6920 | tf_op jit(solution)/shard_map/ppermute | solution.py:124
  47.7 87.9 %collective-permute-start.1 = (bf16[4,288]{1,0:T(4,128)(2,1)S(1)}, bf16[4,288]{1,0:T(4,128)(2,1)S(1)}, u32[]{:S(2)}, u32[]{:S(2)}) collective-permute-start(bf16[4,288]{1,0:T(4,128)(2,1)S(1)} %convert_element_type.267), channel_id=1, source_target_pairs={{0,2},{1,3},{2,0},{3,1},{4,6},{5,7},{6,4},{7,5},{8,10},{9,11},{10,... | collective-permute-start | bytes 6920 | tf_op jit(solution)/shard_map/ppermute | solution.py:124
  51.5 83.8 %collective-permute-start = (bf16[4,288]{1,0:T(4,128)(2,1)S(1)}, bf16[4,288]{1,0:T(4,128)(2,1)S(1)}, u32[]{:S(2)}, u32[]{:S(2)}) collective-permute-start(bf16[4,288]{1,0:T(4,128)(2,1)S(1)} %convert_element_type.267), channel_id=1, source_target_pairs={{0,1},{1,2},{2,3},{3,0},{4,5},{5,6},{6,7},{7,4},{8,9},{9,10},{10,1... | collective-permute-start | bytes 6920 | tf_op jit(solution)/shard_map/ppermute | solution.py:124
  97.3 35.5 %collective-permute-start.6 = (bf16[320,1152]{1,0:T(8,128)(2,1)}, bf16[320,1152]{1,0:T(8,128)(2,1)}, u32[]{:S(2)}, u32[]{:S(2)}) collective-permute-start(bf16[320,1152]{1,0:T(8,128)(2,1)} %get-tuple-element.457), channel_id=1, source_target_pairs={{0,8},{4,12},{8,0},{12,4},{16,24},{20,28},{24,16},{28,20},{1,9},{5... | collective-permute-start | bytes 2211848 | tf_op jit(solution)/shard_map/ppermute | solution.py:142
  101.7 60.4 %collective-permute-start.9 = (bf16[320,1152]{1,0:T(8,128)(2,1)}, bf16[320,1152]{1,0:T(8,128)(2,1)}, u32[]{:S(2)}, u32[]{:S(2)}) collective-permute-start(bf16[320,1152]{1,0:T(8,128)(2,1)} %get-tuple-element.456), channel_id=1, source_target_pairs={{0,8},{4,12},{8,0},{12,4},{16,24},{20,28},{24,16},{28,20},{1,9},{5... | collective-permute-start | bytes 2211848 | tf_op jit(solution)/shard_map/ppermute | solution.py:142
  135.1 29.9 %collective-permute-start.7 = (bf16[320,1152]{1,0:T(8,128)(2,1)}, bf16[320,1152]{1,0:T(8,128)(2,1)}, u32[]{:S(2)}, u32[]{:S(2)}) collective-permute-start(bf16[320,1152]{1,0:T(8,128)(2,1)} %get-tuple-element.459), channel_id=1, source_target_pairs={{0,4},{4,0},{8,12},{12,8},{16,20},{20,16},{24,28},{28,24},{1,5},{5... | collective-permute-start | bytes 2211848 | tf_op jit(solution)/shard_map/ppermute | solution.py:142
  164.5 62.9 %collective-permute-start.11 = (bf16[320,1152]{1,0:T(8,128)(2,1)}, bf16[320,1152]{1,0:T(8,128)(2,1)}, u32[]{:S(2)}, u32[]{:S(2)}) collective-permute-start(bf16[320,1152]{1,0:T(8,128)(2,1)} %get-tuple-element.454), channel_id=1, source_target_pairs={{0,4},{4,0},{8,12},{12,8},{16,20},{20,16},{24,28},{28,24},{1,5},{5... | collective-permute-start | bytes 2211848 | tf_op jit(solution)/shard_map/ppermute | solution.py:142
  469.2 162.2 %reduce-scatter.25.cloned.1.call-start = ((), (), s32[]{:S(2)}) async-start(), calls=%async_computation.15 | async-start | bytes 8460288
  483.9 199.3 %reduce-scatter.27.cloned.1.call-start = ((), (), s32[]{:S(2)}) async-start(), calls=%async_computation.16 | async-start | bytes 8460288
  544.3 196.2 %reduce-scatter.29.cloned.1.call-start = ((), (), s32[]{:S(2)}) async-start(), calls=%async_computation.17 | async-start | bytes 8460288
  562.5 249.6 %reduce-scatter.31.cloned.1.call-start = ((), (), s32[]{:S(2)}) async-start(), calls=%async_computation.18 | async-start | bytes 8460288
  585.5 289.7 %reduce-scatter.21.cloned.1.call-start = ((), (), s32[]{:S(2)}) async-start(), calls=%async_computation.11 | async-start | bytes 6635520 | tf_op jit(solution)/shard_map/reduce_scatter | solution.py:326
  599.1 339.3 %reduce-scatter.19.cloned.1.call-start = ((), (), s32[]{:S(2)}) async-start(), calls=%async_computation.10 | async-start | bytes 6635520 | tf_op jit(solution)/shard_map/reduce_scatter | solution.py:326
  631.3 370.8 %reduce-scatter.23.cloned.1.call-start = ((), (), s32[]{:S(2)}) async-start(), calls=%async_computation.12 | async-start | bytes 6635520 | tf_op jit(solution)/shard_map/reduce_scatter | solution.py:313
  631.4 49.6 %collective-permute-start.13 = (bf16[320,1152]{1,0:T(8,128)(2,1)}, bf16[320,1152]{1,0:T(8,128)(2,1)S(1)}, u32[]{:S(2)}, u32[]{:S(2)}) collective-permute-start(bf16[320,1152]{1,0:T(8,128)(2,1)} %reduce-scatter.17.cloned.1.call-done), channel_id=1, source_target_pairs={{0,1},{2,3},{4,5},{6,7},{8,9},{10,11},{12,13},{14,15},{16,17},{18,... | collective-permute-start | bytes 2211848 | tf_op jit(solution)/shard_map/ppermute | solution.py:334
  635.7 46.4 %collective-permute-start.12 = (bf16[408,1152]{1,0:T(8,128)(2,1)}, bf16[408,1152]{1,0:T(8,128)(2,1)S(1)}, u32[]{:S(2)}, u32[]{:S(2)}) collective-permute-start(bf16[408,1152]{1,0:T(8,128)(2,1)} %reduce-scatter.25.cloned.1.call-done), channel_id=1, source_target_pairs={{0,1},{2,3},{4,5},{6,7},{8,9},{10,11},{12,13},{14,15},{16,17},{18,... | collective-permute-start | bytes 2820104 | tf_op jit(solution)/shard_map/ppermute | solution.py:334
  696.9 24.9 %collective-permute-start.14 = (bf16[408,1152]{1,0:T(8,128)(2,1)}, bf16[408,1152]{1,0:T(8,128)(2,1)}, u32[]{:S(2)}, u32[]{:S(2)}) collective-permute-start(bf16[408,1152]{1,0:T(8,128)(2,1)} %reduce-scatter.27.cloned.1.call-done), channel_id=1, source_target_pairs={{3,2},{1,0},{7,6},{5,4},{11,10},{9,8},{15,14},{13,12},{19,18},{17,... | collective-permute-start | bytes 2820104 | tf_op jit(solution)/shard_map/ppermute | solution.py:334
  740.5 58.9 %collective-permute-start.15 = (bf16[408,1152]{1,0:T(8,128)(2,1)}, bf16[408,1152]{1,0:T(8,128)(2,1)}, u32[]{:S(2)}, u32[]{:S(2)}) collective-permute-start(bf16[408,1152]{1,0:T(8,128)(2,1)} %reduce-scatter.29.cloned.1.call-done), channel_id=1, source_target_pairs={{0,1},{3,2},{4,5},{7,6},{8,9},{11,10},{12,13},{15,14},{16,17},{19,... | collective-permute-start | bytes 2820104 | tf_op jit(solution)/shard_map/ppermute | solution.py:334
  830.3 244.5 %all-gather.8.cloned.1.call-start = ((), (), s32[]{:S(2)}) async-start(), calls=%async_computation.14 | async-start | bytes 8460288 | tf_op jit(solution)/shard_map/all_gather | solution.py:436
  830.3 24.0 %collective-permute-start.24 = (bf16[408,1152]{1,0:T(8,128)(2,1)}, bf16[408,1152]{1,0:T(8,128)(2,1)S(1)}, u32[]{:S(2)}, u32[]{:S(2)}) collective-permute-start(bf16[408,1152]{1,0:T(8,128)(2,1)} %reduce-scatter.31.cloned.1.call-done), channel_id=1, source_target_pairs={{3,2},{0,1},{7,6},{4,5},{11,10},{8,9},{15,14},{12,13},{19,18},{16,... | collective-permute-start | bytes 2820104 | tf_op jit(solution)/shard_map/ppermute | solution.py:334
  833.9 24.4 %collective-permute-start.23 = (bf16[408,1152]{1,0:T(8,128)(2,1)}, bf16[408,1152]{1,0:T(8,128)(2,1)}, u32[]{:S(2)}, u32[]{:S(2)}) collective-permute-start(bf16[408,1152]{1,0:T(8,128)(2,1)} %add_convert_fusion.9), channel_id=1, source_target_pairs={{1,3},{5,7},{9,11},{13,15},{17,19},{21,23},{25,27},{29,31}} | collective-permute-start | bytes 2820104 | tf_op jit(solution)/shard_map/ppermute | solution.py:334
  835.5 26.8 %collective-permute-start.27 = (bf16[408,1152]{1,0:T(8,128)(2,1)}, bf16[408,1152]{1,0:T(8,128)(2,1)}, u32[]{:S(2)}, u32[]{:S(2)}) collective-permute-start(bf16[408,1152]{1,0:T(8,128)(2,1)} %add_convert_fusion.8), channel_id=1, source_target_pairs={{2,0},{6,4},{10,8},{14,12},{18,16},{22,20},{26,24},{30,28}} | collective-permute-start | bytes 2820104 | tf_op jit(solution)/shard_map/ppermute | solution.py:334
  836.8 25.5 %collective-permute-start.26 = (bf16[408,1152]{1,0:T(8,128)(2,1)}, bf16[408,1152]{1,0:T(8,128)(2,1)}, u32[]{:S(2)}, u32[]{:S(2)}) collective-permute-start(bf16[408,1152]{1,0:T(8,128)(2,1)} %add_convert_fusion.7), channel_id=1, source_target_pairs={{2,1},{6,5},{10,9},{14,13},{18,17},{22,21},{26,25},{30,29}} | collective-permute-start | bytes 2820104 | tf_op jit(solution)/shard_map/ppermute | solution.py:334
  867.8 249.4 %all-gather.6.cloned.1.call-start = ((), (), s32[]{:S(2)}) async-start(), calls=%async_computation.13 | async-start | bytes 6635520 | tf_op jit(solution)/shard_map/all_gather | solution.py:437
  875.2 128.3 %collective-permute-start.19 = (bf16[320,1152]{1,0:T(8,128)(2,1)}, bf16[320,1152]{1,0:T(8,128)(2,1)}, u32[]{:S(2)}, u32[]{:S(2)}) collective-permute-start(bf16[320,1152]{1,0:T(8,128)(2,1)} %reduce-scatter.21.cloned.1.call-done), channel_id=1, source_target_pairs={{0,1},{3,2},{4,5},{7,6},{8,9},{11,10},{12,13},{15,14},{16,17},{19,... | collective-permute-start | bytes 2211848 | tf_op jit(solution)/shard_map/ppermute | solution.py:334
  938.4 67.4 %collective-permute-start.17 = (bf16[320,1152]{1,0:T(8,128)(2,1)}, bf16[320,1152]{1,0:T(8,128)(2,1)}, u32[]{:S(2)}, u32[]{:S(2)}) collective-permute-start(bf16[320,1152]{1,0:T(8,128)(2,1)} %reduce-scatter.19.cloned.1.call-done), channel_id=1, source_target_pairs={{3,2},{0,1},{7,6},{4,5},{11,10},{8,9},{15,14},{12,13},{19,18},{16,... | collective-permute-start | bytes 2211848 | tf_op jit(solution)/shard_map/ppermute | solution.py:334
  1002.1 20.3 %collective-permute-start.21 = (bf16[320,1152]{1,0:T(8,128)(2,1)}, bf16[320,1152]{1,0:T(8,128)(2,1)S(1)}, u32[]{:S(2)}, u32[]{:S(2)}) collective-permute-start(bf16[320,1152]{1,0:T(8,128)(2,1)} %reduce-scatter.23.cloned.1.call-done), channel_id=1, source_target_pairs={{3,2},{1,0},{7,6},{5,4},{11,10},{9,8},{15,14},{13,12},{19,18},{17,... | collective-permute-start | bytes 2211848 | tf_op jit(solution)/shard_map/ppermute | solution.py:334
  1022.6 20.1 %collective-permute-start.22 = (bf16[320,1152]{1,0:T(8,128)(2,1)S(1)}, bf16[320,1152]{1,0:T(8,128)(2,1)S(1)}, u32[]{:S(2)}, u32[]{:S(2)}) collective-permute-start(bf16[320,1152]{1,0:T(8,128)(2,1)S(1)} %add_convert_fusion.11), channel_id=1, source_target_pairs={{2,0},{6,4},{10,8},{14,12},{18,16},{22,20},{26,24},{30,28}} | collective-permute-start | bytes 2211848 | tf_op jit(solution)/shard_map/ppermute | solution.py:334
  (117 other events, 2412.3 us)
Sparse Core Ops, SparseCore 0:
  11.5 347.9 all-gather.3
  469.4 57.7 reduce-scatter.16
  531.3 67.4 reduce-scatter.24
  602.1 67.5 reduce-scatter.26
  672.9 67.5 reduce-scatter.28
  744.4 67.5 reduce-scatter.30
  815.5 59.6 reduce-scatter.20
  878.7 59.6 reduce-scatter.18
  942.4 59.6 reduce-scatter.22
  1004.4 50.5 all-gather.7
  1056.9 43.7 all-gather.5

commit v2 on v1

--- a/solution.py
+++ b/solution.py
@@ -170,16 +170,15 @@
     return own
 
 
-def row_block(count):
-    return max(size for size in range(8, 329, 8) if count % size == 0)
-
-
-def adam_rows(first, grad_low, state, carried):
+def adam_rows(place, block, grad_low, state, carried):
     count = grad_low.shape[0]
-    block = row_block(count)
-    spec = pl.BlockSpec((pl.Element(block), pl.Element(D)), lambda i: (pl.multiple_of(first + i * block, 8), 0))
-
-    def body(grad_ref, param_ref, first_ref, second_ref, *rest):
+
+    def rows_of(i, place_ref):
+        return (pl.multiple_of(place_ref[0] + i * place_ref[1], 8), 0)
+
+    spec = pl.BlockSpec((pl.Element(block), pl.Element(D)), rows_of)
+
+    def body(place_ref, grad_ref, param_ref, first_ref, second_ref, *rest):
         out_refs = rest[-4:]
         grad = grad_ref[...].astype(jnp.float32)
         param_new, first_new, second_new = adam_update(
@@ -191,19 +190,22 @@
     shape = jax.ShapeDtypeStruct(state[0].shape, jnp.float32)
     return pl.pallas_call(
         body,
-        grid=(count // block,),
-        in_specs=[pl.BlockSpec((block, D), lambda i: (i, 0))]
-        + [spec] * 3
-        + [pl.BlockSpec(memory_space=pl.ANY)] * len(carried),
-        out_specs=[spec] * 4,
+        grid_spec=pltpu.PrefetchScalarGridSpec(
+            num_scalar_prefetch=1,
+            grid=(count // block,),
+            in_specs=[pl.BlockSpec((block, D), lambda i, place_ref: (i, 0))]
+            + [spec] * 3
+            + [pl.BlockSpec(memory_space=pl.ANY)] * len(carried),
+            out_specs=[spec] * 4,
+        ),
         out_shape=[shape] * 4,
-        input_output_aliases={4 + k: k for k in range(len(carried))},
+        input_output_aliases={5 + k: k for k in range(len(carried))},
         cost_estimate=pl.CostEstimate(
             flops=20 * count * D, transcendentals=count * D, bytes_accessed=30 * count * D
         ),
-        compiler_params=pltpu.CompilerParams(vmem_limit_bytes=48 * 2**20),
+        compiler_params=pltpu.CompilerParams(vmem_limit_bytes=56 * 2**20),
         name="adam_rows",
-    )(grad_low, *state, *carried)
+    )(place, grad_low, *state, *carried)
 
 
 def per_device(
@@ -293,11 +295,11 @@
     branch_low = branch_grad.astype(jnp.bfloat16)
     tree = wide_count == 8 and shard_count == 4
     factors = {"down": (gate_end, total_rows, hidden_low, branch_low)}
-    reduced, steps = {}, {}
-
-    def bounds(owner, part):
-        edges = (0, early_rows, owner_rows)
-        return owner * owner_rows + edges[part], owner * owner_rows + edges[part + 1]
+    steps = {}
+    late_rows = qkv_rows
+
+    def bounds(key):
+        return (max(key * owner_rows, late_rows), (key + 1) * owner_rows)
 
     def plane_terms(first, last):
         parts = [
@@ -309,27 +311,21 @@
         ]
         return parts[0] if len(parts) == 1 else jnp.concatenate(parts, axis=0)
 
-    def plane_sum(first, last):
-        return lax.psum_scatter(
-            plane_terms(first, last), "wide", scatter_dimension=0, tiled=True
-        )
-
     def start_ready(anchor, lowest):
         keys = [
-            (owner, part)
-            for part in (1, 0)
-            for owner in range(shard_count)
-            if (owner, part) not in reduced and bounds(owner, part)[0] >= lowest
+            key
+            for key in reversed(range(shard_count))
+            if key not in steps and bounds(key)[0] >= lowest
         ]
-        terms = [plane_terms(*bounds(*key)) for key in keys]
+        if not tree or not keys:
+            return anchor
+        terms = [plane_terms(*bounds(key)) for key in keys]
         for key, term in zip(keys, terms):
-            reduced[key] = lax.psum_scatter(term, "wide", scatter_dimension=0, tiled=True)
-            steps[key] = [reduced[key]]
+            steps[key] = [lax.psum_scatter(term, "wide", scatter_dimension=0, tiled=True)]
         return tied(anchor, terms)[0]
 
     def advance(key):
-        owner, _ = key
-        pairs = owner_tree[owner][len(steps[key]) - 1]
+        pairs = owner_tree[max(key, 0)][len(steps[key]) - 1]
         held = steps[key][-1]
         steps[key].append(add_low(held, lax.ppermute(held, "shard", pairs)))
 
@@ -345,12 +341,15 @@
     branch_low = start_ready(branch_low, gate_end)
     hidden_grad = times_transposed(branch_low, w_down)
     gate_grad, up_grad = pull_fourth(hidden_grad)
-    gate_up_low = jnp.concatenate([gate_grad, up_grad], axis=1).astype(jnp.bfloat16)
-    factors["gate_up"] = (out_end, gate_end, gate_up_low, ffn_low)
-    gate_up_low = start_ready(gate_up_low, out_end)
-    gate_up_low = tick(gate_up_low, (3, 1), (3, 0))
-    ffn_input_grad = jnp.dot(gate_up_low, w_gate_up, preferred_element_type=jnp.float32)
-    ffn_input_grad = tick(ffn_input_grad, (3, 1), (3, 0), (0, 1))
+    gate_low, up_low = gate_grad.astype(jnp.bfloat16), up_grad.astype(jnp.bfloat16)
+    factors["gate"] = (out_end, out_end + FF, gate_low, ffn_low)
+    factors["up"] = (out_end + FF, gate_end, up_low, ffn_low)
+    gate_low, up_low = start_ready((gate_low, up_low), out_end)
+    gate_low, up_low = tick((gate_low, up_low), 3)
+    ffn_input_grad = jnp.dot(
+        gate_low, w_gate_up[:FF], preferred_element_type=jnp.float32
+    ) + jnp.dot(up_low, w_gate_up[FF:], preferred_element_type=jnp.float32)
+    ffn_input_grad = tick(ffn_input_grad, 3)
     sum_grad_part, gain_three = pull_third(ffn_input_grad)
     sum_grad = upstream + sum_grad_part
     attended_grad, gain_two = pull_second(sum_grad)
@@ -362,7 +361,8 @@
         .reshape(block_count, block_rows, KV_HEADS, per_group, HD)
     )
 
-    mixed_grad = tick(mixed_grad, (0, 1), (1, 1))
+    mixed_grad = start_ready(mixed_grad, late_rows)
+    mixed_grad = tick(mixed_grad, 2)
 
     def backward_block(running, inputs_block):
         key_acc, value_acc = running
@@ -398,7 +398,7 @@
         (zero_heads, zero_heads),
         (query_blocks, mixed_grad, segment_blocks, block_starts, log_totals),
     )
-    query_grad = tick(query_grad, (1, 1), (2, 1))
+    query_grad = tick(query_grad, 2, 1)
     query_raw_grad = rotate(
         query_grad.reshape(row_count, HEADS, HD) * query_scale, cosine_table, -sine_table
     )
@@ -415,29 +415,45 @@
     normed_grad = jnp.dot(qkv_low, w_qkv, preferred_element_type=jnp.float32)
     input_part, gain_one = pull_first(normed_grad)
     input_grad = sum_grad + input_part
-    reduced[0, 0] = plane_sum(0, early_rows)
-    steps[0, 0] = [reduced[0, 0]]
+    state = (params, first_moment, second_moment)
     if tree:
-        for key in sorted(reduced, key=lambda k: k[1], reverse=True):
+        steps[-1] = [
+            lax.psum_scatter(plane_terms(0, late_rows), "wide", scatter_dimension=0, tiled=True)
+        ]
+        for key in (3, 2, 1, 0, -1):
             while len(steps[key]) < 3:
                 advance(key)
-        late_piece = choose_owner([steps[owner, 1][-1] for owner in range(shard_count)])
-        early_piece = choose_owner([steps[owner, 0][-1] for owner in range(shard_count)])
+        late_part = late_rows // wide_count
+        early_part = owner_rows // wide_count - late_part
+        whole_pieces = [steps[owner][-1] for owner in range(1, shard_count)]
+        early_piece = choose_owner([steps[0][-1]] + [p[:early_part] for p in whole_pieces])
+        late_piece = choose_owner([steps[-1][-1]] + [p[early_part:] for p in whole_pieces])
+        first_owner = lax.axis_index("shard") == 0
+        early_place = jnp.where(
+            first_owner,
+            jnp.array([late_rows, early_part], jnp.int32),
+            jnp.array([0, early_part + late_part], jnp.int32),
+        )
+        late_place = jnp.where(
+            first_owner,
+            jnp.array([0, late_part], jnp.int32),
+            jnp.array([early_part, early_part + late_part], jnp.int32),
+        )
+        early_low = lax.all_gather(early_piece, "wide", axis=0, tiled=True)
+        late_low = lax.all_gather(late_piece, "wide", axis=0, tiled=True)
+        carried = adam_rows(early_place, early_part, early_low, state, ())
+        row_grad, new_params, new_first, new_second = adam_rows(
+            late_place, late_part, late_low, state, carried
+        )
     else:
-        late_piece, early_piece = [
-            lax.psum_scatter(
-                jnp.concatenate([reduced[owner, part] for owner in range(shard_count)], axis=0),
-                "shard",
-                scatter_dimension=0,
-                tiled=True,
-            )
-            for part in (1, 0)
-        ]
-    late_low = lax.all_gather(late_piece, "wide", axis=0, tiled=True)
-    early_low = lax.all_gather(early_piece, "wide", axis=0, tiled=True)
-    state = (params, first_moment, second_moment)
-    carried = adam_rows(early_rows, late_low, state, ())
-    row_grad, new_params, new_first, new_second = adam_rows(0, early_low, state, carried)
+        own = lax.psum_scatter(
+            plane_terms(0, total_rows), ("shard", "wide"), scatter_dimension=0, tiled=True
+        )
+        own_low = lax.all_gather(own, "wide", axis=0, tiled=True)
+        block = max(size for size in range(8, 329, 8) if owner_rows % size == 0)
+        row_grad, new_params, new_first, new_second = adam_rows(
+            jnp.array([0, block], jnp.int32), block, own_low, state, ()
+        )
     gain_terms = jnp.stack([gain_one, gain_two, gain_three, gain_four])
     gain_total = butterfly_sum(butterfly_sum(gain_terms, "wide"), "shard")
     gain_grad = lax.dynamic_slice_in_dim(

time: 1170 us -> 1110 us (0.949)
  waiting for transfers between devices: 446 us -> 395 us
  starting transfers between devices: 74.3 us -> 40.6 us
    reduce_scatter x4 -> x1, waiting for transfers between devices: 115 us -> 0.02 us  [per_device(): lax.psum_scatter(plane_terms(0, late_rows), 'wide', scatter_dimension=0,...]
    unnamed x11 -> x9, waiting for transfers between devices: 0.18 us -> 57.6 us
    concatenate x2 -> x3, other arithmetic: 9.14 us -> 51 us  [plane_terms(): return parts[0] if len(parts) == 1 else jnp.concatenate(parts, axis=0)]
    ppermute x16 -> x10, starting transfers between devices: 45.2 us -> 18.8 us  [advance(): steps[key].append(add_low(held, lax.ppermute(held, 'shard', pairs)))]
    ppermute x16 -> x10, waiting for transfers between devices: 58.3 us -> 84.4 us  [advance(): steps[key].append(add_low(held, lax.ppermute(held, 'shard', pairs)))]
    optimization_barrier x4 -> x3, waiting for transfers between devices: 26.3 us -> 0.38 us  [tied(): return lax.optimization_barrier((anchor, values))]
    concatenate x1 -> x0, other arithmetic: 20.6 us -> none  [per_device(): jnp.concatenate([gate_grad, up_grad], axis=1).astype(jnp.bfloat16)]
    dot_general x1 -> x2, matrix products: 43.9 us -> 48.4 us  [the longest x1 24.9 us: per_device(): jnp.dot(gate_low, w_gate_up[:FF], preferred_element_type=jnp.float32)]
  transfers between devices with their start and end apart: 44 -> 35, of which waited for: 21 -> 19; matrix products, arithmetic and copies ran while one was open for 35% -> 37% of each run, Pallas kernels for 4% -> 5%
where the time goes in v2:
time: 1110 us; the launch traced here: 1100 us
  waiting for transfers between devices  395 us (36%)
  matrix products  339 us (31%)
  other arithmetic  166 us (15%)
  Pallas kernels  74 us (7%)
  local copies, waits for them, and re-layouts  62.7 us (6%)
  starting transfers between devices  40.6 us (4%)
  between operations  16.7 us (2%)
    all_gather x1, waiting for transfers between devices, per_device(): lax.all_gather(own_slice(0, owner_rows), ('shard', 'wide'), axis=0, tiled...  122 us
    dot_general x8, matrix products, contract_rows(): lax.dot_general(left_side, right_side, (((0,), (0,)), ((), ())), preferre...  111 us
    dot_general x4, matrix products, times_transposed(): lax.dot_general(left_side, right_side, (((1,), (1,)), ((), ())), preferre...  106 us
    ppermute x10, waiting for transfers between devices, advance(): steps[key].append(add_low(held, lax.ppermute(held, 'shard', pairs)))  84.4 us
    pallas_call x2, Pallas kernels, adam_rows(): pl.pallas_call(body, grid_spec=pltpu.PrefetchScalarGridSpec(num_scalar_pr...  74 us
    ppermute x7, waiting for transfers between devices, spread_first(): other = lax.ppermute(block, 'wide', [(i, i ^ bit) for i in range(8)])  68.2 us
    unnamed x9, waiting for transfers between devices  57.6 us
    concatenate x3, other arithmetic, plane_terms(): return parts[0] if len(parts) == 1 else jnp.concatenate(parts, axis=0)  51 us
  transfers between devices with their start and end apart: 35, of which 19 were waited for; matrix products, arithmetic and copies ran while one was open for 37% of the time, Pallas kernels for 5%

profile of v2, /device:TPU:0, one launch (start us, length us, event | category | flops | bytes accessed | tf_op | source)
XLA Modules:
  0.0 1095.2 jit_solution(329016817337835394)
XLA Ops:
  12.2 6.9 collective-permute-start.3
  19.1 24.9 %collective-permute-done.3 = bf16[320,1152]{1,0:T(8,128)(2,1)} collective-permute-done((bf16[320,1152]{1,0:T(8,128)(2,1)S(1)}, bf16[320,1152]{1,0:T(8,128)(2,1)}, u32[]{:S(2)}, u32[]{:S(2)}) %collective-permute-start.3) | collective-permute-done | bytes 737312 | tf_op jit(solution)/shard_map/ppermute | solution.py:132
  54.7 23.6 %collective-permute-done.4 = bf16[320,1152]{1,0:T(8,128)(2,1)} collective-permute-done((bf16[320,1152]{1,0:T(8,128)(2,1)S(1)}, bf16[320,1152]{1,0:T(8,128)(2,1)}, u32[]{:S(2)}, u32[]{:S(2)}) %collective-permute-start.4) | collective-permute-done | bytes 737312 | tf_op jit(solution)/shard_map/ppermute | solution.py:134
  83.4 11.5 %collective-permute-done.5 = bf16[320,1152]{1,0:T(8,128)(2,1)} collective-permute-done((bf16[320,1152]{1,0:T(8,128)(2,1)S(1)}, bf16[320,1152]{1,0:T(8,128)(2,1)}, u32[]{:S(2)}, u32[]{:S(2)}) %collective-permute-start.5) | collective-permute-done | bytes 737312 | tf_op jit(solution)/shard_map/ppermute | solution.py:142
  102.6 30.2 %collective-permute-done.6 = bf16[320,1152]{1,0:T(8,128)(2,1)} collective-permute-done((bf16[320,1152]{1,0:T(8,128)(2,1)}, bf16[320,1152]{1,0:T(8,128)(2,1)}, u32[]{:S(2)}, u32[]{:S(2)}) %collective-permute-start.6) | collective-permute-done | bytes 737312 | tf_op jit(solution)/shard_map/ppermute | solution.py:142
  137.0 25.2 %collective-permute-done.9 = bf16[320,1152]{1,0:T(8,128)(2,1)} collective-permute-done((bf16[320,1152]{1,0:T(8,128)(2,1)}, bf16[320,1152]{1,0:T(8,128)(2,1)}, u32[]{:S(2)}, u32[]{:S(2)}) %collective-permute-start.9) | collective-permute-done | bytes 737312 | tf_op jit(solution)/shard_map/ppermute | solution.py:142
  195.4 27.0 %while.31 = (s32[]{:T(128)}, bf16[2,512,1,4,256]{4,1,3,2,0:T(8,128)(2,1)}, f32[2,1,4,512,1]{3,2,4,1,0:T(4,128)S(1)}, s32[2,512]{1,0:T(2,128)S(1)}, s32[1024]{0:T...) while((s32[]{:T(128)}, ...), condition=%wide.region_6.7_spmd.clone, body=%wide.region_3.6_spmd.sunk.clone | while | flops 2186279424 | bytes 50411736 | solution.py:280
  237.3 122.2 %all-gather.4.cloned.1.call-done = bf16[23296,1152]{1,0:T(8,128)(2,1)} async-done(((bf16[728,1152]{1,0:T(8,128)(2,1)}), bf16[23296,1152]{1,0:T(8,128)(2,1)}) %all-gather.4.cloned.1.call-update) | async-done | bytes 53674000 | tf_op jit(solution)/shard_map/all_gather | solution.py:227
  359.5 44.3 %fusion.66 = f32[1024,13824]{1,0:T(8,128)} fusion(bf16[1024,1152]{1,0:T(8,128)(2,1)S(1)} %multiply_convert_fusion.2, bf16[23296,1152]{1,0:T(8,128)(2,1)} %all-gather.4.cloned.1.call-done), kind=kOutput, calls=%fused_computation.78 | convolution fusion | flops 32614907904 | bytes 90832896 | tf_op jit(solution)/shard_map/dot_general | solution.py:76
  403.8 24.9 %multiply_convert_fusion.1 = bf16[1024,6912]{1,0:T(8,128)(2,1)} fusion(f32[1024,13824]{1,0:T(8,128)} %fusion.66), kind=kLoop, calls=%fused_computation.88 | loop fusion | flops 70778880 | bytes 70778880 | tf_op jit(solution)/shard_map/convert_element_type | solution.py:289
  428.7 23.3 %multiply_reduce_fusion.4 = (f32[1024]{0:T(1024)S(1)}, f32[1024,1152]{1,0:T(8,128)S(1)}) fusion(bf16[1024,6912]{1,0:T(8,128)(2,1)} %multiply_convert_fusion.1, bf16[23296,1152]{1,0:T(8,128)(2,1)} %all-gather.4.cloned.1.call-done), kind=kOutput, calls=%fused_computation.143 | convolution fusion | flops 16309812224 | bytes 34803712 | tf_op jit(solution)/shard_map/dot_general | solution.py:290
  458.3 41.2 %convolution_convert_fusion = bf16[5824,1152]{1,0:T(8,128)(2,1)} fusion(bf16[1024,1152]{1,0:T(8,128)(2,1)S(1)} %get-tuple-element.232, bf16[1024,6912]{1,0:T(8,128)(2,1)} %multiply_convert_fusion.1), kind=kOutput, calls=%fused_computation.90 | convolution fusion | flops 13747249152 | bytes 27836416 | tf_op jit(solution)/shard_map/dot_general | solution.py:70
  505.1 50.7 %multiply_convert_fusion = (bf16[1024,6912]{1,0:T(8,128)(2,1)}, bf16[1024,6912]{1,0:T(8,128)(2,1)}) fusion(f32[1024,13824]{1,0:T(8,128)} %fusion.66, bf16[1024,1152]{1,0:T(8,128)(2,1)} %copy-done.25, bf16[23296,1152]{1,0:T(8,128)(2,1)} %all-gather.4.cloned.1.call-done), kind=kOutput, calls=%fused_computation.87 | convolution fusion | flops 16477323264 | bytes 103219200 | tf_op jit(solution)/shard_map/dot_general | solution.py:76
  555.8 17.0 %convolution_convert_fusion.1 = bf16[4736,1152]{1,0:T(8,128)(2,1)S(1)} fusion(bf16[1024,1152]{1,0:T(8,128)(2,1)} %copy-done.26, bf16[1024,6912]{1,0:T(8,128)(2,1)} %get-tuple-element.236), kind=kOutput, calls=%fused_computation.91 | convolution fusion | flops 11179081728 | bytes 22970368 | tf_op jit(solution)/shard_map/dot_general | solution.py:70
  572.8 18.2 %pad_maximum_fusion = bf16[5824,1152]{1,0:T(8,128)(2,1)} fusion(bf16[1088,1152]{1,0:T(8,128)(2,1)S(1)} %convolution_convert_fusion.6, bf16[4736,1152]{1,0:T(8,128)(2,1)S(1)} %convolution_convert_fusion.1), kind=kLoop, calls=%fused_computation.102 | loop fusion | flops 26836992 | bytes 26836992 | tf_op jit(solution)/shard_map/concatenate | solution.py:312
  592.7 8.4 convolution_convert_fusion.4
  601.1 14.5 %convolution_convert_fusion.3 = bf16[3648,1152]{1,0:T(8,128)(2,1)S(1)} fusion(bf16[1024,1152]{1,0:T(8,128)(2,1)S(1)} %copy-done.27, bf16[1024,6912]{1,0:T(8,128)(2,1)} %get-tuple-element.235), kind=kOutput, calls=%fused_computation.97 | convolution fusion | flops 8610914304 | bytes 18366464 | tf_op jit(solution)/shard_map/dot_general | solution.py:70
  615.6 18.7 %pad_maximum_fusion.1 = bf16[5824,1152]{1,0:T(8,128)(2,1)} fusion(bf16[2176,1152]{1,0:T(8,128)(2,1)S(1)} %convolution_convert_fusion.4, bf16[3648,1152]{1,0:T(8,128)(2,1)S(1)} %convolution_convert_fusion.3), kind=kLoop, calls=%fused_computation.103 | loop fusion | flops 26836992 | bytes 26836992 | tf_op jit(solution)/shard_map/concatenate | solution.py:312
  634.3 13.3 %convolution_convert_fusion.2 = bf16[3264,1152]{1,0:T(8,128)(2,1)} fusion(bf16[1024,1152]{1,0:T(8,128)(2,1)S(1)} %copy-done.27, bf16[1024,6912]{1,0:T(8,128)(2,1)} %get-tuple-element.235), kind=kOutput, calls=%fused_computation.96 | convolution fusion | flops 7704502272 | bytes 16695296 | tf_op jit(solution)/shard_map/dot_general | solution.py:70
  649.1 23.4 %fusion.75 = f32[1024,1152]{1,0:T(8,128)S(1)} fusion(bf16[1024,6912]{1,0:T(8,128)(2,1)} %get-tuple-element.236, bf16[23296,1152]{1,0:T(8,128)(2,1)} %all-gather.4.cloned.1.call-done), kind=kOutput, calls=%fused_computation.92 | convolution fusion | flops 16307453952 | bytes 34799616 | tf_op jit(solution)/shard_map/dot_general | solution.py:351
  672.5 24.9 %fusion.101 = f32[1024,1152]{1,0:T(8,128)S(1)} fusion(f32[1024,1152]{1,0:T(8,128)S(1)} %fusion.75, bf16[1024,6912]{1,0:T(8,128)(2,1)} %get-tuple-element.235, bf16[23296,1152]{1,0:T(8,128)(2,1)} %all-gather.4.cloned.1.call-done), kind=kOutput, calls=%fused_computation.147 | convolution fusion | flops 16308633600 | bytes 39518208 | tf_op jit(solution)/shard_map/dot_general | solution.py:349
  713.1 14.1 %pad_maximum_fusion.2 = bf16[4288,1152]{1,0:T(8,128)(2,1)} fusion(bf16[3264,1152]{1,0:T(8,128)(2,1)S(1)} %bitcast.321, bf16[1024,1152]{1,0:T(8,128)(2,1)S(1)} %convolution_convert_fusion.7), kind=kLoop, calls=%fused_computation.106 | loop fusion | flops 19759104 | bytes 19759104 | tf_op jit(solution)/shard_map/concatenate | solution.py:312
  741.0 48.9 %while.32 = (s32[]{:T(128)}, f32[1024,1,256]{0,2,1:T(8,128)S(1)}, f32[1024,1,256]{0,2,1:T(8,128)}, f32[2,512,1,4,256]{4,1,3,2,0:T(8,128)}, bf16[2,512,1,4,256]{4...) while((s32[]{:T(128)}, f32[1024,1,256]{0,2,1:T(8,128)S(1)}, ...), condition=%wide.region_17.18_spmd.clone.clone, body=%wide.region_15.17_spmd.clone.sunk.clone | while | flops 5423233536 | bytes 125376864 | solution.py:396
  811.8 8.2 convolution_convert_fusion.5
  823.8 57.5 %reduce-scatter.22.cloned.1.call-done = bf16[536,1152]{1,0:T(8,128)(2,1)} async-done(((bf16[4288,1152]{1,0:T(8,128)(2,1)}), bf16[536,1152]{1,0:T(8,128)(2,1)}) %reduce-scatter.22.cloned.1.call-update) | async-done | bytes 1234960
  888.0 24.4 %collective-permute-done.20 = bf16[536,1152]{1,0:T(8,128)(2,1)S(1)} collective-permute-done((bf16[536,1152]{1,0:T(8,128)(2,1)}, bf16[536,1152]{1,0:T(8,128)(2,1)S(1)}, u32[]{:S(2)}, u32[]{:S(2)}) %collective-permute-start.20) | collective-permute-done | bytes 1234976 | tf_op jit(solution)/shard_map/ppermute | solution.py:330
  916.3 37.4 %collective-permute-done.21 = bf16[536,1152]{1,0:T(8,128)(2,1)S(1)} collective-permute-done((bf16[536,1152]{1,0:T(8,128)(2,1)S(1)}, bf16[536,1152]{1,0:T(8,128)(2,1)S(1)}, u32[]{:S(2)}, u32[]{:S(2)}) %collective-permute-start.21) | collective-permute-done | bytes 1234976 | tf_op jit(solution)/shard_map/ppermute | solution.py:330
  957.0 11.4 %collective-permute-done.18 = bf16[192,1152]{1,0:T(8,128)(2,1)S(1)} collective-permute-done((bf16[192,1152]{1,0:T(8,128)(2,1)}, bf16[192,1152]{1,0:T(8,128)(2,1)S(1)}, u32[]{:S(2)}, u32[]{:S(2)}) %collective-permute-start.18) | collective-permute-done | bytes 442400 | tf_op jit(solution)/shard_map/ppermute | solution.py:330
  971.1 11.1 %collective-permute-done.19 = bf16[192,1152]{1,0:T(8,128)(2,1)S(1)} collective-permute-done((bf16[192,1152]{1,0:T(8,128)(2,1)S(1)}, bf16[192,1152]{1,0:T(8,128)(2,1)S(1)}, u32[]{:S(2)}, u32[]{:S(2)}) %collective-permute-start.19) | collective-permute-done | bytes 442400 | tf_op jit(solution)/shard_map/ppermute | solution.py:330
  985.1 8.2 fusion.92
  1013.9 52.0 %adam_rows.2 = (f32[5824,1152]{1,0:T(8,128)}, f32[5824,1152]{1,0:T(8,128)}, f32[5824,1152]{1,0:T(8,128)}, f32[5824,1152]{1,0:T(8,128)}) custom-call(s32[2]{0:T(128)} %broadcast_select_fusion.12.place_ref, bf16[4288,1152]{1,0:T(8,128)(2,1)} %all-gather.8.cloned.1.call-done.grad_ref, f32[5824,1152]{1,0:T(8,128)} %param_ref.3, f32[5824,1152]{1,0:T(8,128)} %first_ref.3, ...), custom_call_target="tpu_custom_call" | custom-call | flops 98795520 | bytes 148193280 | tf_op jit(solution)/shard_map/adam_rows/pallas_call | solution.py:191
  1065.9 22.0 %adam_rows.3 = (f32[5824,1152]{1,0:T(8,128)}, f32[5824,1152]{1,0:T(8,128)}, f32[5824,1152]{1,0:T(8,128)}, f32[5824,1152]{1,0:T(8,128)}) custom-call(s32[2]{0:T(128)} %broadcast_select_fusion.13.place_ref, bf16[1536,1152]{1,0:T(8,128)(2,1)} %all-gather.6.cloned.1.call-done.grad_ref, ...), custom_call_target="tpu_custom_call", output_to_operand_aliasing={{0}: (5, {}), {1}: (6, {}), {2}: (7, {}), {3}: (8, {})} | custom-call | flops 35389440 | bytes 53084160 | tf_op jit(solution)/shard_map/adam_rows/pallas_call | solution.py:191
  (428 shorter events, 264.0 us)
Async XLA Ops:
  7.2 352.3 %all-gather.4.cloned.1.call-start = ((), (), s32[]{:S(2)}) async-start(), calls=%async_computation.5 | async-start | bytes 55351296 | tf_op jit(solution)/shard_map/all_gather | solution.py:227
  10.6 637.1 %reduce-scatter.16.cloned.1.call-start = ((), (), s32[]{:S(2)}) async-start(), calls=%async_computation.9 | async-start | bytes 15095808
  12.2 31.8 %collective-permute-start.3 = (bf16[320,1152]{1,0:T(8,128)(2,1)S(1)}, bf16[320,1152]{1,0:T(8,128)(2,1)}, u32[]{:S(2)}, u32[]{:S(2)}) collective-permute-start(bf16[320,1152]{1,0:T(8,128)(2,1)S(1)} %dynamic-slice_convert_fusion.1), channel_id=1, source_target_pairs={{0,2},{4,6},{8,10},{12,14},{16,18},{20,22},{24,26},{28,30}} | collective-permute-start | bytes 2211848 | tf_op jit(solution)/shard_map/ppermute | solution.py:132
  45.6 32.7 %collective-permute-start.4 = (bf16[320,1152]{1,0:T(8,128)(2,1)S(1)}, bf16[320,1152]{1,0:T(8,128)(2,1)}, u32[]{:S(2)}, u32[]{:S(2)}) collective-permute-start(bf16[320,1152]{1,0:T(8,128)(2,1)S(1)} %broadcast_select_fusion), channel_id=1, source_target_pairs={{0,1},{2,3},{4,5},{6,7},{8,9},{10,11},{12,13},{14,15},{16,17},{18,... | collective-permute-start | bytes 2211848 | tf_op jit(solution)/shard_map/ppermute | solution.py:134
  47.7 88.3 %collective-permute-start.2 = (bf16[4,288]{1,0:T(4,128)(2,1)S(1)}, bf16[4,288]{1,0:T(4,128)(2,1)S(1)}, u32[]{:S(2)}, u32[]{:S(2)}) collective-permute-start(bf16[4,288]{1,0:T(4,128)(2,1)S(1)} %convert_element_type.212), channel_id=1, source_target_pairs={{0,3},{1,0},{2,1},{3,2},{4,7},{5,4},{6,5},{7,6},{8,11},{9,8},{10,9... | collective-permute-start | bytes 6920 | tf_op jit(solution)/shard_map/ppermute | solution.py:124
  47.7 87.9 %collective-permute-start.1 = (bf16[4,288]{1,0:T(4,128)(2,1)S(1)}, bf16[4,288]{1,0:T(4,128)(2,1)S(1)}, u32[]{:S(2)}, u32[]{:S(2)}) collective-permute-start(bf16[4,288]{1,0:T(4,128)(2,1)S(1)} %convert_element_type.212), channel_id=1, source_target_pairs={{0,2},{1,3},{2,0},{3,1},{4,6},{5,7},{6,4},{7,5},{8,10},{9,11},{10,... | collective-permute-start | bytes 6920 | tf_op jit(solution)/shard_map/ppermute | solution.py:124
  51.5 83.8 %collective-permute-start = (bf16[4,288]{1,0:T(4,128)(2,1)S(1)}, bf16[4,288]{1,0:T(4,128)(2,1)S(1)}, u32[]{:S(2)}, u32[]{:S(2)}) collective-permute-start(bf16[4,288]{1,0:T(4,128)(2,1)S(1)} %convert_element_type.212), channel_id=1, source_target_pairs={{0,1},{1,2},{2,3},{3,0},{4,5},{5,6},{6,7},{7,4},{8,9},{9,10},{10,1... | collective-permute-start | bytes 6920 | tf_op jit(solution)/shard_map/ppermute | solution.py:124
  79.5 15.5 %collective-permute-start.5 = (bf16[320,1152]{1,0:T(8,128)(2,1)S(1)}, bf16[320,1152]{1,0:T(8,128)(2,1)}, u32[]{:S(2)}, u32[]{:S(2)}) collective-permute-start(bf16[320,1152]{1,0:T(8,128)(2,1)S(1)} %broadcast_select_fusion.1), channel_id=1, source_target_pairs={{0,16},{4,20},{8,24},{12,28},{16,0},{20,4},{24,8},{28,12},{1,17},{... | collective-permute-start | bytes 2211848 | tf_op jit(solution)/shard_map/ppermute | solution.py:142
  97.3 35.5 %collective-permute-start.6 = (bf16[320,1152]{1,0:T(8,128)(2,1)}, bf16[320,1152]{1,0:T(8,128)(2,1)}, u32[]{:S(2)}, u32[]{:S(2)}) collective-permute-start(bf16[320,1152]{1,0:T(8,128)(2,1)} %get-tuple-element.455), channel_id=1, source_target_pairs={{0,8},{4,12},{8,0},{12,4},{16,24},{20,28},{24,16},{28,20},{1,9},{5... | collective-permute-start | bytes 2211848 | tf_op jit(solution)/shard_map/ppermute | solution.py:142
  101.8 60.4 %collective-permute-start.9 = (bf16[320,1152]{1,0:T(8,128)(2,1)}, bf16[320,1152]{1,0:T(8,128)(2,1)}, u32[]{:S(2)}, u32[]{:S(2)}) collective-permute-start(bf16[320,1152]{1,0:T(8,128)(2,1)} %get-tuple-element.454), channel_id=1, source_target_pairs={{0,8},{4,12},{8,0},{12,4},{16,24},{20,28},{24,16},{28,20},{1,9},{5... | collective-permute-start | bytes 2211848 | tf_op jit(solution)/shard_map/ppermute | solution.py:142
  135.1 29.9 %collective-permute-start.7 = (bf16[320,1152]{1,0:T(8,128)(2,1)}, bf16[320,1152]{1,0:T(8,128)(2,1)}, u32[]{:S(2)}, u32[]{:S(2)}) collective-permute-start(bf16[320,1152]{1,0:T(8,128)(2,1)} %get-tuple-element.457), channel_id=1, source_target_pairs={{0,4},{4,0},{8,12},{12,8},{16,20},{20,16},{24,28},{28,24},{1,5},{5... | collective-permute-start | bytes 2211848 | tf_op jit(solution)/shard_map/ppermute | solution.py:142
  164.5 62.6 %collective-permute-start.11 = (bf16[320,1152]{1,0:T(8,128)(2,1)}, bf16[320,1152]{1,0:T(8,128)(2,1)}, u32[]{:S(2)}, u32[]{:S(2)}) collective-permute-start(bf16[320,1152]{1,0:T(8,128)(2,1)} %get-tuple-element.452), channel_id=1, source_target_pairs={{0,4},{4,0},{8,12},{12,8},{16,20},{20,16},{24,28},{28,24},{1,5},{5... | collective-permute-start | bytes 2211848 | tf_op jit(solution)/shard_map/ppermute | solution.py:142
  164.5 5.0 collective-permute-start.10
  499.5 239.0 %reduce-scatter.18.cloned.1.call-start = ((), (), s32[]{:S(2)}) async-start(), calls=%async_computation.10 | async-start | bytes 15095808
  591.1 207.2 %reduce-scatter.20.cloned.1.call-start = ((), (), s32[]{:S(2)}) async-start(), calls=%async_computation.11 | async-start | bytes 15095808
  634.3 246.9 %reduce-scatter.22.cloned.1.call-start = ((), (), s32[]{:S(2)}) async-start(), calls=%async_computation.12 | async-start | bytes 11114496
  647.7 49.8 %collective-permute-start.12 = (bf16[728,1152]{1,0:T(8,128)(2,1)}, bf16[728,1152]{1,0:T(8,128)(2,1)S(1)}, u32[]{:S(2)}, u32[]{:S(2)}) collective-permute-start(bf16[728,1152]{1,0:T(8,128)(2,1)} %reduce-scatter.16.cloned.1.call-done), channel_id=1, source_target_pairs={{0,1},{2,3},{4,5},{6,7},{8,9},{10,11},{12,13},{14,15},{16,17},{18,... | collective-permute-start | bytes 5031944 | tf_op jit(solution)/shard_map/ppermute | solution.py:330
  727.2 228.5 %reduce-scatter.14.cloned.1.call-start = ((), (), s32[]{:S(2)}) async-start(), calls=%async_computation.6 | async-start | bytes 3981312 | tf_op jit(solution)/shard_map/reduce_scatter | solution.py:421
  738.5 56.3 %collective-permute-start.13 = (bf16[728,1152]{1,0:T(8,128)(2,1)}, bf16[728,1152]{1,0:T(8,128)(2,1)}, u32[]{:S(2)}, u32[]{:S(2)}) collective-permute-start(bf16[728,1152]{1,0:T(8,128)(2,1)} %reduce-scatter.18.cloned.1.call-done), channel_id=1, source_target_pairs={{3,2},{0,1},{7,6},{4,5},{11,10},{8,9},{15,14},{12,13},{19,18},{16,... | collective-permute-start | bytes 5031944 | tf_op jit(solution)/shard_map/ppermute | solution.py:330
  807.2 75.6 %collective-permute-start.16 = (bf16[728,1152]{1,0:T(8,128)(2,1)}, bf16[728,1152]{1,0:T(8,128)(2,1)}, u32[]{:S(2)}, u32[]{:S(2)}) collective-permute-start(bf16[728,1152]{1,0:T(8,128)(2,1)} %reduce-scatter.20.cloned.1.call-done), channel_id=1, source_target_pairs={{0,1},{3,2},{4,5},{7,6},{8,9},{11,10},{12,13},{15,14},{16,17},{19,... | collective-permute-start | bytes 5031944 | tf_op jit(solution)/shard_map/ppermute | solution.py:330
  820.0 194.0 %all-gather.8.cloned.1.call-start = ((), (), s32[]{:S(2)}) async-start(), calls=%async_computation.8 | async-start | bytes 11114496 | tf_op jit(solution)/shard_map/all_gather | solution.py:442
  820.0 66.1 %collective-permute-start.14 = (bf16[728,1152]{1,0:T(8,128)(2,1)}, bf16[728,1152]{1,0:T(8,128)(2,1)}, u32[]{:S(2)}, u32[]{:S(2)}) collective-permute-start(bf16[728,1152]{1,0:T(8,128)(2,1)} %add_convert_fusion.6), channel_id=1, source_target_pairs={{1,3},{5,7},{9,11},{13,15},{17,19},{21,23},{25,27},{29,31}} | collective-permute-start | bytes 5031944 | tf_op jit(solution)/shard_map/ppermute | solution.py:330
  821.9 92.0 %collective-permute-start.15 = (bf16[728,1152]{1,0:T(8,128)(2,1)}, bf16[728,1152]{1,0:T(8,128)(2,1)}, u32[]{:S(2)}, u32[]{:S(2)}) collective-permute-start(bf16[728,1152]{1,0:T(8,128)(2,1)} %add_convert_fusion.5), channel_id=1, source_target_pairs={{1,2},{5,6},{9,10},{13,14},{17,18},{21,22},{25,26},{29,30}} | collective-permute-start | bytes 5031944 | tf_op jit(solution)/shard_map/ppermute | solution.py:330
  881.2 31.1 %collective-permute-start.20 = (bf16[536,1152]{1,0:T(8,128)(2,1)}, bf16[536,1152]{1,0:T(8,128)(2,1)S(1)}, u32[]{:S(2)}, u32[]{:S(2)}) collective-permute-start(bf16[536,1152]{1,0:T(8,128)(2,1)} %reduce-scatter.22.cloned.1.call-done), channel_id=1, source_target_pairs={{3,2},{1,0},{7,6},{5,4},{11,10},{9,8},{15,14},{13,12},{19,18},{17,... | collective-permute-start | bytes 3704840 | tf_op jit(solution)/shard_map/ppermute | solution.py:330
  885.2 30.7 %collective-permute-start.17 = (bf16[728,1152]{1,0:T(8,128)(2,1)S(1)}, bf16[728,1152]{1,0:T(8,128)(2,1)S(1)}, u32[]{:S(2)}, u32[]{:S(2)}) collective-permute-start(bf16[728,1152]{1,0:T(8,128)(2,1)S(1)} %add_convert_fusion.2), channel_id=1, source_target_pairs={{2,1},{6,5},{10,9},{14,13},{18,17},{22,21},{26,25},{30,29}} | collective-permute-start | bytes 5031944 | tf_op jit(solution)/shard_map/ppermute | solution.py:330
  912.6 41.1 %collective-permute-start.21 = (bf16[536,1152]{1,0:T(8,128)(2,1)S(1)}, bf16[536,1152]{1,0:T(8,128)(2,1)S(1)}, u32[]{:S(2)}, u32[]{:S(2)}) collective-permute-start(bf16[536,1152]{1,0:T(8,128)(2,1)S(1)} %add_convert_fusion.8), channel_id=1, source_target_pairs={{2,0},{6,4},{10,8},{14,12},{18,16},{22,20},{26,24},{30,28}} | collective-permute-start | bytes 3704840 | tf_op jit(solution)/shard_map/ppermute | solution.py:330
  955.6 110.3 %all-gather.6.cloned.1.call-start = ((), (), s32[]{:S(2)}) async-start(), calls=%async_computation.7 | async-start | bytes 3981312 | tf_op jit(solution)/shard_map/all_gather | solution.py:443
  955.7 12.7 %collective-permute-start.18 = (bf16[192,1152]{1,0:T(8,128)(2,1)}, bf16[192,1152]{1,0:T(8,128)(2,1)S(1)}, u32[]{:S(2)}, u32[]{:S(2)}) collective-permute-start(bf16[192,1152]{1,0:T(8,128)(2,1)} %reduce-scatter.14.cloned.1.call-done), channel_id=1, source_target_pairs={{3,2},{1,0},{7,6},{5,4},{11,10},{9,8},{15,14},{13,12},{19,18},{17,... | collective-permute-start | bytes 1327112 | tf_op jit(solution)/shard_map/ppermute | solution.py:330
  969.5 12.7 %collective-permute-start.19 = (bf16[192,1152]{1,0:T(8,128)(2,1)S(1)}, bf16[192,1152]{1,0:T(8,128)(2,1)S(1)}, u32[]{:S(2)}, u32[]{:S(2)}) collective-permute-start(bf16[192,1152]{1,0:T(8,128)(2,1)S(1)} %add_convert_fusion.11), channel_id=1, source_target_pairs={{2,0},{6,4},{10,8},{14,12},{18,16},{22,20},{26,24},{30,28}} | collective-permute-start | bytes 1327112 | tf_op jit(solution)/shard_map/ppermute | solution.py:330
  994.6 4.3 collective-permute-start.23
  999.0 4.3 collective-permute-start.24
  1007.1 4.7 collective-permute-start.26
  (110 other events, 2422.1 us)
Sparse Core Ops, SparseCore 0:
  11.5 347.9 all-gather.3
  499.7 95.4 reduce-scatter.15
  599.3 97.4 reduce-scatter.17
  700.7 97.4 reduce-scatter.19
  802.3 78.8 reduce-scatter.21
  885.1 47.9 reduce-scatter.13
  955.7 58.1 all-gather.7
  1015.8 33.6 all-gather.5

commit v3 on v2

--- a/solution.py
+++ b/solution.py
@@ -3,6 +3,7 @@
 from jax import lax
 from jax.experimental import pallas as pl
 from jax.experimental.pallas import tpu as pltpu
+from jax.sharding import Mesh
 from jax.sharding import PartitionSpec as P
 
 D = 1152
@@ -103,8 +104,14 @@
     return count & (count - 1) == 0
 
 
-def butterfly_sum(values, axis_name):
-    count = lax.axis_size(axis_name)
+WIDE = ("chip", "core")
+
+
+def wide_size():
+    return lax.axis_size("chip") * lax.axis_size("core")
+
+
+def butterfly_sum(values, axis_name, count):
     if not power_of_two(count):
         return lax.psum(values, axis_name)
     step = 1
@@ -133,13 +140,13 @@
     rows = jnp.where(
         lax.rem(place, 2) == 1, lax.ppermute(rows, "shard", [(0, 1), (2, 3)]), rows
     )
-    index = lax.axis_index("wide")
+    index = lax.axis_index(WIDE)
     blocks = {0: rows}
     for bit in (4, 2, 1):
         upper = (index & bit) != 0
         grown = {}
         for key, block in blocks.items():
-            other = lax.ppermute(block, "wide", [(i, i ^ bit) for i in range(8)])
+            other = lax.ppermute(block, WIDE, [(i, i ^ bit) for i in range(8)])
             grown[key] = jnp.where(upper, other, block)
             grown[key | bit] = jnp.where(upper, block, other)
         blocks = grown
@@ -170,23 +177,43 @@
     return own
 
 
+def to_partner(values):
+    return lax.ppermute(values, "core", [(0, 1), (1, 0)])
+
+
+def paired(values):
+    return jnp.concatenate([values, to_partner(values)], axis=0)
+
+
+def split_rows(rows):
+    return rows.reshape(rows.shape[0] // 16, 2, 8, rows.shape[1])
+
+
+def one_parity(rows, parity):
+    grouped = split_rows(rows)
+    return lax.dynamic_index_in_dim(grouped, parity, axis=1, keepdims=False).reshape(
+        rows.shape[0] // 2, rows.shape[1]
+    )
+
+
 def adam_rows(place, block, grad_low, state, carried):
-    count = grad_low.shape[0]
+    groups = block // 8
 
     def rows_of(i, place_ref):
-        return (pl.multiple_of(place_ref[0] + i * place_ref[1], 8), 0)
-
-    spec = pl.BlockSpec((pl.Element(block), pl.Element(D)), rows_of)
+        return (place_ref[0] + (i // 2) * place_ref[1], i % 2, 0, 0)
+
+    spec = pl.BlockSpec((pl.Element(groups), pl.Element(1), pl.Element(8), pl.Element(D)), rows_of)
 
     def body(place_ref, grad_ref, param_ref, first_ref, second_ref, *rest):
         out_refs = rest[-4:]
-        grad = grad_ref[...].astype(jnp.float32)
+        grad = grad_ref[...].astype(jnp.float32).reshape(groups, 1, 8, D)
         param_new, first_new, second_new = adam_update(
             param_ref[...], grad, first_ref[...], second_ref[...], weight_decay
         )
         for ref, value in zip(out_refs, (grad, param_new, first_new, second_new)):
             ref[...] = value
 
+    count = grad_low.shape[0]
     shape = jax.ShapeDtypeStruct(state[0].shape, jnp.float32)
     return pl.pallas_call(
         body,
@@ -211,12 +238,14 @@
 def per_device(
     tokens, seg_ids, cotangent, params, gains, first_moment, second_moment, gain_first, gain_second
 ):
-    wide_count = lax.axis_size("wide")
+    wide_count = wide_size()
     shard_count = lax.axis_size("shard")
+    tree = wide_count == 8 and shard_count == 4
     owner_rows = params.shape[0]
     total_rows = owner_rows * shard_count
     early_rows = (HEADS + 2 * KV_HEADS) * HD + HEADS * HD
-    wide_index = lax.axis_index("wide")
+    wide_index = lax.axis_index(WIDE)
+    core_index = lax.axis_index("core")
 
     def own_slice(first, count):
         part = count // wide_count
@@ -224,11 +253,25 @@
             params, first + wide_index * part, part, axis=0
         ).astype(jnp.bfloat16)
 
-    rows_used = lax.all_gather(own_slice(0, owner_rows), ("shard", "wide"), axis=0, tiled=True)
-    if wide_count == 8 and shard_count == 4:
+    if tree:
+        chip_rows = 2 * owner_rows // wide_count
+        chip_slice = lax.dynamic_slice_in_dim(
+            params, lax.axis_index("chip") * chip_rows, chip_rows, axis=0
+        )
+        rows_used = lax.all_gather(
+            one_parity(chip_slice, core_index).astype(jnp.bfloat16),
+            ("shard", "chip"),
+            axis=0,
+            tiled=True,
+        )
         early_used = spread_first(own_slice(0, early_rows))
+        split = 2
     else:
+        rows_used = lax.all_gather(
+            own_slice(0, owner_rows), ("shard",) + WIDE, axis=0, tiled=True
+        )
         early_used = rows_used[:early_rows]
+        split = 1
     gains_used = gather_columns(gains.astype(jnp.bfloat16), "shard")
     gains_float = gains_used.astype(jnp.float32)
     query_width = HEADS * HD
@@ -239,8 +282,14 @@
     gate_end = out_end + 2 * FF
     w_qkv = early_used[:qkv_rows]
     w_out = early_used[qkv_rows:out_end]
-    w_gate_up = rows_used[out_end:gate_end]
-    w_down = rows_used[gate_end:]
+    gate_first, up_first, down_first, hidden_width = (
+        out_end // split,
+        (out_end + FF) // split,
+        gate_end // split,
+        FF // split,
+    )
+    w_gate_up = rows_used[gate_first:down_first]
+    w_down = rows_used[down_first:]
     row_count = tokens.shape[0]
     block_rows = min(512, row_count)
     block_count = row_count // block_rows
@@ -284,29 +333,51 @@
     first_sum = inputs + attn_normed
     ffn_input, pull_third = jax.vjp(rms_scale, first_sum, gains_float[2])
     ffn_low = ffn_input.astype(jnp.bfloat16)
+    if tree:
+        ffn_low = paired(ffn_low)
     gate_up = times_transposed(ffn_low, w_gate_up)
-    hidden, pull_fourth = jax.vjp(geglu, gate_up[:, :FF], gate_up[:, FF:])
+    hidden, pull_fourth = jax.vjp(geglu, gate_up[:, :hidden_width], gate_up[:, hidden_width:])
     hidden_low = hidden.astype(jnp.bfloat16)
-    branch = jnp.dot(hidden_low, w_down, preferred_element_type=jnp.float32)
+    if tree:
+        other_branch = jnp.dot(
+            hidden_low[row_count:], w_down, preferred_element_type=jnp.float32
+        )
+        hidden_low, other_branch = tied(hidden_low, other_branch)
+        own_branch, other_branch = tied(
+            jnp.dot(hidden_low[:row_count], w_down, preferred_element_type=jnp.float32),
+            to_partner(other_branch),
+        )
+        branch = own_branch + other_branch
+    else:
+        branch = jnp.dot(hidden_low, w_down, preferred_element_type=jnp.float32)
     ffn_normed, pull_fifth = jax.vjp(rms_scale, branch, gains_float[3])
     result = first_sum + ffn_normed
     upstream = cotangent.astype(jnp.float32)
     branch_grad, gain_four = pull_fifth(upstream)
     branch_low = branch_grad.astype(jnp.bfloat16)
-    tree = wide_count == 8 and shard_count == 4
-    factors = {"down": (gate_end, total_rows, hidden_low, branch_low)}
+    if tree:
+        branch_low = paired(branch_low)
+
+    def product_rows(left, right):
+        def rows(first, last):
+            return contract_rows(left[:, first:last], right).astype(jnp.bfloat16)
+
+        return rows
+
+    factors = {
+        "down": (down_first, total_rows // split, product_rows(hidden_low, branch_low))
+    }
     steps = {}
-    late_rows = qkv_rows
+    late_rows = qkv_rows // split
+    segment_rows = owner_rows // split
 
     def bounds(key):
-        return (max(key * owner_rows, late_rows), (key + 1) * owner_rows)
+        return (max(key * segment_rows, late_rows), (key + 1) * segment_rows)
 
     def plane_terms(first, last):
         parts = [
-            contract_rows(
-                left[:, max(first, start) - start : min(last, end) - start], right
-            ).astype(jnp.bfloat16)
-            for start, end, left, right in sorted(factors.values(), key=lambda f: f[0])
+            rows(max(first, start) - start, min(last, end) - start)
+            for start, end, rows in sorted(factors.values(), key=lambda f: f[0])
             if max(first, start) < min(last, end)
         ]
         return parts[0] if len(parts) == 1 else jnp.concatenate(parts, axis=0)
@@ -321,7 +392,7 @@
             return anchor
         terms = [plane_terms(*bounds(key)) for key in keys]
         for key, term in zip(keys, terms):
-            steps[key] = [lax.psum_scatter(term, "wide", scatter_dimension=0, tiled=True)]
+            steps[key] = [lax.psum_scatter(term, "chip", scatter_dimension=0, tiled=True)]
         return tied(anchor, terms)[0]
 
     def advance(key):
@@ -338,23 +409,45 @@
             advance(key)
         return anchor
 
-    branch_low = start_ready(branch_low, gate_end)
+    branch_low = start_ready(branch_low, down_first)
     hidden_grad = times_transposed(branch_low, w_down)
     gate_grad, up_grad = pull_fourth(hidden_grad)
     gate_low, up_low = gate_grad.astype(jnp.bfloat16), up_grad.astype(jnp.bfloat16)
-    factors["gate"] = (out_end, out_end + FF, gate_low, ffn_low)
-    factors["up"] = (out_end + FF, gate_end, up_low, ffn_low)
-    gate_low, up_low = start_ready((gate_low, up_low), out_end)
+    factors["gate"] = (gate_first, up_first, product_rows(gate_low, ffn_low))
+    factors["up"] = (up_first, down_first, product_rows(up_low, ffn_low))
+    gate_low, up_low = start_ready((gate_low, up_low), gate_first)
     gate_low, up_low = tick((gate_low, up_low), 3)
-    ffn_input_grad = jnp.dot(
-        gate_low, w_gate_up[:FF], preferred_element_type=jnp.float32
-    ) + jnp.dot(up_low, w_gate_up[FF:], preferred_element_type=jnp.float32)
+
+    def input_grad_of(first, last):
+        return jnp.dot(
+            gate_low[first:last], w_gate_up[:hidden_width], preferred_element_type=jnp.float32
+        ) + jnp.dot(
+            up_low[first:last], w_gate_up[hidden_width:], preferred_element_type=jnp.float32
+        )
+
+    if tree:
+        other_grad = input_grad_of(row_count, 2 * row_count)
+        (gate_low, up_low), other_grad = tied((gate_low, up_low), other_grad)
+        ffn_input_grad = input_grad_of(0, row_count) + to_partner(other_grad)
+    else:
+        ffn_input_grad = input_grad_of(0, row_count)
     ffn_input_grad = tick(ffn_input_grad, 3)
     sum_grad_part, gain_three = pull_third(ffn_input_grad)
     sum_grad = upstream + sum_grad_part
     attended_grad, gain_two = pull_second(sum_grad)
     attended_low = attended_grad.astype(jnp.bfloat16)
-    factors["out"] = (qkv_rows, out_end, mixed_low, attended_low)
+    out_rows = product_rows(mixed_low, attended_low)
+
+    def summed_out_rows(first, last):
+        rows = out_rows(first * 2, last * 2)
+        other = to_partner(one_parity(rows, 1 - core_index))
+        return add_low(one_parity(rows, core_index), other)
+
+    factors["out"] = (
+        qkv_rows // split,
+        gate_first,
+        summed_out_rows if tree else out_rows,
+    )
     mixed_grad = (
         times_transposed(attended_low, w_out)
         .astype(jnp.bfloat16)
@@ -411,51 +504,59 @@
         ],
         axis=1,
     ).astype(jnp.bfloat16)
-    factors["qkv"] = (0, qkv_rows, qkv_low, normed_low)
+    factors["qkv"] = (0, qkv_rows // split, product_rows(qkv_low, normed_low))
     normed_grad = jnp.dot(qkv_low, w_qkv, preferred_element_type=jnp.float32)
     input_part, gain_one = pull_first(normed_grad)
     input_grad = sum_grad + input_part
     state = (params, first_moment, second_moment)
     if tree:
-        steps[-1] = [
-            lax.psum_scatter(plane_terms(0, late_rows), "wide", scatter_dimension=0, tiled=True)
-        ]
+        qkv_grad = product_rows(qkv_low, normed_low)(0, qkv_rows)
+        by_piece = (
+            qkv_grad.reshape(wide_count // 2, -1, 2, 8, D)
+            .transpose(0, 2, 1, 3, 4)
+            .reshape(qkv_rows, D)
+        )
+        steps[-1] = [lax.psum_scatter(by_piece, WIDE, scatter_dimension=0, tiled=True)]
         for key in (3, 2, 1, 0, -1):
             while len(steps[key]) < 3:
                 advance(key)
-        late_part = late_rows // wide_count
+        late_part = qkv_rows // wide_count
         early_part = owner_rows // wide_count - late_part
         whole_pieces = [steps[owner][-1] for owner in range(1, shard_count)]
         early_piece = choose_owner([steps[0][-1]] + [p[:early_part] for p in whole_pieces])
         late_piece = choose_owner([steps[-1][-1]] + [p[early_part:] for p in whole_pieces])
         first_owner = lax.axis_index("shard") == 0
+        early_groups, late_groups = early_part // 8, late_part // 8
         early_place = jnp.where(
             first_owner,
-            jnp.array([late_rows, early_part], jnp.int32),
-            jnp.array([0, early_part + late_part], jnp.int32),
+            jnp.array([qkv_rows // 16, early_groups], jnp.int32),
+            jnp.array([0, early_groups + late_groups], jnp.int32),
         )
         late_place = jnp.where(
             first_owner,
-            jnp.array([0, late_part], jnp.int32),
-            jnp.array([early_part, early_part + late_part], jnp.int32),
-        )
-        early_low = lax.all_gather(early_piece, "wide", axis=0, tiled=True)
-        late_low = lax.all_gather(late_piece, "wide", axis=0, tiled=True)
+            jnp.array([0, late_groups], jnp.int32),
+            jnp.array([early_groups, early_groups + late_groups], jnp.int32),
+        )
+        early_low = lax.all_gather(early_piece, WIDE, axis=0, tiled=True)
+        late_low = lax.all_gather(late_piece, WIDE, axis=0, tiled=True)
+        state = [split_rows(rows) for rows in (params, first_moment, second_moment)]
         carried = adam_rows(early_place, early_part, early_low, state, ())
-        row_grad, new_params, new_first, new_second = adam_rows(
-            late_place, late_part, late_low, state, carried
-        )
+        row_grad, new_params, new_first, new_second = [
+            rows.reshape(owner_rows, D)
+            for rows in adam_rows(late_place, late_part, late_low, state, carried)
+        ]
     else:
         own = lax.psum_scatter(
-            plane_terms(0, total_rows), ("shard", "wide"), scatter_dimension=0, tiled=True
-        )
-        own_low = lax.all_gather(own, "wide", axis=0, tiled=True)
-        block = max(size for size in range(8, 329, 8) if owner_rows % size == 0)
-        row_grad, new_params, new_first, new_second = adam_rows(
-            jnp.array([0, block], jnp.int32), block, own_low, state, ()
+            plane_terms(0, total_rows), ("shard",) + WIDE, scatter_dimension=0, tiled=True
+        )
+        row_grad = lax.all_gather(own, WIDE, axis=0, tiled=True).astype(jnp.float32)
+        new_params, new_first, new_second = adam_update(
+            params, row_grad, first_moment, second_moment, weight_decay
         )
     gain_terms = jnp.stack([gain_one, gain_two, gain_three, gain_four])
-    gain_total = butterfly_sum(butterfly_sum(gain_terms, "wide"), "shard")
+    gain_total = butterfly_sum(
+        butterfly_sum(gain_terms, WIDE, wide_count), "shard", shard_count
+    )
     gain_grad = lax.dynamic_slice_in_dim(
         gain_total, lax.axis_index("shard") * gains.shape[1], gains.shape[1], axis=1
     )
@@ -477,13 +578,17 @@
 
 
 def solution(mesh):
+    split_mesh = Mesh(
+        mesh.devices.reshape(mesh.shape["wide"] // 2, 2, mesh.shape["shard"]),
+        ("chip", "core", "shard"),
+    )
     return jax.shard_map(
         per_device,
-        mesh=mesh,
+        mesh=split_mesh,
         in_specs=(
-            P(("wide", "shard"), None),
-            P(("wide", "shard")),
-            P(("wide", "shard"), None),
+            P(("chip", "core", "shard"), None),
+            P(("chip", "core", "shard")),
+            P(("chip", "core", "shard"), None),
             P("shard", None),
             P(None, "shard"),
             P("shard", None),
@@ -492,8 +597,8 @@
             P(None, "shard"),
         ),
         out_specs=(
-            P(("wide", "shard"), None),
-            P(("wide", "shard"), None),
+            P(("chip", "core", "shard"), None),
+            P(("chip", "core", "shard"), None),
             P("shard", None),
             P(None, "shard"),
             P("shard", None),

time: 1110 us -> 1070 us (0.964)
  other arithmetic: 166 us -> 141 us
  waiting for transfers between devices: 395 us -> 377 us
    unnamed x9, waiting for transfers between devices: 57.6 us -> 0.13 us
    ppermute x10, waiting for transfers between devices: 84.4 us -> 127 us  [advance(): steps[key].append(add_low(held, lax.ppermute(held, 'shard', pairs)))]
    concatenate x3, other arithmetic: 51 us -> 14 us  [plane_terms(): return parts[0] if len(parts) == 1 else jnp.concatenate(parts, axis=0)]
    dot_general x3 -> x6, matrix products: 71.7 us -> 94.3 us  [the longest x2 35 us: input_grad_of(): jnp.dot(gate_low[first:last], w_gate_up[:hidden_width], preferred_element...]
    dot_general x8, matrix products: 111 us -> 97.6 us  [contract_rows(): lax.dot_general(left_side, right_side, (((0,), (0,)), ((), ())), preferre...]
    ppermute x7 -> x12, waiting for transfers between devices: 68.2 us -> 78 us  [the longest x7 69.3 us: spread_first(): other = lax.ppermute(block, WIDE, [(i, i ^ bit) for i in range(8)])]
  transfers between devices with their start and end apart: 35 -> 40, of which waited for: 19 -> 21; matrix products, arithmetic and copies ran while one was open for 37% -> 39% of each run, Pallas kernels for 5% -> 5%
where the time goes in v3:
time: 1070 us; the launch traced here: 1060 us
  waiting for transfers between devices  377 us (35%)
  matrix products  341 us (32%)
  other arithmetic  141 us (13%)
  Pallas kernels  74.1 us (7%)
  local copies, waits for them, and re-layouts  65.1 us (6%)
  starting transfers between devices  44.7 us (4%)
  between operations  16.7 us (2%)
    ppermute x10, waiting for transfers between devices, advance(): steps[key].append(add_low(held, lax.ppermute(held, 'shard', pairs)))  127 us
    all_gather x1, waiting for transfers between devices, per_device(): lax.all_gather(one_parity(chip_slice, core_index).astype(jnp.bfloat16), (...  111 us
    dot_general x4, matrix products, times_transposed(): lax.dot_general(left_side, right_side, (((1,), (1,)), ((), ())), preferre...  98.9 us
    dot_general x8, matrix products, contract_rows(): lax.dot_general(left_side, right_side, (((0,), (0,)), ((), ())), preferre...  97.6 us
    pallas_call x2, Pallas kernels, adam_rows(): pl.pallas_call(body, grid_spec=pltpu.PrefetchScalarGridSpec(num_scalar_pr...  74.1 us
    ppermute x7, waiting for transfers between devices, spread_first(): other = lax.ppermute(block, WIDE, [(i, i ^ bit) for i in range(8)])  69.3 us
    dot_general x2, matrix products, input_grad_of(): jnp.dot(gate_low[first:last], w_gate_up[:hidden_width], preferred_element...  35 us
    dot_general x2, matrix products, input_grad_of(): jnp.dot(up_low[first:last], w_gate_up[hidden_width:], preferred_element_t...  29 us
  transfers between devices with their start and end apart: 40, of which 21 were waited for; matrix products, arithmetic and copies ran while one was open for 39% of the time, Pallas kernels for 5%

profile of v3, /device:TPU:0, one launch (start us, length us, event | category | flops | bytes accessed | tf_op | source)
XLA Modules:
  0.0 1060.7 jit_solution(194356730900470557)
XLA Ops:
  13.5 6.8 collective-permute-start.3
  20.4 25.8 %collective-permute-done.3 = bf16[320,1152]{1,0:T(8,128)(2,1)} collective-permute-done((bf16[320,1152]{1,0:T(8,128)(2,1)S(1)}, bf16[320,1152]{1,0:T(8,128)(2,1)}, u32[]{:S(2)}, u32[]{:S(2)}) %collective-permute-start.3) | collective-permute-done | bytes 737312 | tf_op jit(solution)/shard_map/ppermute | solution.py:139
  56.8 23.6 %collective-permute-done.4 = bf16[320,1152]{1,0:T(8,128)(2,1)} collective-permute-done((bf16[320,1152]{1,0:T(8,128)(2,1)S(1)}, bf16[320,1152]{1,0:T(8,128)(2,1)}, u32[]{:S(2)}, u32[]{:S(2)}) %collective-permute-start.4) | collective-permute-done | bytes 737312 | tf_op jit(solution)/shard_map/ppermute | solution.py:141
  85.6 13.1 %collective-permute-done.5 = bf16[320,1152]{1,0:T(8,128)(2,1)} collective-permute-done((bf16[320,1152]{1,0:T(8,128)(2,1)S(1)}, bf16[320,1152]{1,0:T(8,128)(2,1)}, u32[]{:S(2)}, u32[]{:S(2)}) %collective-permute-start.5) | collective-permute-done | bytes 737312 | tf_op jit(solution)/shard_map/ppermute | solution.py:149
  106.3 30.2 %collective-permute-done.6 = bf16[320,1152]{1,0:T(8,128)(2,1)} collective-permute-done((bf16[320,1152]{1,0:T(8,128)(2,1)}, bf16[320,1152]{1,0:T(8,128)(2,1)}, u32[]{:S(2)}, u32[]{:S(2)}) %collective-permute-start.6) | collective-permute-done | bytes 737312 | tf_op jit(solution)/shard_map/ppermute | solution.py:149
  140.6 24.7 %collective-permute-done.9 = bf16[320,1152]{1,0:T(8,128)(2,1)} collective-permute-done((bf16[320,1152]{1,0:T(8,128)(2,1)}, bf16[320,1152]{1,0:T(8,128)(2,1)}, u32[]{:S(2)}, u32[]{:S(2)}) %collective-permute-start.9) | collective-permute-done | bytes 737312 | tf_op jit(solution)/shard_map/ppermute | solution.py:149
  198.5 26.9 %while.31 = (s32[]{:T(128)}, bf16[2,512,1,4,256]{4,1,3,2,0:T(8,128)(2,1)}, f32[2,1,4,512,1]{3,2,4,1,0:T(4,128)S(1)}, s32[2,512]{1,0:T(2,128)S(1)}, s32[1024]{0:T...) while((s32[]{:T(128)}, ...), condition=%wide.region_6.7_spmd.clone, body=%wide.region_3.6_spmd.sunk.clone | while | flops 2186279424 | bytes 50411736 | solution.py:329
  245.1 111.1 %all-gather.4.cloned.1.call-done = bf16[11648,1152]{1,0:T(8,128)(2,1)} async-done(((bf16[728,1152]{1,0:T(8,128)(2,1)}), bf16[11648,1152]{1,0:T(8,128)(2,1)}) %all-gather.4.cloned.1.call-update) | async-done | bytes 26837008 | tf_op jit(solution)/shard_map/all_gather | solution.py:261
  356.2 44.0 %fusion.73 = f32[2048,6912]{1,0:T(8,128)} fusion(bf16[11648,1152]{1,0:T(8,128)(2,1)} %all-gather.4.cloned.1.call-done, bf16[1024,1152]{1,0:T(8,128)(2,1)} %collective-permute-done.12, bf16[1024,1152]{1,0:T(8,128)(2,1)S(1)} %multiply_convert_fusion.2), kind=kOutput, calls=%fused_computation.88 | convolution fusion | flops 32624345088 | bytes 77266944 | tf_op jit(solution)/shard_map/dot_general | solution.py:77
  400.3 25.2 %multiply_convert_fusion.1 = bf16[2048,3456]{1,0:T(8,128)(2,1)} fusion(f32[2048,6912]{1,0:T(8,128)} %fusion.73), kind=kLoop, calls=%fused_computation.86 | loop fusion | flops 70778880 | bytes 70778880 | tf_op jit(solution)/shard_map/convert_element_type | solution.py:340
  425.4 15.6 %fusion.86 = f32[1024,1152]{1,0:T(8,128)} fusion(bf16[2048,3456]{1,0:T(8,128)(2,1)} %multiply_convert_fusion.1, bf16[11648,1152]{1,0:T(8,128)(2,1)} %all-gather.4.cloned.1.call-done), kind=kOutput, calls=%fused_computation.106 | convolution fusion | flops 8153726976 | bytes 19759104 | tf_op jit(solution)/shard_map/dot_general | solution.py:342
  441.1 14.6 %fusion.96 = f32[1024,1152]{1,0:T(8,128)} fusion(bf16[2048,3456]{1,0:T(8,128)(2,1)S(1)} %copy-done.13, bf16[11648,1152]{1,0:T(8,128)(2,1)} %all-gather.4.cloned.1.call-done), kind=kOutput, calls=%fused_computation.116 | convolution fusion | flops 8153726976 | bytes 19759104 | tf_op jit(solution)/shard_map/dot_general | solution.py:347
  469.6 22.2 %fusion.77 = bf16[2912,1152]{1,0:T(8,128)(2,1)} fusion(bf16[2048,3456]{1,0:T(8,128)(2,1)} %multiply_convert_fusion.1, bf16[1024,1152]{1,0:T(8,128)(2,1)S(1)} %collective-permute-done.14, bf16[1024,1152]{1,0:T(8,128)(2,1)S(1)} %get-tuple-element.461), kind=kOutput, calls=%fused_computation.92 | convolution fusion | flops 13753331712 | bytes 23486464 | tf_op jit(solution)/shard_map/dot_general | solution.py:71
  496.5 6.5 convolution_convert_fusion.5
  503.0 45.0 %multiply_convert_fusion = (bf16[2048,3456]{1,0:T(8,128)(2,1)}, bf16[2048,3456]{1,0:T(8,128)(2,1)}) fusion(f32[2048,6912]{1,0:T(8,128)} %fusion.73, bf16[2048,1152]{1,0:T(8,128)(2,1)} %pad_maximum_fusion.4, bf16[11648,1152]{1,0:T(8,128)(2,1)} %all-gather.4.cloned.1.call-done), kind=kOutput, calls=%fused_computation.85 | convolution fusion | flops 16477323264 | bytes 97615872 | tf_op jit(solution)/shard_map/dot_general | solution.py:77
  548.0 20.4 %convolution_convert_fusion = bf16[2368,1152]{1,0:T(8,128)(2,1)} fusion(bf16[2048,3456]{1,0:T(8,128)(2,1)} %get-tuple-element.249, bf16[1024,1152]{1,0:T(8,128)(2,1)} %collective-permute-done.12, bf16[1024,1152]{1,0:T(8,128)(2,1)S(1)} %copy-done.28), kind=kOutput, calls=%fused_computation.93 | convolution fusion | flops 11185790976 | bytes 20135936 | tf_op jit(solution)/shard_map/dot_general | solution.py:71
  574.4 9.9 convolution_convert_fusion.3
  584.3 14.7 %fusion.83 = bf16[1824,1152]{1,0:T(8,128)(2,1)S(1)} fusion(bf16[2048,3456]{1,0:T(8,128)(2,1)} %get-tuple-element.248, bf16[1024,1152]{1,0:T(8,128)(2,1)} %collective-permute-done.12, bf16[1024,1152]{1,0:T(8,128)(2,1)S(1)} %copy-done.29), kind=kOutput, calls=%fused_computation.103 | convolution fusion | flops 8618250240 | bytes 16785408 | tf_op jit(solution)/shard_map/dot_general | solution.py:71
  602.4 13.2 %fusion.92 = f32[1024,1152]{1,0:T(8,128)S(1)} fusion(bf16[2048,3456]{1,0:T(8,128)(2,1)} %get-tuple-element.249, bf16[11648,1152]{1,0:T(8,128)(2,1)} %all-gather.4.cloned.1.call-done), kind=kOutput, calls=%fused_computation.112 | convolution fusion | flops 8153726976 | bytes 19759104 | tf_op jit(solution)/shard_map/dot_general | solution.py:424
  615.7 15.8 %fusion.111 = f32[1024,1152]{1,0:T(8,128)} fusion(f32[1024,1152]{1,0:T(8,128)S(1)} %fusion.92, bf16[11648,1152]{1,0:T(8,128)(2,1)} %all-gather.4.cloned.1.call-done, bf16[2048,3456]{1,0:T(8,128)(2,1)} %get-tuple-element.248), kind=kOutput, calls=%fused_computation.141 | convolution fusion | flops 8154906624 | bytes 24477696 | tf_op jit(solution)/shard_map/dot_general | solution.py:422
  634.3 15.8 %fusion.88 = f32[1024,1152]{1,0:T(8,128)} fusion(bf16[2048,3456]{1,0:T(8,128)(2,1)} %get-tuple-element.249, bf16[11648,1152]{1,0:T(8,128)(2,1)} %all-gather.4.cloned.1.call-done), kind=kOutput, calls=%fused_computation.108 | convolution fusion | flops 8153726976 | bytes 19759104 | tf_op jit(solution)/shard_map/dot_general | solution.py:424
  650.1 20.6 %collective-permute-done.16 = bf16[728,1152]{1,0:T(8,128)(2,1)S(1)} collective-permute-done((bf16[728,1152]{1,0:T(8,128)(2,1)S(1)}, bf16[728,1152]{1,0:T(8,128)(2,1)S(1)}, u32[]{:S(2)}, u32[]{:S(2)}) %collective-permute-start.16) | collective-permute-done | bytes 1677344 | tf_op jit(solution)/shard_map/ppermute | solution.py:401
  672.4 19.2 %fusion.121 = f32[1024,1152]{1,0:T(8,128)} fusion(f32[1024,1152]{1,0:T(8,128)} %collective-permute-done.15, f32[1024,1152]{1,0:T(8,128)} %fusion.88, bf16[11648,1152]{1,0:T(8,128)(2,1)} %all-gather.4.cloned.1.call-done, bf16[2048,3456]{1,0:T(8,128)(2,1)} %get-tuple-element.248), kind=kOutput, calls=%fused_computation.143 | convolution fusion | flops 8156086272 | bytes 29196288 | tf_op jit(solution)/shard_map/dot_general | solution.py:422
  707.5 14.7 %convolution_convert_fusion.2 = bf16[1632,1152]{1,0:T(8,128)(2,1)} fusion(bf16[2048,3456]{1,0:T(8,128)(2,1)} %get-tuple-element.248, bf16[1024,1152]{1,0:T(8,128)(2,1)} %collective-permute-done.12, bf16[1024,1152]{1,0:T(8,128)(2,1)S(1)} %copy-done.30), kind=kOutput, calls=%fused_computation.104 | convolution fusion | flops 7712059392 | bytes 15294464 | tf_op jit(solution)/shard_map/dot_general | solution.py:71
  744.2 48.9 %while.32 = (s32[]{:T(128)}, f32[1024,1,256]{0,2,1:T(8,128)S(1)}, f32[1024,1,256]{0,2,1:T(8,128)}, f32[2,512,1,4,256]{4,1,3,2,0:T(8,128)}, bf16[2,512,1,4,256]{4...) while((s32[]{:T(128)}, f32[1024,1,256]{0,2,1:T(8,128)S(1)}, ...), condition=%wide.region_17.18_spmd.clone.clone, body=%wide.region_15.17_spmd.clone.sunk.clone | while | flops 5423233536 | bytes 125376864 | solution.py:489
  826.2 21.9 %collective-permute-done.21 = bf16[728,1152]{1,0:T(8,128)(2,1)} collective-permute-done((bf16[728,1152]{1,0:T(8,128)(2,1)}, bf16[728,1152]{1,0:T(8,128)(2,1)}, u32[]{:S(2)}, u32[]{:S(2)}) %collective-permute-start.21) | collective-permute-done | bytes 1677344 | tf_op jit(solution)/shard_map/ppermute | solution.py:401
  861.5 57.4 %collective-permute-done.26 = bf16[536,1152]{1,0:T(8,128)(2,1)S(1)} collective-permute-done((bf16[536,1152]{1,0:T(8,128)(2,1)S(1)}, bf16[536,1152]{1,0:T(8,128)(2,1)S(1)}, u32[]{:S(2)}, u32[]{:S(2)}) %collective-permute-start.26) | collective-permute-done | bytes 1234976 | tf_op jit(solution)/shard_map/ppermute | solution.py:401
  922.0 11.5 %collective-permute-done.23 = bf16[192,1152]{1,0:T(8,128)(2,1)S(1)} collective-permute-done((bf16[192,1152]{1,0:T(8,128)(2,1)}, bf16[192,1152]{1,0:T(8,128)(2,1)S(1)}, u32[]{:S(2)}, u32[]{:S(2)}) %collective-permute-start.23) | collective-permute-done | bytes 442400 | tf_op jit(solution)/shard_map/ppermute | solution.py:401
  936.2 11.2 %collective-permute-done.24 = bf16[192,1152]{1,0:T(8,128)(2,1)S(1)} collective-permute-done((bf16[192,1152]{1,0:T(8,128)(2,1)S(1)}, bf16[192,1152]{1,0:T(8,128)(2,1)S(1)}, u32[]{:S(2)}, u32[]{:S(2)}) %collective-permute-start.24) | collective-permute-done | bytes 442400 | tf_op jit(solution)/shard_map/ppermute | solution.py:401
  950.1 8.2 fusion.127
  979.3 52.0 %adam_rows.2 = (f32[364,2,8,1152]{3,2,1,0:T(8,128)}, f32[364,2,8,1152]{3,2,1,0:T(8,128)}, f32[364,2,8,1152]{3,2,1,0:T(8,128)}, f32[364,2,8,1152]{3,2,1,0:T(8,128)}) custom-call(s32[2]{0:T(128)} %broadcast_select_fusion.12.place_ref, bf16[4288,1152]{1,0:T(8,128)(2,1)} %all-gather.8.cloned.1.call-done.grad_ref, f32[364,2,8,1152]{3,2,1,0:T(8,128)} %bitcast.318, ...), custom_call_target="tpu_custom_call" | custom-call | flops 98795520 | bytes 148193280 | tf_op jit(solution)/shard_map/adam_rows/pallas_call | solution.py:218
  1031.3 22.1 %adam_rows.3 = (f32[364,2,8,1152]{3,2,1,0:T(8,128)}, f32[364,2,8,1152]{3,2,1,0:T(8,128)}, f32[364,2,8,1152]{3,2,1,0:T(8,128)}, f32[364,2,8,1152]{3,2,1,0:T(8,128)}) custom-call(s32[2]{0:T(128)} %broadcast_select_fusion.13.place_ref, ...), custom_call_target="tpu_custom_call", output_to_operand_aliasing={{0}: (5, {}), {1}: (6, {}), {2}: (7, {}), {3}: (8, {})} | custom-call | flops 35389440 | bytes 53084160 | tf_op jit(solution)/shard_map/adam_rows/pallas_call | solution.py:218
  (460 shorter events, 306.2 us)
Async XLA Ops:
  7.2 349.1 %all-gather.4.cloned.1.call-start = ((), (), s32[]{:S(2)}) async-start(), calls=%async_computation.5 | async-start | bytes 28514304 | tf_op jit(solution)/shard_map/all_gather | solution.py:261
  11.8 590.6 %reduce-scatter.16.cloned.1.call-start = ((), (), s32[]{:S(2)}) async-start(), calls=%async_computation.9 | async-start | bytes 8386560
  13.5 32.6 %collective-permute-start.3 = (bf16[320,1152]{1,0:T(8,128)(2,1)S(1)}, bf16[320,1152]{1,0:T(8,128)(2,1)}, u32[]{:S(2)}, u32[]{:S(2)}) collective-permute-start(bf16[320,1152]{1,0:T(8,128)(2,1)S(1)} %dynamic-slice_convert_fusion.1), channel_id=1, source_target_pairs={{0,2},{4,6},{8,10},{12,14},{16,18},{20,22},{24,26},{28,30}} | collective-permute-start | bytes 2211848 | tf_op jit(solution)/shard_map/ppermute | solution.py:139
  47.7 32.7 %collective-permute-start.4 = (bf16[320,1152]{1,0:T(8,128)(2,1)S(1)}, bf16[320,1152]{1,0:T(8,128)(2,1)}, u32[]{:S(2)}, u32[]{:S(2)}) collective-permute-start(bf16[320,1152]{1,0:T(8,128)(2,1)S(1)} %broadcast_select_fusion), channel_id=1, source_target_pairs={{0,1},{2,3},{4,5},{6,7},{8,9},{10,11},{12,13},{14,15},{16,17},{18,... | collective-permute-start | bytes 2211848 | tf_op jit(solution)/shard_map/ppermute | solution.py:141
  49.8 89.8 %collective-permute-start.2 = (bf16[4,288]{1,0:T(4,128)(2,1)S(1)}, bf16[4,288]{1,0:T(4,128)(2,1)S(1)}, u32[]{:S(2)}, u32[]{:S(2)}) collective-permute-start(bf16[4,288]{1,0:T(4,128)(2,1)S(1)} %convert_element_type.227), channel_id=1, source_target_pairs={{0,3},{1,0},{2,1},{3,2},{4,7},{5,4},{6,5},{7,6},{8,11},{9,8},{10,9... | collective-permute-start | bytes 6920 | tf_op jit(solution)/shard_map/ppermute | solution.py:131
  49.8 89.5 %collective-permute-start.1 = (bf16[4,288]{1,0:T(4,128)(2,1)S(1)}, bf16[4,288]{1,0:T(4,128)(2,1)S(1)}, u32[]{:S(2)}, u32[]{:S(2)}) collective-permute-start(bf16[4,288]{1,0:T(4,128)(2,1)S(1)} %convert_element_type.227), channel_id=1, source_target_pairs={{0,2},{1,3},{2,0},{3,1},{4,6},{5,7},{6,4},{7,5},{8,10},{9,11},{10,... | collective-permute-start | bytes 6920 | tf_op jit(solution)/shard_map/ppermute | solution.py:131
  53.7 85.4 %collective-permute-start = (bf16[4,288]{1,0:T(4,128)(2,1)S(1)}, bf16[4,288]{1,0:T(4,128)(2,1)S(1)}, u32[]{:S(2)}, u32[]{:S(2)}) collective-permute-start(bf16[4,288]{1,0:T(4,128)(2,1)S(1)} %convert_element_type.227), channel_id=1, source_target_pairs={{0,1},{1,2},{2,3},{3,0},{4,5},{5,6},{6,7},{7,4},{8,9},{9,10},{10,1... | collective-permute-start | bytes 6920 | tf_op jit(solution)/shard_map/ppermute | solution.py:131
  81.6 17.0 %collective-permute-start.5 = (bf16[320,1152]{1,0:T(8,128)(2,1)S(1)}, bf16[320,1152]{1,0:T(8,128)(2,1)}, u32[]{:S(2)}, u32[]{:S(2)}) collective-permute-start(bf16[320,1152]{1,0:T(8,128)(2,1)S(1)} %broadcast_select_fusion.1), channel_id=1, source_target_pairs={{0,16},{4,20},{8,24},{12,28},{16,0},{20,4},{24,8},{28,12},{1,17},{... | collective-permute-start | bytes 2211848 | tf_op jit(solution)/shard_map/ppermute | solution.py:149
  101.0 35.5 %collective-permute-start.6 = (bf16[320,1152]{1,0:T(8,128)(2,1)}, bf16[320,1152]{1,0:T(8,128)(2,1)}, u32[]{:S(2)}, u32[]{:S(2)}) collective-permute-start(bf16[320,1152]{1,0:T(8,128)(2,1)} %get-tuple-element.471), channel_id=1, source_target_pairs={{0,8},{4,12},{8,0},{12,4},{16,24},{20,28},{24,16},{28,20},{1,9},{5... | collective-permute-start | bytes 2211848 | tf_op jit(solution)/shard_map/ppermute | solution.py:149
  105.3 60.0 %collective-permute-start.9 = (bf16[320,1152]{1,0:T(8,128)(2,1)}, bf16[320,1152]{1,0:T(8,128)(2,1)}, u32[]{:S(2)}, u32[]{:S(2)}) collective-permute-start(bf16[320,1152]{1,0:T(8,128)(2,1)} %get-tuple-element.470), channel_id=1, source_target_pairs={{0,8},{4,12},{8,0},{12,4},{16,24},{20,28},{24,16},{28,20},{1,9},{5... | collective-permute-start | bytes 2211848 | tf_op jit(solution)/shard_map/ppermute | solution.py:149
  138.8 29.4 %collective-permute-start.7 = (bf16[320,1152]{1,0:T(8,128)(2,1)}, bf16[320,1152]{1,0:T(8,128)(2,1)}, u32[]{:S(2)}, u32[]{:S(2)}) collective-permute-start(bf16[320,1152]{1,0:T(8,128)(2,1)} %get-tuple-element.473), channel_id=1, source_target_pairs={{0,4},{4,0},{8,12},{12,8},{16,20},{20,16},{24,28},{28,24},{1,5},{5... | collective-permute-start | bytes 2211848 | tf_op jit(solution)/shard_map/ppermute | solution.py:149
  167.7 62.5 %collective-permute-start.11 = (bf16[320,1152]{1,0:T(8,128)(2,1)}, bf16[320,1152]{1,0:T(8,128)(2,1)}, u32[]{:S(2)}, u32[]{:S(2)}) collective-permute-start(bf16[320,1152]{1,0:T(8,128)(2,1)} %get-tuple-element.468), channel_id=1, source_target_pairs={{0,4},{4,0},{8,12},{12,8},{16,20},{20,16},{24,28},{28,24},{1,5},{5... | collective-permute-start | bytes 2211848 | tf_op jit(solution)/shard_map/ppermute | solution.py:149
  167.7 5.0 collective-permute-start.10
  441.1 14.7 %collective-permute-start.13 = (f32[1024,1152]{1,0:T(8,128)}, f32[1024,1152]{1,0:T(8,128)S(1)}, u32[]{:S(2)}, u32[]{:S(2)}) collective-permute-start(f32[1024,1152]{1,0:T(8,128)} %fusion.86), channel_id=1, source_target_pairs={{0,4},{4,0},{1,5},{5,1},{2,6},{6,2},{3,7},{7,3},{8,12},{12,8},{9,1... | collective-permute-start | bytes 14155784 | tf_op jit(solution)/shard_map/ppermute | solution.py:181
  491.8 246.8 %reduce-scatter.18.cloned.1.call-start = ((), (), s32[]{:S(2)}) async-start(), calls=%async_computation.10 | async-start | bytes 8386560
  574.3 226.7 %reduce-scatter.20.cloned.1.call-start = ((), (), s32[]{:S(2)}) async-start(), calls=%async_computation.11 | async-start | bytes 8386560
  631.4 40.9 %collective-permute-start.15 = (f32[1024,1152]{1,0:T(8,128)}, f32[1024,1152]{1,0:T(8,128)}, u32[]{:S(2)}, u32[]{:S(2)}) collective-permute-start(f32[1024,1152]{1,0:T(8,128)} %fusion.111), channel_id=1, source_target_pairs={{0,4},{4,0},{1,5},{5,1},{2,6},{6,2},{3,7},{7,3},{8,12},{12,8},{9,1... | collective-permute-start | bytes 14155784 | tf_op jit(solution)/shard_map/ppermute | solution.py:181
  631.7 192.9 %reduce-scatter.22.cloned.1.call-start = ((), (), s32[]{:S(2)}) async-start(), calls=%async_computation.12 | async-start | bytes 6174720
  632.9 37.8 %collective-permute-start.16 = (bf16[728,1152]{1,0:T(8,128)(2,1)S(1)}, bf16[728,1152]{1,0:T(8,128)(2,1)S(1)}, u32[]{:S(2)}, u32[]{:S(2)}) collective-permute-start(bf16[728,1152]{1,0:T(8,128)(2,1)S(1)} %copy-done.38), channel_id=1, source_target_pairs={{0,1},{2,3},{4,5},{6,7},{8,9},{10,11},{12,13},{14,15},{16,17},{18,... | collective-permute-start | bytes 5031944 | tf_op jit(solution)/shard_map/ppermute | solution.py:401
  707.4 24.9 %collective-permute-start.17 = (bf16[512,1152]{1,0:T(8,128)(2,1)}, bf16[512,1152]{1,0:T(8,128)(2,1)}, u32[]{:S(2)}, u32[]{:S(2)}) collective-permute-start(bf16[512,1152]{1,0:T(8,128)(2,1)} %dynamic-slice_bitcast_fusion.1), channel_id=1, source_target_pairs={{0,4},{4,0},{1,5},{5,1},{2,6},{6,2},{3,7},{7,3},{8,12},{12,8},{9,1... | collective-permute-start | bytes 3538952 | tf_op jit(solution)/shard_map/ppermute | solution.py:181
  738.6 182.1 %reduce-scatter.14.cloned.1.call-start = ((), (), s32[]{:S(2)}) async-start(), calls=%async_computation.6 | async-start | bytes 3981312 | tf_op jit(solution)/shard_map/reduce_scatter | solution.py:519
  738.6 59.3 %collective-permute-start.18 = (bf16[728,1152]{1,0:T(8,128)(2,1)}, bf16[728,1152]{1,0:T(8,128)(2,1)}, u32[]{:S(2)}, u32[]{:S(2)}) collective-permute-start(bf16[728,1152]{1,0:T(8,128)(2,1)} %reduce-scatter.18.cloned.1.call-done), channel_id=1, source_target_pairs={{3,2},{0,1},{7,6},{4,5},{11,10},{8,9},{15,14},{12,13},{19,18},{16,... | collective-permute-start | bytes 5031944 | tf_op jit(solution)/shard_map/ppermute | solution.py:401
  810.1 38.0 %collective-permute-start.21 = (bf16[728,1152]{1,0:T(8,128)(2,1)}, bf16[728,1152]{1,0:T(8,128)(2,1)}, u32[]{:S(2)}, u32[]{:S(2)}) collective-permute-start(bf16[728,1152]{1,0:T(8,128)(2,1)} %reduce-scatter.20.cloned.1.call-done), channel_id=1, source_target_pairs={{0,1},{3,2},{4,5},{7,6},{8,9},{11,10},{12,13},{15,14},{16,17},{19,... | collective-permute-start | bytes 5031944 | tf_op jit(solution)/shard_map/ppermute | solution.py:401
  820.8 158.6 %all-gather.8.cloned.1.call-start = ((), (), s32[]{:S(2)}) async-start(), calls=%async_computation.8 | async-start | bytes 11114496 | tf_op jit(solution)/shard_map/all_gather | solution.py:540
  820.8 30.5 %collective-permute-start.19 = (bf16[728,1152]{1,0:T(8,128)(2,1)}, bf16[728,1152]{1,0:T(8,128)(2,1)}, u32[]{:S(2)}, u32[]{:S(2)}) collective-permute-start(bf16[728,1152]{1,0:T(8,128)(2,1)} %add_convert_fusion.6), channel_id=1, source_target_pairs={{1,3},{5,7},{9,11},{13,15},{17,19},{21,23},{25,27},{29,31}} | collective-permute-start | bytes 5031944 | tf_op jit(solution)/shard_map/ppermute | solution.py:401
  822.7 36.3 %collective-permute-start.20 = (bf16[728,1152]{1,0:T(8,128)(2,1)}, bf16[728,1152]{1,0:T(8,128)(2,1)}, u32[]{:S(2)}, u32[]{:S(2)}) collective-permute-start(bf16[728,1152]{1,0:T(8,128)(2,1)} %add_convert_fusion.5), channel_id=1, source_target_pairs={{1,2},{5,6},{9,10},{13,14},{17,18},{21,22},{25,26},{29,30}} | collective-permute-start | bytes 5031944 | tf_op jit(solution)/shard_map/ppermute | solution.py:401
  824.6 32.9 %collective-permute-start.25 = (bf16[536,1152]{1,0:T(8,128)(2,1)}, bf16[536,1152]{1,0:T(8,128)(2,1)S(1)}, u32[]{:S(2)}, u32[]{:S(2)}) collective-permute-start(bf16[536,1152]{1,0:T(8,128)(2,1)} %reduce-scatter.22.cloned.1.call-done), channel_id=1, source_target_pairs={{3,2},{1,0},{7,6},{5,4},{11,10},{9,8},{15,14},{13,12},{19,18},{17,... | collective-permute-start | bytes 3704840 | tf_op jit(solution)/shard_map/ppermute | solution.py:401
  850.5 10.5 collective-permute-start.22
  857.8 61.0 %collective-permute-start.26 = (bf16[536,1152]{1,0:T(8,128)(2,1)S(1)}, bf16[536,1152]{1,0:T(8,128)(2,1)S(1)}, u32[]{:S(2)}, u32[]{:S(2)}) collective-permute-start(bf16[536,1152]{1,0:T(8,128)(2,1)S(1)} %add_convert_fusion.8), channel_id=1, source_target_pairs={{2,0},{6,4},{10,8},{14,12},{18,16},{22,20},{26,24},{30,28}} | collective-permute-start | bytes 3704840 | tf_op jit(solution)/shard_map/ppermute | solution.py:401
  920.7 110.7 %all-gather.6.cloned.1.call-start = ((), (), s32[]{:S(2)}) async-start(), calls=%async_computation.7 | async-start | bytes 3981312 | tf_op jit(solution)/shard_map/all_gather | solution.py:541
  920.7 12.8 %collective-permute-start.23 = (bf16[192,1152]{1,0:T(8,128)(2,1)}, bf16[192,1152]{1,0:T(8,128)(2,1)S(1)}, u32[]{:S(2)}, u32[]{:S(2)}) collective-permute-start(bf16[192,1152]{1,0:T(8,128)(2,1)} %reduce-scatter.14.cloned.1.call-done), channel_id=1, source_target_pairs={{3,2},{1,0},{7,6},{5,4},{11,10},{9,8},{15,14},{13,12},{19,18},{17,... | collective-permute-start | bytes 1327112 | tf_op jit(solution)/shard_map/ppermute | solution.py:401
  934.6 12.7 %collective-permute-start.24 = (bf16[192,1152]{1,0:T(8,128)(2,1)S(1)}, bf16[192,1152]{1,0:T(8,128)(2,1)S(1)}, u32[]{:S(2)}, u32[]{:S(2)}) collective-permute-start(bf16[192,1152]{1,0:T(8,128)(2,1)S(1)} %add_convert_fusion.11), channel_id=1, source_target_pairs={{2,0},{6,4},{10,8},{14,12},{18,16},{22,20},{26,24},{30,28}} | collective-permute-start | bytes 1327112 | tf_op jit(solution)/shard_map/ppermute | solution.py:401
  (122 other events, 2589.0 us)
Sparse Core Ops, SparseCore 0:
  12.0 344.2 all-gather.3
  491.9 72.3 reduce-scatter.15
  574.5 72.1 reduce-scatter.17
  650.1 74.1 reduce-scatter.19
  738.7 59.6 reduce-scatter.21
  820.9 46.2 reduce-scatter.13
  920.8 58.5 all-gather.7
  981.2 33.6 all-gather.5

commit v4 on v3

--- a/solution.py
+++ b/solution.py
@@ -5,6 +5,7 @@
 from jax.experimental.pallas import tpu as pltpu
 from jax.sharding import Mesh
 from jax.sharding import PartitionSpec as P
+
 
 D = 1152
 FF = 6912
@@ -335,8 +336,17 @@
     ffn_low = ffn_input.astype(jnp.bfloat16)
     if tree:
         ffn_low = paired(ffn_low)
-    gate_up = times_transposed(ffn_low, w_gate_up)
-    hidden, pull_fourth = jax.vjp(geglu, gate_up[:, :hidden_width], gate_up[:, hidden_width:])
+    gate_up_kept = lax.optimization_barrier(
+        times_transposed(ffn_low, w_gate_up).astype(jnp.bfloat16)
+    )
+
+    def both_wide(gate_up):
+        return (
+            gate_up[:, :hidden_width].astype(jnp.float32),
+            gate_up[:, hidden_width:].astype(jnp.float32),
+        )
+
+    hidden = geglu(*both_wide(gate_up_kept))
     hidden_low = hidden.astype(jnp.bfloat16)
     if tree:
         other_branch = jnp.dot(
@@ -398,7 +408,8 @@
     def advance(key):
         pairs = owner_tree[max(key, 0)][len(steps[key]) - 1]
         held = steps[key][-1]
-        steps[key].append(add_low(held, lax.ppermute(held, "shard", pairs)))
+        moved = lax.ppermute(held, "shard", pairs)
+        steps[key].append(add_low(held, moved))
 
     def tick(anchor, *keys):
         if not tree:
@@ -411,6 +422,8 @@
 
     branch_low = start_ready(branch_low, down_first)
     hidden_grad = times_transposed(branch_low, w_down)
+    gate_up_again, branch_low = tied(gate_up_kept, branch_low)
+    _, pull_fourth = jax.vjp(geglu, *both_wide(gate_up_again))
     gate_grad, up_grad = pull_fourth(hidden_grad)
     gate_low, up_low = gate_grad.astype(jnp.bfloat16), up_grad.astype(jnp.bfloat16)
     factors["gate"] = (gate_first, up_first, product_rows(gate_low, ffn_low))
@@ -431,7 +444,7 @@
         ffn_input_grad = input_grad_of(0, row_count) + to_partner(other_grad)
     else:
         ffn_input_grad = input_grad_of(0, row_count)
-    ffn_input_grad = tick(ffn_input_grad, 3)
+    ffn_input_grad = tick(ffn_input_grad, 2)
     sum_grad_part, gain_three = pull_third(ffn_input_grad)
     sum_grad = upstream + sum_grad_part
     attended_grad, gain_two = pull_second(sum_grad)
@@ -455,7 +468,7 @@
     )
 
     mixed_grad = start_ready(mixed_grad, late_rows)
-    mixed_grad = tick(mixed_grad, 2)
+    mixed_grad = tick(mixed_grad, 3, 1)
 
     def backward_block(running, inputs_block):
         key_acc, value_acc = running
@@ -491,7 +504,7 @@
         (zero_heads, zero_heads),
         (query_blocks, mixed_grad, segment_blocks, block_starts, log_totals),
     )
-    query_grad = tick(query_grad, 2, 1)
+    query_grad = tick(query_grad, 2, 1, 0)
     query_raw_grad = rotate(
         query_grad.reshape(row_count, HEADS, HD) * query_scale, cosine_table, -sine_table
     )
@@ -511,6 +524,7 @@
     state = (params, first_moment, second_moment)
     if tree:
         qkv_grad = product_rows(qkv_low, normed_low)(0, qkv_rows)
+        qkv_grad = tick(qkv_grad, 0)
         by_piece = (
             qkv_grad.reshape(wide_count // 2, -1, 2, 8, D)
             .transpose(0, 2, 1, 3, 4)
@@ -578,8 +592,10 @@
 
 
 def solution(mesh):
+    wide = mesh.shape["wide"]
+
     split_mesh = Mesh(
-        mesh.devices.reshape(mesh.shape["wide"] // 2, 2, mesh.shape["shard"]),
+        mesh.devices.reshape(wide // 2, 2, mesh.shape["shard"]),
         ("chip", "core", "shard"),
     )
     return jax.shard_map(

time: 1070 us -> 1070 us (level)
  waiting for transfers between devices: 377 us -> 364 us
    ppermute x10, waiting for transfers between devices: 127 us -> 108 us  [advance(): moved = lax.ppermute(held, 'shard', pairs)]
where the time goes in v4:
time: 1070 us; the launch traced here: 1060 us
  waiting for transfers between devices  364 us (34%)
  matrix products  349 us (33%)
  other arithmetic  144 us (13%)
  Pallas kernels  74.1 us (7%)
  local copies, waits for them, and re-layouts  65.3 us (6%)
  starting transfers between devices  43.7 us (4%)
  between operations  16.5 us (2%)
    all_gather x1, waiting for transfers between devices, per_device(): lax.all_gather(one_parity(chip_slice, core_index).astype(jnp.bfloat16), (...  111 us
    ppermute x10, waiting for transfers between devices, advance(): moved = lax.ppermute(held, 'shard', pairs)  108 us
    dot_general x4, matrix products, times_transposed(): lax.dot_general(left_side, right_side, (((1,), (1,)), ((), ())), preferre...  107 us
    dot_general x8, matrix products, contract_rows(): lax.dot_general(left_side, right_side, (((0,), (0,)), ((), ())), preferre...  98 us
    pallas_call x2, Pallas kernels, adam_rows(): pl.pallas_call(body, grid_spec=pltpu.PrefetchScalarGridSpec(num_scalar_pr...  74.1 us
    ppermute x7, waiting for transfers between devices, spread_first(): other = lax.ppermute(block, WIDE, [(i, i ^ bit) for i in range(8)])  69.3 us
    dot_general x2, matrix products, input_grad_of(): jnp.dot(gate_low[first:last], w_gate_up[:hidden_width], preferred_element...  32.7 us
    dot_general x2, matrix products, input_grad_of(): jnp.dot(up_low[first:last], w_gate_up[hidden_width:], preferred_element_t...  26.4 us
  transfers between devices with their start and end apart: 40, of which 21 were waited for; matrix products, arithmetic and copies ran while one was open for 39% of the time, Pallas kernels for 5%

profile of v4, /device:TPU:0, one launch (start us, length us, event | category | flops | bytes accessed | tf_op | source)
XLA Modules:
  0.0 1057.3 jit_solution(12664783172706215652)
XLA Ops:
  13.5 6.8 collective-permute-start.3
  20.4 25.8 %collective-permute-done.3 = bf16[320,1152]{1,0:T(8,128)(2,1)} collective-permute-done((bf16[320,1152]{1,0:T(8,128)(2,1)S(1)}, bf16[320,1152]{1,0:T(8,128)(2,1)}, u32[]{:S(2)}, u32[]{:S(2)}) %collective-permute-start.3) | collective-permute-done | bytes 737312 | tf_op jit(solution)/shard_map/ppermute | solution.py:140
  56.8 23.6 %collective-permute-done.4 = bf16[320,1152]{1,0:T(8,128)(2,1)} collective-permute-done((bf16[320,1152]{1,0:T(8,128)(2,1)S(1)}, bf16[320,1152]{1,0:T(8,128)(2,1)}, u32[]{:S(2)}, u32[]{:S(2)}) %collective-permute-start.4) | collective-permute-done | bytes 737312 | tf_op jit(solution)/shard_map/ppermute | solution.py:142
  85.6 13.1 %collective-permute-done.5 = bf16[320,1152]{1,0:T(8,128)(2,1)} collective-permute-done((bf16[320,1152]{1,0:T(8,128)(2,1)S(1)}, bf16[320,1152]{1,0:T(8,128)(2,1)}, u32[]{:S(2)}, u32[]{:S(2)}) %collective-permute-start.5) | collective-permute-done | bytes 737312 | tf_op jit(solution)/shard_map/ppermute | solution.py:150
  106.3 30.2 %collective-permute-done.6 = bf16[320,1152]{1,0:T(8,128)(2,1)} collective-permute-done((bf16[320,1152]{1,0:T(8,128)(2,1)}, bf16[320,1152]{1,0:T(8,128)(2,1)}, u32[]{:S(2)}, u32[]{:S(2)}) %collective-permute-start.6) | collective-permute-done | bytes 737312 | tf_op jit(solution)/shard_map/ppermute | solution.py:150
  140.6 24.7 %collective-permute-done.9 = bf16[320,1152]{1,0:T(8,128)(2,1)} collective-permute-done((bf16[320,1152]{1,0:T(8,128)(2,1)}, bf16[320,1152]{1,0:T(8,128)(2,1)}, u32[]{:S(2)}, u32[]{:S(2)}) %collective-permute-start.9) | collective-permute-done | bytes 737312 | tf_op jit(solution)/shard_map/ppermute | solution.py:150
  198.5 26.9 %while.31 = (s32[]{:T(128)}, bf16[2,512,1,4,256]{4,1,3,2,0:T(8,128)(2,1)}, f32[2,1,4,512,1]{3,2,4,1,0:T(4,128)S(1)}, s32[2,512]{1,0:T(2,128)S(1)}, s32[1024]{0:T...) while((s32[]{:T(128)}, ...), condition=%wide.region_6.7_spmd.clone, body=%wide.region_3.6_spmd.sunk.clone | while | flops 2186279424 | bytes 50411736 | solution.py:330
  245.1 111.2 %all-gather.4.cloned.1.call-done = bf16[11648,1152]{1,0:T(8,128)(2,1)} async-done(((bf16[728,1152]{1,0:T(8,128)(2,1)}), bf16[11648,1152]{1,0:T(8,128)(2,1)}) %all-gather.4.cloned.1.call-update) | async-done | bytes 26837008 | tf_op jit(solution)/shard_map/all_gather | solution.py:262
  356.2 44.8 %convolution_convert_fusion = bf16[2048,6912]{1,0:T(8,128)(2,1)} fusion(bf16[11648,1152]{1,0:T(8,128)(2,1)} %all-gather.4.cloned.1.call-done, bf16[1024,1152]{1,0:T(8,128)(2,1)} %collective-permute-done.12, bf16[1024,1152]{1,0:T(8,128)(2,1)S(1)} %multiply_convert_fusion), kind=kOutput, calls=%fused_computation.103 | convolution fusion | flops 32638500864 | bytes 48955392 | tf_op jit(solution)/shard_map/dot_general | solution.py:78
  401.1 15.4 %fusion.76 = bf16[2048,3456]{1,0:T(8,128)(2,1)S(1)} fusion(bf16[2048,6912]{1,0:T(8,128)(2,1)} %convolution_convert_fusion), kind=kLoop, calls=%fused_computation.95 | loop fusion | flops 84934656 | bytes 42467328 | tf_op jit(solution)/shard_map/convert_element_type | solution.py:350
  416.5 20.2 %fusion.96 = f32[1024,1152]{1,0:T(8,128)} fusion(bf16[2048,3456]{1,0:T(8,128)(2,1)S(1)} %fusion.76, bf16[11648,1152]{1,0:T(8,128)(2,1)} %all-gather.4.cloned.1.call-done), kind=kOutput, calls=%fused_computation.121 | convolution fusion | flops 8153726976 | bytes 19759104 | tf_op jit(solution)/shard_map/dot_general | solution.py:352
  436.7 14.5 %fusion.106 = f32[1024,1152]{1,0:T(8,128)} fusion(bf16[2048,3456]{1,0:T(8,128)(2,1)S(1)} %fusion.76, bf16[11648,1152]{1,0:T(8,128)(2,1)} %all-gather.4.cloned.1.call-done), kind=kOutput, calls=%fused_computation.131 | convolution fusion | flops 8153726976 | bytes 19759104 | tf_op jit(solution)/shard_map/dot_general | solution.py:357
  465.0 22.4 %fusion.87 = bf16[2912,1152]{1,0:T(8,128)(2,1)} fusion(bf16[2048,3456]{1,0:T(8,128)(2,1)} %copy-done.13, bf16[1024,1152]{1,0:T(8,128)(2,1)S(1)} %collective-permute-done.14, bf16[1024,1152]{1,0:T(8,128)(2,1)S(1)} %get-tuple-element.471), kind=kOutput, calls=%fused_computation.107 | convolution fusion | flops 13753331712 | bytes 23486464 | tf_op jit(solution)/shard_map/dot_general | solution.py:72
  491.9 6.7 convolution_convert_fusion.6
  498.5 51.6 %fusion.83 = (bf16[2048,3456]{1,0:T(8,128)(2,1)}, bf16[2048,3456]{1,0:T(8,128)(2,1)}) fusion(bf16[2048,6912]{1,0:T(8,128)(2,1)} %convolution_convert_fusion, bf16[2048,1152]{1,0:T(8,128)(2,1)} %pad_maximum_fusion.4, bf16[11648,1152]{1,0:T(8,128)(2,1)} %all-gather.4.cloned.1.call-done), kind=kOutput, calls=%fused_computation.102 | convolution fusion | flops 16491479040 | bytes 69304320 | tf_op jit(solution)/shard_map/dot_general | solution.py:78
  550.2 20.6 %convolution_convert_fusion.1 = bf16[2368,1152]{1,0:T(8,128)(2,1)} fusion(bf16[2048,3456]{1,0:T(8,128)(2,1)} %get-tuple-element.255, bf16[1024,1152]{1,0:T(8,128)(2,1)} %collective-permute-done.12, bf16[1024,1152]{1,0:T(8,128)(2,1)S(1)} %copy-done.29), kind=kOutput, calls=%fused_computation.108 | convolution fusion | flops 11185790976 | bytes 20135936 | tf_op jit(solution)/shard_map/dot_general | solution.py:72
  576.8 9.9 convolution_convert_fusion.4
  586.7 14.7 %fusion.93 = bf16[1824,1152]{1,0:T(8,128)(2,1)S(1)} fusion(bf16[2048,3456]{1,0:T(8,128)(2,1)} %get-tuple-element.254, bf16[1024,1152]{1,0:T(8,128)(2,1)} %collective-permute-done.12, bf16[1024,1152]{1,0:T(8,128)(2,1)S(1)} %copy-done.30), kind=kOutput, calls=%fused_computation.118 | convolution fusion | flops 8618250240 | bytes 16785408 | tf_op jit(solution)/shard_map/dot_general | solution.py:72
  604.8 13.2 %fusion.102 = f32[1024,1152]{1,0:T(8,128)S(1)} fusion(bf16[2048,3456]{1,0:T(8,128)(2,1)} %get-tuple-element.255, bf16[11648,1152]{1,0:T(8,128)(2,1)} %all-gather.4.cloned.1.call-done), kind=kOutput, calls=%fused_computation.127 | convolution fusion | flops 8153726976 | bytes 19759104 | tf_op jit(solution)/shard_map/dot_general | solution.py:437
  618.0 15.8 %fusion.121 = f32[1024,1152]{1,0:T(8,128)} fusion(f32[1024,1152]{1,0:T(8,128)S(1)} %fusion.102, bf16[11648,1152]{1,0:T(8,128)(2,1)} %all-gather.4.cloned.1.call-done, bf16[2048,3456]{1,0:T(8,128)(2,1)} %get-tuple-element.254), kind=kOutput, calls=%fused_computation.156 | convolution fusion | flops 8154906624 | bytes 24477696 | tf_op jit(solution)/shard_map/dot_general | solution.py:435
  635.5 14.6 %convolution_convert_fusion.3 = bf16[1632,1152]{1,0:T(8,128)(2,1)} fusion(bf16[2048,3456]{1,0:T(8,128)(2,1)} %get-tuple-element.254, bf16[1024,1152]{1,0:T(8,128)(2,1)} %collective-permute-done.12, bf16[1024,1152]{1,0:T(8,128)(2,1)S(1)} %copy-done.31), kind=kOutput, calls=%fused_computation.119 | convolution fusion | flops 7712059392 | bytes 15294464 | tf_op jit(solution)/shard_map/dot_general | solution.py:72
  652.5 13.2 %fusion.98 = f32[1024,1152]{1,0:T(8,128)S(1)} fusion(bf16[2048,3456]{1,0:T(8,128)(2,1)} %get-tuple-element.255, bf16[11648,1152]{1,0:T(8,128)(2,1)} %all-gather.4.cloned.1.call-done), kind=kOutput, calls=%fused_computation.123 | convolution fusion | flops 8153726976 | bytes 19759104 | tf_op jit(solution)/shard_map/dot_general | solution.py:437
  665.7 16.9 %fusion.131 = f32[1024,1152]{1,0:T(8,128)} fusion(f32[1024,1152]{1,0:T(8,128)} %collective-permute-done.15, f32[1024,1152]{1,0:T(8,128)S(1)} %fusion.98, bf16[11648,1152]{1,0:T(8,128)(2,1)} %all-gather.4.cloned.1.call-done, bf16[2048,3456]{1,0:T(8,128)(2,1)} %get-tuple-element.254), kind=kOutput, calls=%fused_computation.158 | convolution fusion | flops 8156086272 | bytes 29196288 | tf_op jit(solution)/shard_map/dot_general | solution.py:435
  688.7 6.1 multiply_reduce_fusion.1
  730.9 48.8 %while.32 = (s32[]{:T(128)}, f32[1024,1,256]{0,2,1:T(8,128)S(1)}, f32[1024,1,256]{0,2,1:T(8,128)}, f32[2,512,1,4,256]{4,1,3,2,0:T(8,128)}, bf16[2,512,1,4,256]{4...) while((s32[]{:T(128)}, f32[1024,1,256]{0,2,1:T(8,128)S(1)}, ...), condition=%wide.region_18.19_spmd.clone.clone, body=%wide.region_16.18_spmd.clone.sunk.clone | while | flops 5423233536 | bytes 125376864 | solution.py:502
  810.6 17.2 %collective-permute-done.23 = bf16[536,1152]{1,0:T(8,128)(2,1)} collective-permute-done((bf16[536,1152]{1,0:T(8,128)(2,1)}, bf16[536,1152]{1,0:T(8,128)(2,1)}, u32[]{:S(2)}, u32[]{:S(2)}) %collective-permute-start.23) | collective-permute-done | bytes 1234976 | tf_op jit(solution)/shard_map/ppermute | solution.py:411
  847.4 59.7 %collective-permute-done.26 = bf16[536,1152]{1,0:T(8,128)(2,1)S(1)} collective-permute-done((bf16[536,1152]{1,0:T(8,128)(2,1)S(1)}, bf16[536,1152]{1,0:T(8,128)(2,1)S(1)}, u32[]{:S(2)}, u32[]{:S(2)}) %collective-permute-start.26) | collective-permute-done | bytes 1234976 | tf_op jit(solution)/shard_map/ppermute | solution.py:411
  910.3 15.9 %collective-permute-done.24 = bf16[192,1152]{1,0:T(8,128)(2,1)S(1)} collective-permute-done((bf16[192,1152]{1,0:T(8,128)(2,1)}, bf16[192,1152]{1,0:T(8,128)(2,1)S(1)}, u32[]{:S(2)}, u32[]{:S(2)}) %collective-permute-start.24) | collective-permute-done | bytes 442400 | tf_op jit(solution)/shard_map/ppermute | solution.py:411
  928.8 11.5 %collective-permute-done.25 = bf16[192,1152]{1,0:T(8,128)(2,1)S(1)} collective-permute-done((bf16[192,1152]{1,0:T(8,128)(2,1)S(1)}, bf16[192,1152]{1,0:T(8,128)(2,1)S(1)}, u32[]{:S(2)}, u32[]{:S(2)}) %collective-permute-start.25) | collective-permute-done | bytes 442400 | tf_op jit(solution)/shard_map/ppermute | solution.py:411
  942.8 8.5 fusion.137
  976.2 52.0 %adam_rows.2 = (f32[364,2,8,1152]{3,2,1,0:T(8,128)}, f32[364,2,8,1152]{3,2,1,0:T(8,128)}, f32[364,2,8,1152]{3,2,1,0:T(8,128)}, f32[364,2,8,1152]{3,2,1,0:T(8,128)}) custom-call(s32[2]{0:T(128)} %broadcast_select_fusion.12.place_ref, bf16[4288,1152]{1,0:T(8,128)(2,1)} %all-gather.8.cloned.1.call-done.grad_ref, f32[364,2,8,1152]{3,2,1,0:T(8,128)} %bitcast.317, ...), custom_call_target="tpu_custom_call" | custom-call | flops 98795520 | bytes 148193280 | tf_op jit(solution)/shard_map/adam_rows/pallas_call | solution.py:219
  1028.2 22.1 %adam_rows.3 = (f32[364,2,8,1152]{3,2,1,0:T(8,128)}, f32[364,2,8,1152]{3,2,1,0:T(8,128)}, f32[364,2,8,1152]{3,2,1,0:T(8,128)}, f32[364,2,8,1152]{3,2,1,0:T(8,128)}) custom-call(s32[2]{0:T(128)} %broadcast_select_fusion.13.place_ref, ...), custom_call_target="tpu_custom_call", output_to_operand_aliasing={{0}: (5, {}), {1}: (6, {}), {2}: (7, {}), {3}: (8, {})} | custom-call | flops 35389440 | bytes 53084160 | tf_op jit(solution)/shard_map/adam_rows/pallas_call | solution.py:219
  (455 shorter events, 317.4 us)
Async XLA Ops:
  7.2 349.1 %all-gather.4.cloned.1.call-start = ((), (), s32[]{:S(2)}) async-start(), calls=%async_computation.5 | async-start | bytes 28514304 | tf_op jit(solution)/shard_map/all_gather | solution.py:262
  11.8 592.9 %reduce-scatter.16.cloned.1.call-start = ((), (), s32[]{:S(2)}) async-start(), calls=%async_computation.9 | async-start | bytes 8386560
  13.5 32.6 %collective-permute-start.3 = (bf16[320,1152]{1,0:T(8,128)(2,1)S(1)}, bf16[320,1152]{1,0:T(8,128)(2,1)}, u32[]{:S(2)}, u32[]{:S(2)}) collective-permute-start(bf16[320,1152]{1,0:T(8,128)(2,1)S(1)} %dynamic-slice_convert_fusion.1), channel_id=1, source_target_pairs={{0,2},{4,6},{8,10},{12,14},{16,18},{20,22},{24,26},{28,30}} | collective-permute-start | bytes 2211848 | tf_op jit(solution)/shard_map/ppermute | solution.py:140
  47.7 32.7 %collective-permute-start.4 = (bf16[320,1152]{1,0:T(8,128)(2,1)S(1)}, bf16[320,1152]{1,0:T(8,128)(2,1)}, u32[]{:S(2)}, u32[]{:S(2)}) collective-permute-start(bf16[320,1152]{1,0:T(8,128)(2,1)S(1)} %broadcast_select_fusion), channel_id=1, source_target_pairs={{0,1},{2,3},{4,5},{6,7},{8,9},{10,11},{12,13},{14,15},{16,17},{18,... | collective-permute-start | bytes 2211848 | tf_op jit(solution)/shard_map/ppermute | solution.py:142
  49.8 89.8 %collective-permute-start.2 = (bf16[4,288]{1,0:T(4,128)(2,1)S(1)}, bf16[4,288]{1,0:T(4,128)(2,1)S(1)}, u32[]{:S(2)}, u32[]{:S(2)}) collective-permute-start(bf16[4,288]{1,0:T(4,128)(2,1)S(1)} %convert_element_type.242), channel_id=1, source_target_pairs={{0,3},{1,0},{2,1},{3,2},{4,7},{5,4},{6,5},{7,6},{8,11},{9,8},{10,9... | collective-permute-start | bytes 6920 | tf_op jit(solution)/shard_map/ppermute | solution.py:132
  49.8 89.5 %collective-permute-start.1 = (bf16[4,288]{1,0:T(4,128)(2,1)S(1)}, bf16[4,288]{1,0:T(4,128)(2,1)S(1)}, u32[]{:S(2)}, u32[]{:S(2)}) collective-permute-start(bf16[4,288]{1,0:T(4,128)(2,1)S(1)} %convert_element_type.242), channel_id=1, source_target_pairs={{0,2},{1,3},{2,0},{3,1},{4,6},{5,7},{6,4},{7,5},{8,10},{9,11},{10,... | collective-permute-start | bytes 6920 | tf_op jit(solution)/shard_map/ppermute | solution.py:132
  53.7 85.4 %collective-permute-start = (bf16[4,288]{1,0:T(4,128)(2,1)S(1)}, bf16[4,288]{1,0:T(4,128)(2,1)S(1)}, u32[]{:S(2)}, u32[]{:S(2)}) collective-permute-start(bf16[4,288]{1,0:T(4,128)(2,1)S(1)} %convert_element_type.242), channel_id=1, source_target_pairs={{0,1},{1,2},{2,3},{3,0},{4,5},{5,6},{6,7},{7,4},{8,9},{9,10},{10,1... | collective-permute-start | bytes 6920 | tf_op jit(solution)/shard_map/ppermute | solution.py:132
  81.6 17.0 %collective-permute-start.5 = (bf16[320,1152]{1,0:T(8,128)(2,1)S(1)}, bf16[320,1152]{1,0:T(8,128)(2,1)}, u32[]{:S(2)}, u32[]{:S(2)}) collective-permute-start(bf16[320,1152]{1,0:T(8,128)(2,1)S(1)} %broadcast_select_fusion.1), channel_id=1, source_target_pairs={{0,16},{4,20},{8,24},{12,28},{16,0},{20,4},{24,8},{28,12},{1,17},{... | collective-permute-start | bytes 2211848 | tf_op jit(solution)/shard_map/ppermute | solution.py:150
  101.0 35.5 %collective-permute-start.6 = (bf16[320,1152]{1,0:T(8,128)(2,1)}, bf16[320,1152]{1,0:T(8,128)(2,1)}, u32[]{:S(2)}, u32[]{:S(2)}) collective-permute-start(bf16[320,1152]{1,0:T(8,128)(2,1)} %get-tuple-element.481), channel_id=1, source_target_pairs={{0,8},{4,12},{8,0},{12,4},{16,24},{20,28},{24,16},{28,20},{1,9},{5... | collective-permute-start | bytes 2211848 | tf_op jit(solution)/shard_map/ppermute | solution.py:150
  105.3 60.0 %collective-permute-start.9 = (bf16[320,1152]{1,0:T(8,128)(2,1)}, bf16[320,1152]{1,0:T(8,128)(2,1)}, u32[]{:S(2)}, u32[]{:S(2)}) collective-permute-start(bf16[320,1152]{1,0:T(8,128)(2,1)} %get-tuple-element.480), channel_id=1, source_target_pairs={{0,8},{4,12},{8,0},{12,4},{16,24},{20,28},{24,16},{28,20},{1,9},{5... | collective-permute-start | bytes 2211848 | tf_op jit(solution)/shard_map/ppermute | solution.py:150
  138.8 29.4 %collective-permute-start.7 = (bf16[320,1152]{1,0:T(8,128)(2,1)}, bf16[320,1152]{1,0:T(8,128)(2,1)}, u32[]{:S(2)}, u32[]{:S(2)}) collective-permute-start(bf16[320,1152]{1,0:T(8,128)(2,1)} %get-tuple-element.483), channel_id=1, source_target_pairs={{0,4},{4,0},{8,12},{12,8},{16,20},{20,16},{24,28},{28,24},{1,5},{5... | collective-permute-start | bytes 2211848 | tf_op jit(solution)/shard_map/ppermute | solution.py:150
  167.7 62.5 %collective-permute-start.11 = (bf16[320,1152]{1,0:T(8,128)(2,1)}, bf16[320,1152]{1,0:T(8,128)(2,1)}, u32[]{:S(2)}, u32[]{:S(2)}) collective-permute-start(bf16[320,1152]{1,0:T(8,128)(2,1)} %get-tuple-element.478), channel_id=1, source_target_pairs={{0,4},{4,0},{8,12},{12,8},{16,20},{20,16},{24,28},{28,24},{1,5},{5... | collective-permute-start | bytes 2211848 | tf_op jit(solution)/shard_map/ppermute | solution.py:150
  167.7 5.0 collective-permute-start.10
  436.7 14.5 %collective-permute-start.13 = (f32[1024,1152]{1,0:T(8,128)}, f32[1024,1152]{1,0:T(8,128)S(1)}, u32[]{:S(2)}, u32[]{:S(2)}) collective-permute-start(f32[1024,1152]{1,0:T(8,128)} %fusion.96), channel_id=1, source_target_pairs={{0,4},{4,0},{1,5},{5,1},{2,6},{6,2},{3,7},{7,3},{8,12},{12,8},{9,1... | collective-permute-start | bytes 14155784 | tf_op jit(solution)/shard_map/ppermute | solution.py:182
  487.4 195.2 %reduce-scatter.18.cloned.1.call-start = ((), (), s32[]{:S(2)}) async-start(), calls=%async_computation.10 | async-start | bytes 8386560
  576.7 149.6 %reduce-scatter.20.cloned.1.call-start = ((), (), s32[]{:S(2)}) async-start(), calls=%async_computation.11 | async-start | bytes 8386560
  633.8 31.9 %collective-permute-start.15 = (f32[1024,1152]{1,0:T(8,128)}, f32[1024,1152]{1,0:T(8,128)}, u32[]{:S(2)}, u32[]{:S(2)}) collective-permute-start(f32[1024,1152]{1,0:T(8,128)} %fusion.121), channel_id=1, source_target_pairs={{0,4},{4,0},{1,5},{5,1},{2,6},{6,2},{3,7},{7,3},{8,12},{12,8},{9,1... | collective-permute-start | bytes 14155784 | tf_op jit(solution)/shard_map/ppermute | solution.py:182
  634.4 159.8 %reduce-scatter.22.cloned.1.call-start = ((), (), s32[]{:S(2)}) async-start(), calls=%async_computation.12 | async-start | bytes 6174720
  650.0 52.8 %collective-permute-start.17 = (bf16[728,1152]{1,0:T(8,128)(2,1)}, bf16[728,1152]{1,0:T(8,128)(2,1)}, u32[]{:S(2)}, u32[]{:S(2)}) collective-permute-start(bf16[728,1152]{1,0:T(8,128)(2,1)} %reduce-scatter.16.cloned.1.call-done), channel_id=1, source_target_pairs={{0,1},{2,3},{4,5},{6,7},{8,9},{10,11},{12,13},{14,15},{16,17},{18,... | collective-permute-start | bytes 5031944 | tf_op jit(solution)/shard_map/ppermute | solution.py:411
  702.3 17.4 %collective-permute-start.16 = (bf16[512,1152]{1,0:T(8,128)(2,1)}, bf16[512,1152]{1,0:T(8,128)(2,1)}, u32[]{:S(2)}, u32[]{:S(2)}) collective-permute-start(bf16[512,1152]{1,0:T(8,128)(2,1)} %dynamic-slice_bitcast_fusion.1), channel_id=1, source_target_pairs={{0,4},{4,0},{1,5},{5,1},{2,6},{6,2},{3,7},{7,3},{8,12},{12,8},{9,1... | collective-permute-start | bytes 3538952 | tf_op jit(solution)/shard_map/ppermute | solution.py:182
  717.3 67.5 %collective-permute-start.18 = (bf16[728,1152]{1,0:T(8,128)(2,1)}, bf16[728,1152]{1,0:T(8,128)(2,1)}, u32[]{:S(2)}, u32[]{:S(2)}) collective-permute-start(bf16[728,1152]{1,0:T(8,128)(2,1)} %reduce-scatter.18.cloned.1.call-done), channel_id=1, source_target_pairs={{3,2},{0,1},{7,6},{4,5},{11,10},{8,9},{15,14},{12,13},{19,18},{16,... | collective-permute-start | bytes 5031944 | tf_op jit(solution)/shard_map/ppermute | solution.py:411
  726.1 182.9 %reduce-scatter.14.cloned.1.call-start = ((), (), s32[]{:S(2)}) async-start(), calls=%async_computation.6 | async-start | bytes 3981312 | tf_op jit(solution)/shard_map/reduce_scatter | solution.py:533
  726.3 64.8 %collective-permute-start.19 = (bf16[728,1152]{1,0:T(8,128)(2,1)}, bf16[728,1152]{1,0:T(8,128)(2,1)}, u32[]{:S(2)}, u32[]{:S(2)}) collective-permute-start(bf16[728,1152]{1,0:T(8,128)(2,1)} %reduce-scatter.20.cloned.1.call-done), channel_id=1, source_target_pairs={{0,1},{3,2},{4,5},{7,6},{8,9},{11,10},{12,13},{15,14},{16,17},{19,... | collective-permute-start | bytes 5031944 | tf_op jit(solution)/shard_map/ppermute | solution.py:411
  796.9 30.8 %collective-permute-start.23 = (bf16[536,1152]{1,0:T(8,128)(2,1)}, bf16[536,1152]{1,0:T(8,128)(2,1)}, u32[]{:S(2)}, u32[]{:S(2)}) collective-permute-start(bf16[536,1152]{1,0:T(8,128)(2,1)} %reduce-scatter.22.cloned.1.call-done), channel_id=1, source_target_pairs={{3,2},{1,0},{7,6},{5,4},{11,10},{9,8},{15,14},{13,12},{19,18},{17,... | collective-permute-start | bytes 3704840 | tf_op jit(solution)/shard_map/ppermute | solution.py:411
  832.9 143.3 %all-gather.8.cloned.1.call-start = ((), (), s32[]{:S(2)}) async-start(), calls=%async_computation.8 | async-start | bytes 11114496 | tf_op jit(solution)/shard_map/all_gather | solution.py:554
  833.0 5.6 collective-permute-start.20
  834.8 7.9 collective-permute-start.21
  836.7 8.1 collective-permute-start.22
  841.2 65.9 %collective-permute-start.26 = (bf16[536,1152]{1,0:T(8,128)(2,1)S(1)}, bf16[536,1152]{1,0:T(8,128)(2,1)S(1)}, u32[]{:S(2)}, u32[]{:S(2)}) collective-permute-start(bf16[536,1152]{1,0:T(8,128)(2,1)S(1)} %copy-done.22), channel_id=1, source_target_pairs={{2,0},{6,4},{10,8},{14,12},{18,16},{22,20},{26,24},{30,28}} | collective-permute-start | bytes 3704840 | tf_op jit(solution)/shard_map/ppermute | solution.py:411
  908.9 119.2 %all-gather.6.cloned.1.call-start = ((), (), s32[]{:S(2)}) async-start(), calls=%async_computation.7 | async-start | bytes 3981312 | tf_op jit(solution)/shard_map/all_gather | solution.py:555
  909.0 17.2 %collective-permute-start.24 = (bf16[192,1152]{1,0:T(8,128)(2,1)}, bf16[192,1152]{1,0:T(8,128)(2,1)S(1)}, u32[]{:S(2)}, u32[]{:S(2)}) collective-permute-start(bf16[192,1152]{1,0:T(8,128)(2,1)} %reduce-scatter.14.cloned.1.call-done), channel_id=1, source_target_pairs={{3,2},{1,0},{7,6},{5,4},{11,10},{9,8},{15,14},{13,12},{19,18},{17,... | collective-permute-start | bytes 1327112 | tf_op jit(solution)/shard_map/ppermute | solution.py:411
  927.3 12.9 %collective-permute-start.25 = (bf16[192,1152]{1,0:T(8,128)(2,1)S(1)}, bf16[192,1152]{1,0:T(8,128)(2,1)S(1)}, u32[]{:S(2)}, u32[]{:S(2)}) collective-permute-start(bf16[192,1152]{1,0:T(8,128)(2,1)S(1)} %add_convert_fusion.11), channel_id=1, source_target_pairs={{2,0},{6,4},{10,8},{14,12},{18,16},{22,20},{26,24},{30,28}} | collective-permute-start | bytes 1327112 | tf_op jit(solution)/shard_map/ppermute | solution.py:411
  (120 other events, 2462.4 us)
Sparse Core Ops, SparseCore 0:
  12.0 344.2 all-gather.3
  487.6 72.3 reduce-scatter.15
  576.8 71.8 reduce-scatter.17
  652.1 74.1 reduce-scatter.19
  729.8 59.2 reduce-scatter.21
  833.1 48.2 reduce-scatter.13
  909.1 67.0 all-gather.7
  978.1 33.6 all-gather.5
